TPU v7x, 256 devices: a whole 4x4x8 slice. The times are simulated.
256 devices in a mesh: member: 8 (over z), cell: 32 (over x, y, core).
Axes of the slice: x: 4, y: 4, z: 8, core: 2. Of those that a mesh axis runs over, the one named last changes fastest.
Arguments:
- prior: float32 [64, 524288], P('member', 'cell')
- samples: float32 [64, 524288], P('member', 'cell')
- noise: float32 [2, 64, 524288], P(None, 'member', 'cell'), may hold values from -6 to 6
- obs_cells: int32 [2, 65536], P(None, 'cell'), may hold values from 0 to 524287, as said below
- obs_values: float32 [2, 65536], P(None, 'cell'), may hold values from -6 to 6
- seismic_mask: int32 [2, 4096], P(None, 'cell'), may hold values 0 or 1
Outputs:
- analysis: float32 [64, 524288], P('member', 'cell')
Inputs may be any that keep to these rules, and one draw needn't show every extreme that they name: obs_cells[s, o] lies in cells k * 16384 to (k + 1) * 16384 - 1 where k = o // 2048; cells may repeat.
All inputs are finite; a program needn't handle non-finite values. No bound on the sum of `seismic_mask` on one device may be relied on, other than what follows from the above.
Results may differ from a plain program's by a relative error of at most 0.0003.
Values sent between devices are 32-bit elements; how exact they have to be, the bound alone decides.
No kernel may reach another device: no remote copies, remote signals or barrier semaphores. Data moves between devices by JAX's collectives and lax.ppermute only.
A program may use at most 64 MiB of HBM per device.

v0:
```python
import math

import jax
import jax.numpy as jnp
from jax import lax
from jax.sharding import PartitionSpec as P

STEPS = 2


def advance(state, fresh, prior_slab, prior_part, precision_slab, target_slab, step, ncell):
    time_now = 0.6 - 0.1 * step
    alpha = 1.0 - 0.95 * time_now
    drift = -0.95 / alpha
    diffusion = 1.0 - 2.0 * drift * time_now
    cross_part = lax.dot_general(
        state,
        prior_slab,
        (((1,), (1,)), ((), ())),
        precision=lax.Precision.HIGHEST,
        preferred_element_type=jnp.float32,
    )
    cross, prior_sq = lax.psum((cross_part, prior_part), ("member", "cell"))
    dist = alpha * alpha * prior_sq[None, :] - 2.0 * alpha * cross
    weights = jax.nn.softmax(-dist / (2.0 * time_now * math.sqrt(ncell)), axis=1)
    mean = jnp.dot(
        weights, prior_slab, precision=lax.Precision.HIGHEST, preferred_element_type=jnp.float32
    )
    score = (alpha * mean - state) / time_now - (1.0 - time_now) * (
        precision_slab[None, :] * state - target_slab[None, :]
    )
    return state - 0.1 * (drift * state - diffusion * score) + math.sqrt(0.1 * diffusion) * fresh


def per_device(prior, samples, noise, obs_cells, obs_values, seismic_mask):
    cells = prior.shape[1]
    groups = lax.axis_size("member")
    width = cells // groups
    ncell = cells * lax.axis_size("cell")
    shard = lax.axis_index("cell")
    member_pos = lax.axis_index("member")
    local = obs_cells - shard * cells
    precision_field = jnp.zeros((cells,), jnp.float32)
    target_field = jnp.zeros((cells,), jnp.float32)
    for survey in range(obs_cells.shape[0]):
        where = local[survey]
        flags = seismic_mask[survey].astype(jnp.float32)
        weight = flags[where // 128]
        precision_field = precision_field.at[where].add(weight)
        target_field = target_field.at[where].add(weight * obs_values[survey])
    precision_slab = lax.dynamic_slice_in_dim(precision_field, member_pos * width, width)
    target_slab = lax.dynamic_slice_in_dim(target_field, member_pos * width, width)
    prior_slab = lax.all_to_all(prior, "member", split_axis=1, concat_axis=0, tiled=True)
    prior_part = jnp.sum(prior_slab * prior_slab, axis=1)
    state = samples
    for step in range(STEPS):
        slab, fresh = (
            lax.all_to_all(state, "member", split_axis=1, concat_axis=0, tiled=True),
            lax.all_to_all(noise[step], "member", split_axis=1, concat_axis=0, tiled=True),
        )
        slab = advance(
            slab, fresh, prior_slab, prior_part, precision_slab, target_slab, step, ncell
        )
        state = lax.all_to_all(slab, "member", split_axis=0, concat_axis=1, tiled=True)
    return state


def solution(mesh):
    in_specs = (
        P("member", "cell"),
        P("member", "cell"),
        P(None, "member", "cell"),
        P(None, "cell"),
        P(None, "cell"),
        P(None, "cell"),
    )
    out_specs = P("member", "cell")
    return jax.shard_map(
        per_device, mesh=mesh, in_specs=in_specs, out_specs=out_specs, check_vma=False
    )
```

profile of v0, /device:TPU:1, one launch (start us, length us, event | category | flops | bytes accessed | tf_op | source)
XLA Modules:
  0.0 345.3 jit_solution(6709701843080657037)
XLA Ops:
  0.0 0.0 copy-start
  0.0 9.1 %all-to-all-start.1 = ((f32[8,8,2048]{2,0,1:T(8,128)}), f32[8,8,2048]{2,0,1:T(8,128)S(1)}, u32[]{:S(2)}, u32[]{:S(2)}) async-start(f32[8,8,2048]{2,0,1:T(8,128)} %bitcast.90), calls=%async_computation.1 | async-start | bytes 1048576 | tf_op jit(solution)/shard_map/all_to_all | solution.py:53
  9.1 0.0 copy-done
  9.2 0.0 copy-start.1
  9.2 1.0 fusion.55
  10.2 0.0 copy-done.1
  10.2 16.9 %all-to-all-done.1 = f32[8,8,2048]{2,0,1:T(8,128)S(1)} async-done(((f32[8,8,2048]{2,0,1:T(8,128)}), f32[8,8,2048]{2,0,1:T(8,128)S(1)}, u32[]{:S(2)}, u32[]{:S(2)}) %all-to-all-start.1) | async-done | bytes 524320 | tf_op jit(solution)/shard_map/all_to_all | solution.py:53
  27.1 3.5 %all-to-all-start = ((f32[8,8,2048]{2,0,1:T(8,128)}), f32[8,8,2048]{2,0,1:T(8,128)S(1)}, u32[]{:S(2)}, u32[]{:S(2)}) async-start(f32[8,8,2048]{2,0,1:T(8,128)} %bitcast), calls=%async_computation | async-start | bytes 1048576 | tf_op jit(solution)/shard_map/all_to_all | solution.py:58
  30.6 0.1 compare_select_fusion
  30.7 0.0 copy-start.2
  30.8 0.7 copy-done.2
  31.5 17.0 %all-to-all-done = f32[8,8,2048]{2,0,1:T(8,128)S(1)} async-done(((f32[8,8,2048]{2,0,1:T(8,128)}), f32[8,8,2048]{2,0,1:T(8,128)S(1)}, u32[]{:S(2)}, u32[]{:S(2)}) %all-to-all-start) | async-done | bytes 524320 | tf_op jit(solution)/shard_map/all_to_all | solution.py:58
  48.5 0.0 copy-start.3
  48.5 3.6 %all-to-all-start.2 = ((f32[8,8,2048]{2,0,1:T(8,128)}), f32[8,8,2048]{2,0,1:T(8,128)S(1)}, u32[]{:S(2)}, u32[]{:S(2)}) async-start(f32[8,8,2048]{2,0,1:T(8,128)} %bitcast.17), calls=%async_computation.2 | async-start | bytes 1048576 | tf_op jit(solution)/shard_map/all_to_all | solution.py:59
  52.1 0.0 copy-done.3
  52.1 12.6 %gather_fusion = f32[2048]{0:T(1024)S(1)} fusion(f32[128]{0:T(128)S(1)} %get-tuple-element.16, s32[2048]{0:T(1024)S(1)} %broadcast_clamp_fusion.1), kind=kCustom, calls=%fused_computation | custom fusion | bytes 24576 | tf_op jit(solution)/shard_map/gather | solution.py:48
  64.8 11.3 %scatter_custom_fusion = f32[16384]{0:T(1024)S(1)} fusion(s32[2048]{0:T(1024)S(1)} %bitcast.97, f32[2048]{0:T(1024)S(1)} %gather_fusion, f32[]{:T(128)} %constant.33.clone.1), kind=kCustom, calls=%fused_computation.51 | custom fusion | flops 2048 | bytes 65540 | tf_op jit(solution)/shard_map/scatter-add | solution.py:49
  76.1 11.3 %scatter_custom_fusion.2 = f32[16384]{0:T(1024)S(1)} fusion(s32[2048]{0:T(1024)S(1)} %bitcast.98, f32[2048]{0:T(1024)S(1)} %mul.145, f32[]{:T(128)} %constant.33.clone.1), kind=kCustom, calls=%fused_computation.49 | custom fusion | flops 2048 | bytes 65540 | tf_op jit(solution)/shard_map/scatter-add | solution.py:50
  87.3 12.6 %gather_fusion.1 = f32[2048]{0:T(1024)S(1)} fusion(f32[128]{0:T(128)S(1)} %get-tuple-element.15, s32[2048]{0:T(1024)S(1)} %broadcast_clamp_fusion), kind=kCustom, calls=%fused_computation.1 | custom fusion | bytes 24576 | tf_op jit(solution)/shard_map/gather | solution.py:48
  100.0 11.6 %scatter_fusion = f32[16384]{0:T(1024)S(1)} fusion(f32[16384]{0:T(1024)S(1)} %scatter_custom_fusion, s32[2048]{0:T(1024)S(1)} %bitcast.91, f32[2048]{0:T(1024)S(1)} %gather_fusion.1), kind=kCustom, calls=%fused_computation.3 | custom fusion | flops 2048 | bytes 32768 | tf_op jit(solution)/shard_map/scatter-add | solution.py:49
  111.6 11.6 %scatter_fusion.1 = f32[16384]{0:T(1024)S(1)} fusion(f32[16384]{0:T(1024)S(1)} %scatter_custom_fusion.2, s32[2048]{0:T(1024)S(1)} %bitcast.92, f32[2048]{0:T(1024)S(1)} %mul.146), kind=kCustom, calls=%fused_computation.5 | custom fusion | flops 2048 | bytes 32768 | tf_op jit(solution)/shard_map/scatter-add | solution.py:50
  123.2 0.1 fusion.27
  123.3 0.1 reduce_sum.30
  123.4 0.6 fusion.22
  123.9 77.8 %all-reduce = (f32[64,64]{1,0:T(8,128)S(1)}, f32[64]{0:T(128)S(1)}) all-reduce(f32[64,64]{1,0:T(8,128)S(1)} %fusion.22, f32[64]{0:T(128)S(1)} %reduce_sum.30), channel_id=1, replica_groups=mesh['member'=8,'cell'=32] {'member','cell'}, use_global_device_ids=true, to_apply=%region_2.3 | all-reduce | flops 4160 | bytes 33280 | tf_op jit(solution)/shard_map/psum | solution.py:23
  201.7 0.1 fusion.39
  201.9 0.2 fusion.37
  202.1 0.0 all-to-all-done.2
  202.1 0.9 fusion.17
  202.9 21.0 %all_to_all.115 = f32[8,8,2048]{2,1,0:T(8,128)S(1)} all-to-all(f32[8,8,2048]{2,1,0:T(8,128)S(1)} %fusion.17), channel_id=1, replica_groups=mesh['member'=8,'cell'=32] {'member'}, dimensions={0} | all-to-all | bytes 1048576 | tf_op jit(solution)/shard_map/all_to_all | solution.py:64
  223.9 17.2 %all_to_all.116 = f32[8,8,2048]{2,0,1:T(8,128)S(1)} all-to-all(f32[8,8,2048]{2,0,1:T(8,128)S(1)} %bitcast.88), channel_id=1, replica_groups=mesh['member'=8,'cell'=32] {'member'}, dimensions={1} | all-to-all | bytes 1048576 | tf_op jit(solution)/shard_map/all_to_all | solution.py:58
  241.0 3.5 %all-to-all-start.5 = ((f32[8,8,2048]{2,0,1:T(8,128)}), f32[8,8,2048]{2,0,1:T(8,128)S(1)}, u32[]{:S(2)}, u32[]{:S(2)}) async-start(f32[8,8,2048]{2,0,1:T(8,128)} %bitcast.26), calls=%async_computation.5 | async-start | bytes 1048576 | tf_op jit(solution)/shard_map/all_to_all | solution.py:59
  244.5 0.6 fusion.19
  245.1 77.3 %psum.26 = f32[64,64]{1,0:T(8,128)S(1)} all-reduce(f32[64,64]{1,0:T(8,128)S(1)} %fusion.19), channel_id=1, replica_groups=mesh['member'=8,'cell'=32] {'member','cell'}, use_global_device_ids=true, to_apply=%region_9.10 | all-reduce | flops 4096 | bytes 32768 | tf_op jit(solution)/shard_map/psum | solution.py:23
  322.5 0.1 fusion.40
  322.6 0.2 fusion.38
  322.8 0.0 all-to-all-done.5
  322.8 0.8 fusion.15
  323.6 20.9 %all_to_all.117 = f32[8,8,2048]{2,1,0:T(8,128)S(1)} all-to-all(f32[8,8,2048]{2,1,0:T(8,128)S(1)} %fusion.15), channel_id=1, replica_groups=mesh['member'=8,'cell'=32] {'member'}, dimensions={0} | all-to-all | bytes 1048576 | tf_op jit(solution)/shard_map/all_to_all | solution.py:64
  344.6 0.8 copy.10
  (10 shorter events, 0.1 us)
Async XLA Ops:
  0.0 9.2 %copy-start = (f32[2,8,16384]{2,1,0:T(8,128)S(1)}, f32[2,8,16384]{2,1,0:T(8,128)}, u32[]{:S(2)}) copy-start(f32[2,8,16384]{2,1,0:T(8,128)} %param.8) | copy-start | bytes 3145732
  0.0 27.1 %all-to-all-start.1 = ((f32[8,8,2048]{2,0,1:T(8,128)}), f32[8,8,2048]{2,0,1:T(8,128)S(1)}, u32[]{:S(2)}, u32[]{:S(2)}) async-start(f32[8,8,2048]{2,0,1:T(8,128)} %bitcast.90), calls=%async_computation.1 | async-start | bytes 1048576 | tf_op jit(solution)/shard_map/all_to_all | solution.py:53
  9.2 1.0 copy-start.1
  27.1 21.4 %all-to-all-start = ((f32[8,8,2048]{2,0,1:T(8,128)}), f32[8,8,2048]{2,0,1:T(8,128)S(1)}, u32[]{:S(2)}, u32[]{:S(2)}) async-start(f32[8,8,2048]{2,0,1:T(8,128)} %bitcast), calls=%async_computation | async-start | bytes 1048576 | tf_op jit(solution)/shard_map/all_to_all | solution.py:58
  30.7 0.7 copy-start.2
  48.5 3.6 %copy-start.3 = (s32[2,128]{1,0:T(2,128)S(1)}, s32[2,128]{1,0:T(2,128)}, u32[]{:S(2)}) copy-start(s32[2,128]{1,0:T(2,128)} %param.11) | copy-start | bytes 3076
  48.5 153.6 %all-to-all-start.2 = ((f32[8,8,2048]{2,0,1:T(8,128)}), f32[8,8,2048]{2,0,1:T(8,128)S(1)}, u32[]{:S(2)}, u32[]{:S(2)}) async-start(f32[8,8,2048]{2,0,1:T(8,128)} %bitcast.17), calls=%async_computation.2 | async-start | bytes 1048576 | tf_op jit(solution)/shard_map/all_to_all | solution.py:59
  241.0 81.7 %all-to-all-start.5 = ((f32[8,8,2048]{2,0,1:T(8,128)}), f32[8,8,2048]{2,0,1:T(8,128)S(1)}, u32[]{:S(2)}, u32[]{:S(2)}) async-start(f32[8,8,2048]{2,0,1:T(8,128)} %bitcast.26), calls=%async_computation.5 | async-start | bytes 1048576 | tf_op jit(solution)/shard_map/all_to_all | solution.py:59
where the time goes:
time: 347 us; the launch traced here: 345 us
  blocking collectives  214 us (62%)
  other arithmetic  46.5 us (13%)
  waiting for transfers between devices  33.9 us (10%)
  local copies, waits for them, and re-layouts  27.9 us (8%)
  starting transfers between devices  19.8 us (6%)
    psum x2, blocking collectives, advance(): cross, prior_sq = lax.psum((cross_part, prior_part), ('member', 'cell'))  155 us
    all_to_all x2, blocking collectives, per_device(): lax.all_to_all(slab, 'member', split_axis=0, concat_axis=1, tiled=True)  41.9 us
    gather x2, local copies, waits for them, and re-layouts, per_device(): weight = flags[where // 128]  25.2 us
    scatter-add x2, other arithmetic, per_device(): precision_field = precision_field.at[where].add(weight)  22.8 us
    scatter-add x2, other arithmetic, per_device(): target_field = target_field.at[where].add(weight * obs_values[survey])  22.8 us
    all_to_all x1, blocking collectives, per_device(): lax.all_to_all(state, 'member', split_axis=1, concat_axis=0, tiled=True)  17.2 us
    all_to_all x1, waiting for transfers between devices, per_device(): lax.all_to_all(state, 'member', split_axis=1, concat_axis=0, tiled=True)  17 us
    all_to_all x1, waiting for transfers between devices, per_device(): lax.all_to_all(prior, 'member', split_axis=1, concat_axis=0, tiled=True)  16.9 us
  transfers between devices with their start and end apart: 4, of which 2 were waited for; matrix products, arithmetic and copies ran while one was open for 21% of the time, Pallas kernels for 0%

commit v1 on v0

v1 whole, which is shorter than its diff:
```python
import math

import jax
import jax.numpy as jnp
from jax import lax
from jax.experimental import pallas as pl
from jax.experimental.pallas import tpu as pltpu
from jax.sharding import PartitionSpec as P

STEPS = 2
RINGS = 8
ROWS = 8
BF = jnp.bfloat16
F32 = jnp.float32
NT = (((1,), (1,)), ((), ()))
NN = (((1,), (0,)), ((), ()))


def constants(step):
    t = 0.6 - 0.1 * step
    alpha = 1.0 - 0.95 * t
    drift = -0.95 / alpha
    diffusion = 1.0 - 2.0 * drift * t
    return dict(
        t=t,
        alpha=alpha,
        gain=1.0 - 0.1 * drift - 0.1 * diffusion / t,
        pull=0.1 * diffusion * (1.0 - t),
        lift=0.1 * diffusion * alpha / t,
        kick=math.sqrt(0.1 * diffusion),
    )


def split3(x):
    a = x.astype(BF).astype(F32)
    r = x - a
    b = r.astype(BF).astype(F32)
    return a, b, r - b


def prep_kernel(cells, vals, mask, samples, noise, u_ref, base_ref, ab_ref, prec, targ):
    width = prec.shape[0]
    obs = cells.shape[1]
    rows = lax.broadcasted_iota(jnp.int32, (width, obs), 0)
    eye = lax.broadcasted_iota(jnp.int32, (width, width), 0) == lax.broadcasted_iota(
        jnp.int32, (width, width), 1
    )
    p_sum = jnp.zeros((width, width), F32)
    t_sum = jnp.zeros((width, width), F32)
    for s in range(cells.shape[0]):
        local = cells[s : s + 1, :] & (width * width - 1)
        high = jnp.where(rows == (local >> 7), 1.0, 0.0).astype(BF)
        low = rows == (local & 127)
        pieces = [jnp.ones((1, obs), F32), *split3(vals[s : s + 1, :])]
        sums = [
            lax.dot_general(
                high, jnp.where(low, piece, 0.0).astype(BF), NT, preferred_element_type=F32
            )
            for piece in pieces
        ]
        flags = mask[s : s + 1, :].astype(F32)
        flags = jnp.sum(jnp.where(eye, flags, 0.0), axis=1, keepdims=True)
        p_sum += flags * sums[0]
        t_sum += flags * (sums[1] + sums[2] + sums[3])
    prec[...] = p_sum
    targ[...] = t_sum
    k0, k1 = constants(0), constants(1)

    def body(h, carry):
        where = pl.ds(pl.multiple_of(h * width, width), width)
        p = prec[pl.ds(h, 1), :]
        t = targ[pl.ds(h, 1), :]
        u = (
            (k0["gain"] - k0["pull"] * p) * samples[:, where]
            + k0["pull"] * t
            + k0["kick"] * noise[0, :, where]
        )
        a1 = k1["gain"] - k1["pull"] * p
        u_ref[:, where] = u
        base_ref[:, where] = a1 * u + k1["pull"] * t + k1["kick"] * noise[1, :, where]
        ab_ref[:, where] = jnp.broadcast_to(k0["lift"] * a1, (ROWS, width))
        return carry

    lax.fori_loop(0, width, body, 0, unroll=4)


def prep(cells, vals, mask, samples, noise):
    shape = jax.ShapeDtypeStruct(samples.shape, F32)
    return pl.pallas_call(
        prep_kernel,
        out_shape=(shape, shape, shape),
        scratch_shapes=[pltpu.VMEM((128, 128), F32), pltpu.VMEM((128, 128), F32)],
        cost_estimate=pl.CostEstimate(flops=10**9, bytes_accessed=4 * 10**6, transcendentals=0),
        name="prep",
    )(cells, vals, mask, samples, noise)


CHUNK = 1024


def products(lhs, rhs):
    halves = len(lhs[0])
    acc = None
    for half in range(halves):
        left = [x[half] for x in lhs]
        right = [x[half] for x in rhs]

        def body(i, acc, left=left, right=right):
            where = pl.ds(pl.multiple_of(i * CHUNK, CHUNK), CHUNK)
            a = jnp.concatenate([x[:, where] for x in left], axis=0)
            b = jnp.concatenate([x[:, where] for x in right], axis=0)
            a = jnp.concatenate(split3(a), axis=0).astype(BF)
            b = jnp.concatenate(split3(b), axis=0).astype(BF)
            return acc + lax.dot_general(a, b, NT, preferred_element_type=F32)

        if acc is None:
            acc = jnp.zeros((3 * ROWS * len(lhs), 3 * ROWS * len(rhs)), F32)
        acc = lax.fori_loop(0, left[0].shape[1] // CHUNK, body, acc)
    m, n = ROWS * len(lhs), ROWS * len(rhs)
    acc = acc[:m] + acc[m : 2 * m] + acc[2 * m :]
    return acc[:, :n] + acc[:, n : 2 * n] + acc[:, 2 * n :]


def pieces_of(full):
    half = full.shape[1] // 2
    return [full.at[:, :half], full.at[:, half:]]


def gram_kernel(samples, u, own, *refs):
    blocks, out = refs[:-1], refs[-1]
    blocks = [blocks[i : i + 2] for i in range(0, len(blocks), 2)]
    p = [pieces_of(own), *blocks]
    out[...] = products([pieces_of(samples), pieces_of(u), *p], p)


def last_kernel(samples, u, own, *refs):
    blocks, early, out = refs[:-2], refs[-2], refs[-1]
    blocks = [blocks[i : i + 2] for i in range(0, len(blocks), 2)]
    p = [pieces_of(own), *blocks]
    last = products([pieces_of(samples), pieces_of(u), *p], p[-1:])
    m, n = early.shape
    out[:m, :n] = early[...]
    out[:, n:] = last
    out[m:, :n] = last[2 * ROWS : m, :].T


def gram(kernel, shape, *args):
    return pl.pallas_call(
        kernel,
        out_shape=jax.ShapeDtypeStruct(shape, F32),
        cost_estimate=pl.CostEstimate(flops=10**9, bytes_accessed=4 * 10**6, transcendentals=0),
        name=kernel.__name__,
    )(*args)


def softmax(x):
    e = jnp.exp(x - jnp.max(x, axis=1, keepdims=True))
    return e / jnp.sum(e, axis=1, keepdims=True)


def final_kernel(ncell, z, base, ab, own, *refs):
    blocks, out = refs[:-1], refs[-1]
    blocks = [pieces_of(own), *[blocks[i : i + 2] for i in range(0, len(blocks), 2)]]
    n = z.shape[1]
    k0, k1 = constants(0), constants(1)
    pp = z[2 * ROWS :, :]
    eye = lax.broadcasted_iota(jnp.int32, (n, n), 0) == lax.broadcasted_iota(jnp.int32, (n, n), 1)
    norm = jnp.sum(jnp.where(eye, pp, 0.0), axis=0, keepdims=True)

    def weights(k, cross):
        dist = k["alpha"] * k["alpha"] * norm - 2.0 * k["alpha"] * cross
        return softmax(-dist / (2.0 * k["t"] * math.sqrt(ncell)))

    w0 = weights(k0, z[:ROWS, :])
    cross = z[ROWS : 2 * ROWS, :] + k0["lift"] * lax.dot_general(
        w0, pp, NN, precision=lax.Precision.HIGHEST, preferred_element_type=F32
    )
    w1 = k1["lift"] * weights(k1, cross)
    w = jnp.concatenate([w0, w1], axis=0)
    wh = w.astype(BF)
    wl = (w - wh.astype(F32)).astype(BF)
    w2 = jnp.concatenate([wh, wl], axis=0)
    half = out.shape[1] // 2
    for h in range(2):
        pieces = [b[h] for b in blocks]

        def body(i, carry, h=h, pieces=pieces):
            where = pl.ds(pl.multiple_of(i * CHUNK, CHUNK), CHUNK)
            to = pl.ds(pl.multiple_of(i * CHUNK + h * half, CHUNK), CHUNK)
            x = jnp.concatenate([b[:, where] for b in pieces], axis=0)
            xh = x.astype(BF)
            xl = (x - xh.astype(F32)).astype(BF)
            m = lax.dot_general(w2, xh, NN, preferred_element_type=F32)
            m = m[: 2 * ROWS] + m[2 * ROWS :]
            m += lax.dot_general(wh, xl, NN, preferred_element_type=F32)
            out[:, to] = base[:, to] + ab[:, to] * m[:ROWS] + m[ROWS:]
            return carry

        lax.fori_loop(0, half // CHUNK, body, 0)


def final(ncell, z, base, ab, own, blocks):
    return pl.pallas_call(
        lambda *refs: final_kernel(ncell, *refs),
        out_shape=jax.ShapeDtypeStruct(own.shape, F32),
        cost_estimate=pl.CostEstimate(flops=10**9, bytes_accessed=6 * 10**6, transcendentals=0),
        name="final",
    )(z, base, ab, own, *blocks)


def total(x, size):
    for bits in (1, 2, 6, 8, 24):
        x = x + lax.ppermute(x, "cell", [(i, i ^ bits) for i in range(size)])
    return x


def per_device(prior, samples, noise, obs_cells, obs_values, seismic_mask):
    cells = prior.shape[1]
    half = cells // 2
    size = lax.axis_size("cell")
    ncell = cells * size
    up = [(i, (i + 1) % RINGS) for i in range(RINGS)]
    down = [(i, (i - 1) % RINGS) for i in range(RINGS)]
    rising = [prior[:, :half], prior[:, half:]]
    falling = list(rising)
    blocks = []
    for hop in range(3):
        for c in range(2):
            rising[c] = lax.ppermute(rising[c], "member", up)
            falling[c] = lax.ppermute(falling[c], "member", down)
        blocks += [*rising, *falling]
    far = [lax.ppermute(rising[0], "member", up), lax.ppermute(falling[1], "member", down)]
    u, base, ab = prep(obs_cells, obs_values, seismic_mask, samples, noise)
    early = gram(gram_kernel, (72, 56), samples, u, prior, *blocks)
    blocks += far
    z = gram(last_kernel, (80, 64), samples, u, prior, *blocks, early)
    z = total(z, size)
    return final(ncell, z, base, ab, prior, blocks)


def solution(mesh):
    in_specs = (
        P("member", "cell"),
        P("member", "cell"),
        P(None, "member", "cell"),
        P(None, "cell"),
        P(None, "cell"),
        P(None, "cell"),
    )
    out_specs = P("member", "cell")
    return jax.shard_map(
        per_device, mesh=mesh, in_specs=in_specs, out_specs=out_specs, check_vma=False
    )
```

time: 347 us -> 90.8 us (0.26)
  the two profiles are of different devices: /device:TPU:1 before, /device:TPU:30 now
where the time goes in v1:
time: 90.8 us; the launch traced here: 90.6 us
  waiting for transfers between devices  34.6 us (38%)
  Pallas kernels  27 us (30%)
  starting transfers between devices  24.8 us (27%)
  local copies, waits for them, and re-layouts  2.59 us (3%)
  other arithmetic  1.43 us (2%)
    ppermute x6, starting transfers between devices, per_device(): falling[c] = lax.ppermute(falling[c], 'member', down)  20.9 us
    ppermute x5, waiting for transfers between devices, total(): x = x + lax.ppermute(x, 'cell', [(i, i ^ bits) for i in range(size)])  17.6 us
    pallas_call x2, Pallas kernels, gram(): pl.pallas_call(kernel, out_shape=jax.ShapeDtypeStruct(shape, F32), cost_e...  15.8 us
    ppermute x6, waiting for transfers between devices, per_device(): rising[c] = lax.ppermute(rising[c], 'member', up)  13.6 us
    pallas_call x1, Pallas kernels, final(): pl.pallas_call(lambda *refs: final_kernel(ncell, *refs), out_shape=jax.Sh...  6.46 us
    pallas_call x1, Pallas kernels, prep(): pl.pallas_call(prep_kernel, out_shape=(shape, shape, shape), scratch_shap...  4.76 us
    ppermute x6, waiting for transfers between devices, per_device(): falling[c] = lax.ppermute(falling[c], 'member', down)  3.45 us
    ppermute x5, starting transfers between devices, total(): x = x + lax.ppermute(x, 'cell', [(i, i ^ bits) for i in range(size)])  2.27 us
  transfers between devices with their start and end apart: 19, of which 11 were waited for; matrix products, arithmetic and copies ran while one was open for 0% of the time, Pallas kernels for 14%

profile of v1, /device:TPU:30, one launch (start us, length us, event | category | flops | bytes accessed | tf_op | source)
XLA Modules:
  0.0 90.6 jit_solution(1361089965330113291)
XLA Ops:
  0.0 1.1 %fusion = (f32[8,8192]{1,0:T(8,128)S(1)}, f32[8,8192]{1,0:T(8,128)S(1)}) fusion(f32[8,16384]{1,0:T(8,128)} %refs_3_.1), kind=kLoop, calls=%fused_computation | loop fusion | bytes 1048576 | tf_op jit(solution)/shard_map/slice | solution.py:224
  1.1 5.9 %collective-permute-start.3 = (f32[8,8192]{1,0:T(8,128)S(1)}, f32[8,8192]{1,0:T(8,128)S(1)}, u32[]{:S(2)}, u32[]{:S(2)}) collective-permute-start(f32[8,8192]{1,0:T(8,128)S(1)} %get-tuple-element.11), channel_id=1, source_target_pairs={{0,224},{32,0},{64,32},{96,64},{128,96},{160,128},{192,160},{224,1... | collective-permute-start | bytes 786440 | tf_op jit(solution)/shard_map/ppermute | solution.py:230
  7.0 0.0 collective-permute-start
  7.0 0.0 collective-permute-start.1
  7.0 3.3 %collective-permute-start.2 = (f32[8,8192]{1,0:T(8,128)S(1)}, f32[8,8192]{1,0:T(8,128)S(1)}, u32[]{:S(2)}, u32[]{:S(2)}) collective-permute-start(f32[8,8192]{1,0:T(8,128)S(1)} %get-tuple-element.12), channel_id=1, source_target_pairs={{0,224},{32,0},{64,32},{96,64},{128,96},{160,128},{192,160},{224,1... | collective-permute-start | bytes 786440 | tf_op jit(solution)/shard_map/ppermute | solution.py:230
  10.3 3.4 %collective-permute-done.3.refs_3_.refs_7_ = f32[8,8192]{1,0:T(8,128)S(1)} collective-permute-done((f32[8,8192]{1,0:T(8,128)S(1)}, f32[8,8192]{1,0:T(8,128)S(1)}, u32[]{:S(2)}, u32[]{:S(2)}) %collective-permute-start.3) | collective-permute-done | bytes 262176 | tf_op jit(solution)/shard_map/ppermute | solution.py:230
  13.7 3.7 %collective-permute-start.7 = (f32[8,8192]{1,0:T(8,128)S(1)}, f32[8,8192]{1,0:T(8,128)S(1)}, u32[]{:S(2)}, u32[]{:S(2)}) collective-permute-start(f32[8,8192]{1,0:T(8,128)S(1)} %collective-permute-done.3.refs_3_.refs_7_), channel_id=1, source_target_pairs={{0,224},{32,0},{64,32},{96,64},{128,96},{160,128},{192,160},{224,1... | collective-permute-start | bytes 786440 | tf_op jit(solution)/shard_map/ppermute | solution.py:230
  17.4 0.0 collective-permute-done.refs_0_.refs_4_
  17.4 0.0 collective-permute-start.4
  17.4 5.6 %collective-permute-done.1.refs_1_.refs_5_ = f32[8,8192]{1,0:T(8,128)S(1)} collective-permute-done((f32[8,8192]{1,0:T(8,128)S(1)}, f32[8,8192]{1,0:T(8,128)S(1)}, u32[]{:S(2)}, u32[]{:S(2)}) %collective-permute-start.1) | collective-permute-done | bytes 262176 | tf_op jit(solution)/shard_map/ppermute | solution.py:229
  23.1 0.0 collective-permute-start.5
  23.1 0.0 collective-permute-done.2.refs_2_.refs_6_
  23.1 3.2 %collective-permute-start.6 = (f32[8,8192]{1,0:T(8,128)S(1)}, f32[8,8192]{1,0:T(8,128)S(1)}, u32[]{:S(2)}, u32[]{:S(2)}) collective-permute-start(f32[8,8192]{1,0:T(8,128)S(1)} %collective-permute-done.2.refs_2_.refs_6_), channel_id=1, source_target_pairs={{0,224},{32,0},{64,32},{96,64},{128,96},{160,128},{192,160},{224,1... | collective-permute-start | bytes 786440 | tf_op jit(solution)/shard_map/ppermute | solution.py:230
  26.3 0.0 collective-permute-done.7.refs_7_.refs_11_
  26.3 1.6 %collective-permute-start.11 = (f32[8,8192]{1,0:T(8,128)S(1)}, f32[8,8192]{1,0:T(8,128)S(1)}, u32[]{:S(2)}, u32[]{:S(2)}) collective-permute-start(f32[8,8192]{1,0:T(8,128)S(1)} %collective-permute-done.7.refs_7_.refs_11_), channel_id=1, source_target_pairs={{0,224},{32,0},{64,32},{96,64},{128,96},{160,128},{192,160},{224,1... | collective-permute-start | bytes 786440 | tf_op jit(solution)/shard_map/ppermute | solution.py:230
  27.9 0.8 collective-permute-done.4.refs_4_.refs_8_
  28.7 0.0 collective-permute-start.8
  28.7 5.6 %collective-permute-done.5.refs_5_.refs_9_ = f32[8,8192]{1,0:T(8,128)S(1)} collective-permute-done((f32[8,8192]{1,0:T(8,128)S(1)}, f32[8,8192]{1,0:T(8,128)S(1)}, u32[]{:S(2)}, u32[]{:S(2)}) %collective-permute-start.5) | collective-permute-done | bytes 262176 | tf_op jit(solution)/shard_map/ppermute | solution.py:229
  34.3 0.0 collective-permute-start.9
  34.3 0.0 collective-permute-done.6.refs_6_.refs_10_
  34.3 3.2 %collective-permute-start.10 = (f32[8,8192]{1,0:T(8,128)S(1)}, f32[8,8192]{1,0:T(8,128)S(1)}, u32[]{:S(2)}, u32[]{:S(2)}) collective-permute-start(f32[8,8192]{1,0:T(8,128)S(1)} %collective-permute-done.6.refs_6_.refs_10_), channel_id=1, source_target_pairs={{0,224},{32,0},{64,32},{96,64},{128,96},{160,128},{192,160},{224,1... | collective-permute-start | bytes 786440 | tf_op jit(solution)/shard_map/ppermute | solution.py:230
  37.5 0.0 collective-permute-done.11.refs_11_.refs_15_
  37.5 1.6 %collective-permute-start.13 = (f32[8,8192]{1,0:T(8,128)S(1)}, f32[8,8192]{1,0:T(8,128)S(1)}, u32[]{:S(2)}, u32[]{:S(2)}) collective-permute-start(f32[8,8192]{1,0:T(8,128)S(1)} %collective-permute-done.11.refs_11_.refs_15_), channel_id=1, source_target_pairs={{0,224},{32,0},{64,32},{96,64},{128,96},{160,128},{192,160},{224,1... | collective-permute-start | bytes 786440 | tf_op jit(solution)/shard_map/ppermute | solution.py:232
  39.1 0.8 collective-permute-done.8.refs_8_.refs_12_
  39.9 0.0 collective-permute-start.12
  39.9 4.8 %prep.1 = (f32[8,16384]{1,0:T(8,128)}, f32[8,16384]{1,0:T(8,128)}, f32[8,16384]{1,0:T(8,128)}) custom-call(s32[2,2048]{1,0:T(2,128)} %cells.1, f32[2,2048]{1,0:T(2,128)} %vals.1, s32[2,128]{1,0:T(2,128)} %mask.1, f32[8,16384]{1,0:T(8,128)} %samples.5, f32[2,8,16384]{2,1,0:T(8,128)} %noise.1), custom_call_target="tpu_custom_call" | custom-call | flops 1000000000 | bytes 4000000 | tf_op jit(solution)/shard_map/prep/pallas_call | solution.py:89
  44.8 0.8 collective-permute-done.9.refs_9_.refs_13_
  45.5 0.0 collective-permute-done.10.refs_10_.refs_14_
  45.5 0.7 copy-done.10
  46.2 0.1 copy-done.11
  46.3 7.9 %gram_kernel.1.refs_14_ = f32[72,56]{1,0:T(8,128)} custom-call(f32[8,16384]{1,0:T(8,128)} %samples.5, f32[8,16384]{1,0:T(8,128)} %get-tuple-element.8.u, f32[8,16384]{1,0:T(8,128)} %refs_3_.1, f32[8,8192]{1,0:T(8,128)} %copy-done.1, f32[8,8192]{1,0:T(8,128)} %copy-done.2, f32[8,8192]{1,0:T(8,128)} %copy-done.3, f32[8,8192]{1,0:T(8,128)} %copy-done, ...), custom_call_target="tpu_custom_call" | custom-call | flops 1000000000 | bytes 4000000 | tf_op jit(solution)/shard_map/gram_kernel/pallas_call | solution.py:148
  54.3 0.0 collective-permute-done.13.refs_13_.refs_17_
  54.3 0.0 collective-permute-done.12.refs_12_.refs_16_
  54.3 0.7 copy-done.12
  55.0 7.8 %last_kernel.1 = f32[80,64]{1,0:T(8,128)} custom-call(f32[8,16384]{1,0:T(8,128)} %samples.5, f32[8,16384]{1,0:T(8,128)} %get-tuple-element.8.u, f32[8,16384]{1,0:T(8,128)} %refs_3_.1, f32[8,8192]{1,0:T(8,128)} %copy-done.1, f32[8,8192]{1,0:T(8,128)} %copy-done.2, f32[8,8192]{1,0:T(8,128)} %copy-done.3, f32[8,8192]{1,0:T(8,128)} %copy-done, ...), custom_call_target="tpu_custom_call" | custom-call | flops 1000000000 | bytes 4000000 | tf_op jit(solution)/shard_map/last_kernel/pallas_call | solution.py:148
  62.8 0.0 collective-permute-start.14
  62.8 1.4 %collective-permute-done.14 = f32[80,64]{1,0:T(8,128)S(1)} collective-permute-done((f32[80,64]{1,0:T(8,128)}, f32[80,64]{1,0:T(8,128)S(1)}, u32[]{:S(2)}, u32[]{:S(2)}) %collective-permute-start.14) | collective-permute-done | bytes 20512 | tf_op jit(solution)/shard_map/ppermute | solution.py:213
  64.3 0.8 add.15
  65.0 0.7 collective-permute-start.15
  65.8 3.3 %collective-permute-done.15 = f32[80,64]{1,0:T(8,128)S(1)} collective-permute-done((f32[80,64]{1,0:T(8,128)S(1)}, f32[80,64]{1,0:T(8,128)S(1)}, u32[]{:S(2)}, u32[]{:S(2)}) %collective-permute-start.15) | collective-permute-done | bytes 20512 | tf_op jit(solution)/shard_map/ppermute | solution.py:213
  69.1 0.2 collective-permute-start.16
  69.3 5.0 %collective-permute-done.16 = f32[80,64]{1,0:T(8,128)S(1)} collective-permute-done((f32[80,64]{1,0:T(8,128)S(1)}, f32[80,64]{1,0:T(8,128)S(1)}, u32[]{:S(2)}, u32[]{:S(2)}) %collective-permute-start.16) | collective-permute-done | bytes 20512 | tf_op jit(solution)/shard_map/ppermute | solution.py:213
  74.3 0.8 collective-permute-start.17
  75.1 3.2 %collective-permute-done.17 = f32[80,64]{1,0:T(8,128)S(1)} collective-permute-done((f32[80,64]{1,0:T(8,128)S(1)}, f32[80,64]{1,0:T(8,128)S(1)}, u32[]{:S(2)}, u32[]{:S(2)}) %collective-permute-start.17) | collective-permute-done | bytes 20512 | tf_op jit(solution)/shard_map/ppermute | solution.py:213
  78.3 0.5 collective-permute-start.18
  78.8 4.7 %collective-permute-done.18 = f32[80,64]{1,0:T(8,128)S(1)} collective-permute-done((f32[80,64]{1,0:T(8,128)S(1)}, f32[80,64]{1,0:T(8,128)S(1)}, u32[]{:S(2)}, u32[]{:S(2)}) %collective-permute-start.18) | collective-permute-done | bytes 20512 | tf_op jit(solution)/shard_map/ppermute | solution.py:213
  83.5 0.6 add.19.refs_0_
  84.1 6.5 %final.1 = f32[8,16384]{1,0:T(8,128)} custom-call(f32[80,64]{1,0:T(8,128)} %add.19.refs_0_, f32[8,16384]{1,0:T(8,128)} %get-tuple-element.9.refs_1_, f32[8,16384]{1,0:T(8,128)} %get-tuple-element.10.refs_2_, f32[8,16384]{1,0:T(8,128)} %refs_3_.1, f32[8,8192]{1,0:T(8,128)} %copy-done.1, f32[8,8192]{1,0:T(8,128)} %copy-done.2, f32[8,8192]{1,0:T(8,128)} %copy-done.3, ...), custom_call_target="tpu_custom_call" | custom-call | flops 1000000000 | bytes 6000000 | tf_op jit(solution)/shard_map/final/pallas_call | solution.py:203
  (26 shorter events, 0.1 us)
Async XLA Ops:
  1.1 12.6 %collective-permute-start.3 = (f32[8,8192]{1,0:T(8,128)S(1)}, f32[8,8192]{1,0:T(8,128)S(1)}, u32[]{:S(2)}, u32[]{:S(2)}) collective-permute-start(f32[8,8192]{1,0:T(8,128)S(1)} %get-tuple-element.11), channel_id=1, source_target_pairs={{0,224},{32,0},{64,32},{96,64},{128,96},{160,128},{192,160},{224,1... | collective-permute-start | bytes 786440 | tf_op jit(solution)/shard_map/ppermute | solution.py:230
  7.0 10.4 %collective-permute-start = (f32[8,8192]{1,0:T(8,128)S(1)}, f32[8,8192]{1,0:T(8,128)S(1)}, u32[]{:S(2)}, u32[]{:S(2)}) collective-permute-start(f32[8,8192]{1,0:T(8,128)S(1)} %get-tuple-element.12), channel_id=1, source_target_pairs={{0,32},{32,64},{64,96},{96,128},{128,160},{160,192},{192,224},{224... | collective-permute-start | bytes 786440 | tf_op jit(solution)/shard_map/ppermute | solution.py:229
  7.0 16.1 %collective-permute-start.1 = (f32[8,8192]{1,0:T(8,128)S(1)}, f32[8,8192]{1,0:T(8,128)S(1)}, u32[]{:S(2)}, u32[]{:S(2)}) collective-permute-start(f32[8,8192]{1,0:T(8,128)S(1)} %get-tuple-element.11), channel_id=1, source_target_pairs={{0,32},{32,64},{64,96},{96,128},{128,160},{160,192},{192,224},{224... | collective-permute-start | bytes 786440 | tf_op jit(solution)/shard_map/ppermute | solution.py:229
  7.0 16.1 %collective-permute-start.2 = (f32[8,8192]{1,0:T(8,128)S(1)}, f32[8,8192]{1,0:T(8,128)S(1)}, u32[]{:S(2)}, u32[]{:S(2)}) collective-permute-start(f32[8,8192]{1,0:T(8,128)S(1)} %get-tuple-element.12), channel_id=1, source_target_pairs={{0,224},{32,0},{64,32},{96,64},{128,96},{160,128},{192,160},{224,1... | collective-permute-start | bytes 786440 | tf_op jit(solution)/shard_map/ppermute | solution.py:230
  13.7 31.0 %copy-start = (f32[8,8192]{1,0:T(8,128)}, f32[8,8192]{1,0:T(8,128)S(1)}, u32[]{:S(2)}) copy-start(f32[8,8192]{1,0:T(8,128)S(1)} %collective-permute-done.3.refs_3_.refs_7_) | copy-start | bytes 786436
  13.7 12.6 %collective-permute-start.7 = (f32[8,8192]{1,0:T(8,128)S(1)}, f32[8,8192]{1,0:T(8,128)S(1)}, u32[]{:S(2)}, u32[]{:S(2)}) collective-permute-start(f32[8,8192]{1,0:T(8,128)S(1)} %collective-permute-done.3.refs_3_.refs_7_), channel_id=1, source_target_pairs={{0,224},{32,0},{64,32},{96,64},{128,96},{160,128},{192,160},{224,1... | collective-permute-start | bytes 786440 | tf_op jit(solution)/shard_map/ppermute | solution.py:230
  17.4 27.2 %copy-start.1 = (f32[8,8192]{1,0:T(8,128)}, f32[8,8192]{1,0:T(8,128)S(1)}, u32[]{:S(2)}) copy-start(f32[8,8192]{1,0:T(8,128)S(1)} %collective-permute-done.refs_0_.refs_4_) | copy-start | bytes 786436
  17.4 11.2 %collective-permute-start.4 = (f32[8,8192]{1,0:T(8,128)S(1)}, f32[8,8192]{1,0:T(8,128)S(1)}, u32[]{:S(2)}, u32[]{:S(2)}) collective-permute-start(f32[8,8192]{1,0:T(8,128)S(1)} %collective-permute-done.refs_0_.refs_4_), channel_id=1, source_target_pairs={{0,32},{32,64},{64,96},{96,128},{128,160},{160,192},{192,224},{224... | collective-permute-start | bytes 786440 | tf_op jit(solution)/shard_map/ppermute | solution.py:229
  23.1 21.6 %copy-start.2 = (f32[8,8192]{1,0:T(8,128)}, f32[8,8192]{1,0:T(8,128)S(1)}, u32[]{:S(2)}) copy-start(f32[8,8192]{1,0:T(8,128)S(1)} %collective-permute-done.1.refs_1_.refs_5_) | copy-start | bytes 786436
  23.1 11.2 %collective-permute-start.5 = (f32[8,8192]{1,0:T(8,128)S(1)}, f32[8,8192]{1,0:T(8,128)S(1)}, u32[]{:S(2)}, u32[]{:S(2)}) collective-permute-start(f32[8,8192]{1,0:T(8,128)S(1)} %collective-permute-done.1.refs_1_.refs_5_), channel_id=1, source_target_pairs={{0,32},{32,64},{64,96},{96,128},{128,160},{160,192},{192,224},{224... | collective-permute-start | bytes 786440 | tf_op jit(solution)/shard_map/ppermute | solution.py:229
  23.1 21.6 %copy-start.3 = (f32[8,8192]{1,0:T(8,128)}, f32[8,8192]{1,0:T(8,128)S(1)}, u32[]{:S(2)}) copy-start(f32[8,8192]{1,0:T(8,128)S(1)} %collective-permute-done.2.refs_2_.refs_6_) | copy-start | bytes 786436
  23.1 11.2 %collective-permute-start.6 = (f32[8,8192]{1,0:T(8,128)S(1)}, f32[8,8192]{1,0:T(8,128)S(1)}, u32[]{:S(2)}, u32[]{:S(2)}) collective-permute-start(f32[8,8192]{1,0:T(8,128)S(1)} %collective-permute-done.2.refs_2_.refs_6_), channel_id=1, source_target_pairs={{0,224},{32,0},{64,32},{96,64},{128,96},{160,128},{192,160},{224,1... | collective-permute-start | bytes 786440 | tf_op jit(solution)/shard_map/ppermute | solution.py:230
  26.3 18.4 %copy-start.4 = (f32[8,8192]{1,0:T(8,128)}, f32[8,8192]{1,0:T(8,128)S(1)}, u32[]{:S(2)}) copy-start(f32[8,8192]{1,0:T(8,128)S(1)} %collective-permute-done.7.refs_7_.refs_11_) | copy-start | bytes 786436
  26.3 11.2 %collective-permute-start.11 = (f32[8,8192]{1,0:T(8,128)S(1)}, f32[8,8192]{1,0:T(8,128)S(1)}, u32[]{:S(2)}, u32[]{:S(2)}) collective-permute-start(f32[8,8192]{1,0:T(8,128)S(1)} %collective-permute-done.7.refs_7_.refs_11_), channel_id=1, source_target_pairs={{0,224},{32,0},{64,32},{96,64},{128,96},{160,128},{192,160},{224,1... | collective-permute-start | bytes 786440 | tf_op jit(solution)/shard_map/ppermute | solution.py:230
  28.7 16.0 %copy-start.5 = (f32[8,8192]{1,0:T(8,128)}, f32[8,8192]{1,0:T(8,128)S(1)}, u32[]{:S(2)}) copy-start(f32[8,8192]{1,0:T(8,128)S(1)} %collective-permute-done.4.refs_4_.refs_8_) | copy-start | bytes 786436
  28.7 11.2 %collective-permute-start.8 = (f32[8,8192]{1,0:T(8,128)S(1)}, f32[8,8192]{1,0:T(8,128)S(1)}, u32[]{:S(2)}, u32[]{:S(2)}) collective-permute-start(f32[8,8192]{1,0:T(8,128)S(1)} %collective-permute-done.4.refs_4_.refs_8_), channel_id=1, source_target_pairs={{0,32},{32,64},{64,96},{96,128},{128,160},{160,192},{192,224},{224... | collective-permute-start | bytes 786440 | tf_op jit(solution)/shard_map/ppermute | solution.py:229
  34.3 10.4 %copy-start.6 = (f32[8,8192]{1,0:T(8,128)}, f32[8,8192]{1,0:T(8,128)S(1)}, u32[]{:S(2)}) copy-start(f32[8,8192]{1,0:T(8,128)S(1)} %collective-permute-done.5.refs_5_.refs_9_) | copy-start | bytes 786436
  34.3 11.2 %collective-permute-start.9 = (f32[8,8192]{1,0:T(8,128)S(1)}, f32[8,8192]{1,0:T(8,128)S(1)}, u32[]{:S(2)}, u32[]{:S(2)}) collective-permute-start(f32[8,8192]{1,0:T(8,128)S(1)} %collective-permute-done.5.refs_5_.refs_9_), channel_id=1, source_target_pairs={{0,32},{32,64},{64,96},{96,128},{128,160},{160,192},{192,224},{224... | collective-permute-start | bytes 786440 | tf_op jit(solution)/shard_map/ppermute | solution.py:229
  34.3 10.4 %copy-start.7 = (f32[8,8192]{1,0:T(8,128)}, f32[8,8192]{1,0:T(8,128)S(1)}, u32[]{:S(2)}) copy-start(f32[8,8192]{1,0:T(8,128)S(1)} %collective-permute-done.6.refs_6_.refs_10_) | copy-start | bytes 786436
  34.3 11.2 %collective-permute-start.10 = (f32[8,8192]{1,0:T(8,128)S(1)}, f32[8,8192]{1,0:T(8,128)S(1)}, u32[]{:S(2)}, u32[]{:S(2)}) collective-permute-start(f32[8,8192]{1,0:T(8,128)S(1)} %collective-permute-done.6.refs_6_.refs_10_), channel_id=1, source_target_pairs={{0,224},{32,0},{64,32},{96,64},{128,96},{160,128},{192,160},{224,1... | collective-permute-start | bytes 786440 | tf_op jit(solution)/shard_map/ppermute | solution.py:230
  37.5 7.2 %copy-start.8 = (f32[8,8192]{1,0:T(8,128)}, f32[8,8192]{1,0:T(8,128)S(1)}, u32[]{:S(2)}) copy-start(f32[8,8192]{1,0:T(8,128)S(1)} %collective-permute-done.11.refs_11_.refs_15_) | copy-start | bytes 786436
  37.5 16.7 %collective-permute-start.13 = (f32[8,8192]{1,0:T(8,128)S(1)}, f32[8,8192]{1,0:T(8,128)S(1)}, u32[]{:S(2)}, u32[]{:S(2)}) collective-permute-start(f32[8,8192]{1,0:T(8,128)S(1)} %collective-permute-done.11.refs_11_.refs_15_), channel_id=1, source_target_pairs={{0,224},{32,0},{64,32},{96,64},{128,96},{160,128},{192,160},{224,1... | collective-permute-start | bytes 786440 | tf_op jit(solution)/shard_map/ppermute | solution.py:232
  39.9 4.8 %copy-start.9 = (f32[8,8192]{1,0:T(8,128)}, f32[8,8192]{1,0:T(8,128)S(1)}, u32[]{:S(2)}) copy-start(f32[8,8192]{1,0:T(8,128)S(1)} %collective-permute-done.8.refs_8_.refs_12_) | copy-start | bytes 786436
  39.9 14.4 %collective-permute-start.12 = (f32[8,8192]{1,0:T(8,128)S(1)}, f32[8,8192]{1,0:T(8,128)}, u32[]{:S(2)}, u32[]{:S(2)}) collective-permute-start(f32[8,8192]{1,0:T(8,128)S(1)} %collective-permute-done.8.refs_8_.refs_12_), channel_id=1, source_target_pairs={{0,32},{32,64},{64,96},{96,128},{128,160},{160,192},{192,224},{224... | collective-permute-start | bytes 786440 | tf_op jit(solution)/shard_map/ppermute | solution.py:232
  45.5 0.7 copy-start.10
  45.5 0.8 copy-start.11
  54.3 0.7 copy-start.12
  62.8 1.4 %collective-permute-start.14 = (f32[80,64]{1,0:T(8,128)}, f32[80,64]{1,0:T(8,128)S(1)}, u32[]{:S(2)}, u32[]{:S(2)}) collective-permute-start(f32[80,64]{1,0:T(8,128)} %last_kernel.1), channel_id=1, source_target_pairs={{0,1},{1,0},{2,3},{3,2},{4,5},{5,4},{6,7},{7,6},{8,9},{9,8},{10,11... | collective-permute-start | bytes 61448 | tf_op jit(solution)/shard_map/ppermute | solution.py:213
  65.0 4.0 %collective-permute-start.15 = (f32[80,64]{1,0:T(8,128)S(1)}, f32[80,64]{1,0:T(8,128)S(1)}, u32[]{:S(2)}, u32[]{:S(2)}) collective-permute-start(f32[80,64]{1,0:T(8,128)S(1)} %add.15), channel_id=1, source_target_pairs={{0,2},{1,3},{2,0},{3,1},{4,6},{5,7},{6,4},{7,5},{8,10},{9,11},{10,... | collective-permute-start | bytes 61448 | tf_op jit(solution)/shard_map/ppermute | solution.py:213
  69.1 5.2 %collective-permute-start.16 = (f32[80,64]{1,0:T(8,128)S(1)}, f32[80,64]{1,0:T(8,128)S(1)}, u32[]{:S(2)}, u32[]{:S(2)}) collective-permute-start(f32[80,64]{1,0:T(8,128)S(1)} %add.16), channel_id=1, source_target_pairs={{0,6},{1,7},{2,4},{3,5},{4,2},{5,3},{6,0},{7,1},{8,14},{9,15},{10,... | collective-permute-start | bytes 61448 | tf_op jit(solution)/shard_map/ppermute | solution.py:213
  74.3 4.0 %collective-permute-start.17 = (f32[80,64]{1,0:T(8,128)S(1)}, f32[80,64]{1,0:T(8,128)S(1)}, u32[]{:S(2)}, u32[]{:S(2)}) collective-permute-start(f32[80,64]{1,0:T(8,128)S(1)} %add.17), channel_id=1, source_target_pairs={{0,8},{1,9},{2,10},{3,11},{4,12},{5,13},{6,14},{7,15},{8,0},{9,1},... | collective-permute-start | bytes 61448 | tf_op jit(solution)/shard_map/ppermute | solution.py:213
  78.3 5.2 %collective-permute-start.18 = (f32[80,64]{1,0:T(8,128)S(1)}, f32[80,64]{1,0:T(8,128)S(1)}, u32[]{:S(2)}, u32[]{:S(2)}) collective-permute-start(f32[80,64]{1,0:T(8,128)S(1)} %add.18), channel_id=1, source_target_pairs={{0,24},{1,25},{2,26},{3,27},{4,28},{5,29},{6,30},{7,31},{8,16},{9,... | collective-permute-start | bytes 61448 | tf_op jit(solution)/shard_map/ppermute | solution.py:213

commit v2 on v1

v2 whole, which is shorter than its diff:
```python
import math

import jax
import jax.numpy as jnp
from jax import lax
from jax.experimental import pallas as pl
from jax.experimental.pallas import tpu as pltpu
from jax.sharding import PartitionSpec as P

STEPS = 2
RINGS = 8
ROWS = 8
BF = jnp.bfloat16
F32 = jnp.float32
NT = (((1,), (1,)), ((), ()))
NN = (((1,), (0,)), ((), ()))


def constants(step):
    t = 0.6 - 0.1 * step
    alpha = 1.0 - 0.95 * t
    drift = -0.95 / alpha
    diffusion = 1.0 - 2.0 * drift * t
    return dict(
        t=t,
        alpha=alpha,
        gain=1.0 - 0.1 * drift - 0.1 * diffusion / t,
        pull=0.1 * diffusion * (1.0 - t),
        lift=0.1 * diffusion * alpha / t,
        kick=math.sqrt(0.1 * diffusion),
    )


def split3(x):
    a = x.astype(BF).astype(F32)
    r = x - a
    b = r.astype(BF).astype(F32)
    return a, b, r - b


def prep_kernel(cells, vals, mask, samples, noise, u_ref, base_ref, ab_ref, prec, targ):
    width = prec.shape[0]
    obs = cells.shape[1]
    rows = lax.broadcasted_iota(jnp.int32, (width, obs), 0)
    eye = lax.broadcasted_iota(jnp.int32, (width, width), 0) == lax.broadcasted_iota(
        jnp.int32, (width, width), 1
    )
    p_sum = jnp.zeros((width, width), F32)
    t_sum = jnp.zeros((width, width), F32)
    for s in range(cells.shape[0]):
        local = cells[s : s + 1, :] & (width * width - 1)
        high = jnp.where(rows == (local >> 7), 1.0, 0.0).astype(BF)
        low = rows == (local & 127)
        pieces = [jnp.ones((1, obs), F32), *split3(vals[s : s + 1, :])]
        sums = [
            lax.dot_general(
                high, jnp.where(low, piece, 0.0).astype(BF), NT, preferred_element_type=F32
            )
            for piece in pieces
        ]
        flags = mask[s : s + 1, :].astype(F32)
        flags = jnp.sum(jnp.where(eye, flags, 0.0), axis=1, keepdims=True)
        p_sum += flags * sums[0]
        t_sum += flags * (sums[1] + sums[2] + sums[3])
    prec[...] = p_sum
    targ[...] = t_sum
    k0, k1 = constants(0), constants(1)

    def body(h, carry):
        where = pl.ds(pl.multiple_of(h * width, width), width)
        p = prec[pl.ds(h, 1), :]
        t = targ[pl.ds(h, 1), :]
        u = (
            (k0["gain"] - k0["pull"] * p) * samples[:, where]
            + k0["pull"] * t
            + k0["kick"] * noise[0, :, where]
        )
        a1 = k1["gain"] - k1["pull"] * p
        u_ref[:, where] = u
        base_ref[:, where] = a1 * u + k1["pull"] * t + k1["kick"] * noise[1, :, where]
        ab_ref[:, where] = jnp.broadcast_to(k0["lift"] * a1, (ROWS, width))
        return carry

    lax.fori_loop(0, width, body, 0, unroll=4)


def prep(cells, vals, mask, samples, noise):
    shape = jax.ShapeDtypeStruct(samples.shape, F32)
    scratch = [pltpu.VMEM((128, 128), F32), pltpu.VMEM((128, 128), F32)]
    args = (cells, vals, mask, samples, noise)
    return call(prep_kernel, (shape, shape, shape), args, 10**9, scratch, name="prep")


CHUNK = 4096
LIMIT = pltpu.CompilerParams(vmem_limit_bytes=16 << 20)


def call(kernel, out_shape, args, flops, scratch=(), **kw):
    vmem = pl.BlockSpec(memory_space=pltpu.VMEM)
    return pl.pallas_call(
        kernel,
        out_shape=out_shape,
        in_specs=[vmem] * len(args),
        out_specs=jax.tree.map(lambda _: vmem, out_shape),
        scratch_shapes=scratch,
        compiler_params=LIMIT,
        cost_estimate=pl.CostEstimate(flops=flops, bytes_accessed=4 * 10**6, transcendentals=0),
        **kw,
    )(*args)


def split2(x):
    high = x.astype(BF).astype(F32)
    return jnp.concatenate([high, x - high], axis=0).astype(BF)


def column_chunks(blocks, body, acc):
    done = 0
    for pieces in zip(*blocks, strict=True):
        width = pieces[0].shape[1]
        for start in range(0, width, CHUNK):
            x = jnp.concatenate([p[:, start : start + CHUNK] for p in pieces], axis=0)
            acc = body(slice(done + start, done + start + CHUNK), x, acc)
        done += width
    return acc


def halves(full):
    half = full.shape[1] // 2
    return [full.at[:, :half], full.at[:, half:]]


def fold(z, m, n):
    z = z[:m] + z[m:]
    return z[:, :n] + z[:, n:]


def early_kernel(own, *refs):
    blocks, samples, u, z, stack = refs[:-4], *refs[-4:]
    blocks = [blocks[i : i + 2] for i in range(0, len(blocks), 2)]
    blocks = [halves(own), *blocks, halves(samples), halves(u)]

    def body(where, x, acc):
        y = split2(x)
        stack[:, where] = y
        return acc + lax.dot_general(y, y, NT, preferred_element_type=F32)

    rows = ROWS * len(blocks)
    acc = column_chunks(blocks, body, jnp.zeros((2 * rows, 2 * rows), F32))
    z[...] = fold(acc, rows, rows)[:, : rows - 2 * ROWS]


def early(samples, u, own, blocks):
    rows = ROWS * (3 + len(blocks) // 2)
    shapes = (
        jax.ShapeDtypeStruct((rows, rows - 2 * ROWS), F32),
        jax.ShapeDtypeStruct((2 * rows, own.shape[1]), BF),
    )
    return call(early_kernel, shapes, (own, *blocks, samples, u), 10**9, name="early")


def last_kernel(*refs):
    blocks, z1, stack, z, tail = refs[:-4], *refs[-4:]
    blocks = [blocks[i : i + 2] for i in range(0, len(blocks), 2)]
    new, old = ROWS * len(blocks), stack.shape[0] // 2

    def body(where, x, acc):
        y = split2(x)
        tail[:, where] = y
        a = jnp.concatenate([stack[:, where], y], axis=0)
        return acc + lax.dot_general(y, a, NT, preferred_element_type=F32)

    acc = column_chunks(blocks, body, jnp.zeros((2 * new, 2 * (old + new)), F32))
    acc = acc[:new] + acc[new:]
    left = acc[:, :old] + acc[:, old : 2 * old]
    right = acc[:, 2 * old : 2 * old + new] + acc[:, 2 * old + new :]
    m, n = z1.shape
    z[:m, :n] = z1[...]
    z[m:, :n] = left[:, :n]
    z[:m, n:] = left.T
    z[m:, n:] = right


def last(blocks, z1, stack):
    new = ROWS * (len(blocks) // 2)
    m, n = z1.shape
    shapes = (
        jax.ShapeDtypeStruct((m + new, n + new), F32),
        jax.ShapeDtypeStruct((2 * new, stack.shape[1]), BF),
    )
    return call(last_kernel, shapes, (*blocks, z1, stack), 10**9, name="last")


def softmax(x):
    e = jnp.exp(x - jnp.max(x, axis=1, keepdims=True))
    return e / jnp.sum(e, axis=1, keepdims=True)


def final_kernel(ncell, z_all, stack, tail, base, ab, out):
    z = z_all[0]
    for i in range(1, z_all.shape[0]):
        z = z + z_all[i]
    n = z.shape[1]
    old, new = stack.shape[0] // 2, tail.shape[0] // 2
    first = old - 2 * ROWS
    k0, k1 = constants(0), constants(1)
    pp = jnp.concatenate([z[:first], z[old:]], axis=0)
    eye = lax.broadcasted_iota(jnp.int32, (n, n), 0) == lax.broadcasted_iota(jnp.int32, (n, n), 1)
    norm = jnp.sum(jnp.where(eye, pp, 0.0), axis=0, keepdims=True)

    def weights(k, cross):
        dist = k["alpha"] * k["alpha"] * norm - 2.0 * k["alpha"] * cross
        return softmax(-dist / (2.0 * k["t"] * math.sqrt(ncell)))

    w0 = weights(k0, z[first : first + ROWS])
    cross = z[first + ROWS : old] + k0["lift"] * lax.dot_general(
        w0, pp, NN, precision=lax.Precision.HIGHEST, preferred_element_type=F32
    )
    w1 = k1["lift"] * weights(k1, cross)
    w = jnp.concatenate([w0, w1], axis=0)
    wh = w.astype(BF)
    w2 = jnp.concatenate([wh, (w - wh.astype(F32)).astype(BF)], axis=0)
    width = out.shape[1] // 2
    for start in range(0, out.shape[1], width):
        to = slice(start, start + width)
        high = jnp.concatenate([stack[:first, to], tail[:new, to]], axis=0)
        low = jnp.concatenate([stack[old : old + first, to], tail[new:, to]], axis=0)
        m = lax.dot_general(w2, high, NN, preferred_element_type=F32)
        m = m[: 2 * ROWS] + m[2 * ROWS :]
        m += lax.dot_general(wh, low, NN, preferred_element_type=F32)
        out[:, to] = base[:, to] + ab[:, to] * m[:ROWS] + m[ROWS:]


def final(ncell, z_all, stack, tail, base, ab):
    def final(*refs):
        return final_kernel(ncell, *refs)

    shape = jax.ShapeDtypeStruct(base.shape, F32)
    return call(final, shape, (z_all, stack, tail, base, ab), 10**9, name="final")


def per_device(prior, samples, noise, obs_cells, obs_values, seismic_mask):
    cells = prior.shape[1]
    half = cells // 2
    planes = lax.axis_size("x") * lax.axis_size("y")
    ncell = cells * planes * lax.axis_size("core")
    up = [(i, (i + 1) % RINGS) for i in range(RINGS)]
    down = [(i, (i - 1) % RINGS) for i in range(RINGS)]
    rising = [prior[:, :half], prior[:, half:]]
    falling = list(rising)
    blocks = []
    for hop in range(3):
        if hop == 2:
            rising[0], u = lax.optimization_barrier((rising[0], u))
        for c in range(2):
            rising[c] = lax.ppermute(rising[c], "member", up)
            falling[c] = lax.ppermute(falling[c], "member", down)
        blocks += [*rising, *falling]
        if hop == 0:
            rising[0], samples = lax.optimization_barrier((rising[0], samples))
            u, base, ab = prep(obs_cells, obs_values, seismic_mask, samples, noise)
    far = [lax.ppermute(rising[0], "member", up), lax.ppermute(falling[1], "member", down)]
    z1, stack = early(samples, u, prior, blocks[:8])
    z, tail = last((*blocks[8:], *far), z1, stack)
    z = z + lax.ppermute(z, "core", [(0, 1), (1, 0)])
    z = jnp.broadcast_to(z[None], (planes, *z.shape))
    z = lax.all_to_all(z, ("x", "y"), split_axis=0, concat_axis=0, tiled=True)
    return final(ncell, z, stack, tail, base, ab)


def solution(mesh):
    mesh = jax.sharding.Mesh(mesh.devices.reshape(RINGS, 4, 4, 2), ("member", "x", "y", "core"))
    cell = ("x", "y", "core")
    in_specs = (
        P("member", cell),
        P("member", cell),
        P(None, "member", cell),
        P(None, cell),
        P(None, cell),
        P(None, cell),
    )
    return jax.shard_map(
        per_device, mesh=mesh, in_specs=in_specs, out_specs=P("member", cell), check_vma=False
    )
```

time: 90.8 us -> 78 us (0.86)
  the two profiles are of different devices: /device:TPU:30 before, /device:TPU:1 now
where the time goes in v2:
time: 78 us; the launch traced here: 76.9 us
  starting transfers between devices  26.4 us (34%)
  blocking collectives  17 us (22%)
  waiting for transfers between devices  15.3 us (20%)
  local copies, waits for them, and re-layouts  10.8 us (14%)
  Pallas kernels  7.44 us (10%)
    ppermute x6, starting transfers between devices, per_device(): falling[c] = lax.ppermute(falling[c], 'member', down)  17.4 us
    all_to_all x1, blocking collectives, per_device(): z = lax.all_to_all(z, ('x', 'y'), split_axis=0, concat_axis=0, tiled=True)  17 us
    ppermute x6, waiting for transfers between devices, per_device(): rising[c] = lax.ppermute(rising[c], 'member', up)  8.75 us
    unnamed x18, local copies, waits for them, and re-layouts  8.21 us
    pallas_call x4, Pallas kernels, call(): pl.pallas_call(kernel, out_shape=out_shape, in_specs=[vmem] * len(args),...  7.44 us
    ppermute x1, waiting for transfers between devices, per_device(): lax.ppermute(rising[0], 'member', up)  5.61 us
    ppermute x1, starting transfers between devices, per_device(): z = z + lax.ppermute(z, 'core', [(0, 1), (1, 0)])  3.66 us
    ppermute x1, starting transfers between devices, per_device(): lax.ppermute(falling[1], 'member', down)  2.67 us
  transfers between devices with their start and end apart: 15, of which 6 were waited for; matrix products, arithmetic and copies ran while one was open for 0% of the time, Pallas kernels for 4%

profile of v2, /device:TPU:1, one launch (start us, length us, event | category | flops | bytes accessed | tf_op | source)
XLA Modules:
  0.0 76.9 jit_solution(9140369660909114088)
XLA Ops:
  0.0 1.2 %fusion = (f32[8,8192]{1,0:T(8,128)S(1)}, f32[8,8192]{1,0:T(8,128)S(1)}) fusion(f32[8,16384]{1,0:T(8,128)} %own.1), kind=kLoop, calls=%fused_computation | loop fusion | bytes 1048576 | tf_op jit(solution)/shard_map/slice | solution.py:249
  1.2 2.5 %collective-permute-start = (f32[8,8192]{1,0:T(8,128)S(1)}, f32[8,8192]{1,0:T(8,128)S(1)}, u32[]{:S(2)}, u32[]{:S(2)}) collective-permute-start(f32[8,8192]{1,0:T(8,128)S(1)} %get-tuple-element.28), channel_id=1, source_target_pairs={{0,32},{32,64},{64,96},{96,128},{128,160},{160,192},{192,224},{224... | collective-permute-start | bytes 786440 | tf_op jit(solution)/shard_map/ppermute | solution.py:256
  3.7 4.0 %collective-permute-start.9 = (f32[8,8192]{1,0:T(8,128)S(1)}, f32[8,8192]{1,0:T(8,128)S(1)}, u32[]{:S(2)}, u32[]{:S(2)}) collective-permute-start(f32[8,8192]{1,0:T(8,128)S(1)} %get-tuple-element.27), channel_id=1, source_target_pairs={{0,224},{32,0},{64,32},{96,64},{128,96},{160,128},{192,160},{224,1... | collective-permute-start | bytes 786440 | tf_op jit(solution)/shard_map/ppermute | solution.py:257
  7.7 0.0 collective-permute-start.3
  7.7 2.7 %collective-permute-start.6 = (f32[8,8192]{1,0:T(8,128)S(1)}, f32[8,8192]{1,0:T(8,128)S(1)}, u32[]{:S(2)}, u32[]{:S(2)}) collective-permute-start(f32[8,8192]{1,0:T(8,128)S(1)} %get-tuple-element.28), channel_id=1, source_target_pairs={{0,224},{32,0},{64,32},{96,64},{128,96},{160,128},{192,160},{224,1... | collective-permute-start | bytes 786440 | tf_op jit(solution)/shard_map/ppermute | solution.py:257
  10.4 3.3 %collective-permute-done.refs_0_ = f32[8,8192]{1,0:T(8,128)S(1)} collective-permute-done((f32[8,8192]{1,0:T(8,128)S(1)}, f32[8,8192]{1,0:T(8,128)S(1)}, u32[]{:S(2)}, u32[]{:S(2)}) %collective-permute-start) | collective-permute-done | bytes 262176 | tf_op jit(solution)/shard_map/ppermute | solution.py:256
  13.7 0.0 collective-permute-start.1
  13.7 0.0 collective-permute-done.9.refs_3_
  13.7 2.7 %collective-permute-start.10 = (f32[8,8192]{1,0:T(8,128)S(1)}, f32[8,8192]{1,0:T(8,128)S(1)}, u32[]{:S(2)}, u32[]{:S(2)}) collective-permute-start(f32[8,8192]{1,0:T(8,128)S(1)} %collective-permute-done.9.refs_3_), channel_id=1, source_target_pairs={{0,224},{32,0},{64,32},{96,64},{128,96},{160,128},{192,160},{224,1... | collective-permute-start | bytes 786440 | tf_op jit(solution)/shard_map/ppermute | solution.py:257
  16.4 2.9 %collective-permute-done.3.refs_1_ = f32[8,8192]{1,0:T(8,128)S(1)} collective-permute-done((f32[8,8192]{1,0:T(8,128)S(1)}, f32[8,8192]{1,0:T(8,128)S(1)}, u32[]{:S(2)}, u32[]{:S(2)}) %collective-permute-start.3) | collective-permute-done | bytes 262176 | tf_op jit(solution)/shard_map/ppermute | solution.py:256
  19.3 0.0 collective-permute-start.4
  19.3 0.0 collective-permute-done.6.refs_2_
  19.3 2.7 %collective-permute-start.7 = (f32[8,8192]{1,0:T(8,128)S(1)}, f32[8,8192]{1,0:T(8,128)S(1)}, u32[]{:S(2)}, u32[]{:S(2)}) collective-permute-start(f32[8,8192]{1,0:T(8,128)S(1)} %collective-permute-done.6.refs_2_), channel_id=1, source_target_pairs={{0,224},{32,0},{64,32},{96,64},{128,96},{160,128},{192,160},{224,1... | collective-permute-start | bytes 786440 | tf_op jit(solution)/shard_map/ppermute | solution.py:257
  22.0 1.2 %copy-done.3 = f32[2,8,16384]{2,1,0:T(8,128)S(1)} copy-done((f32[2,8,16384]{2,1,0:T(8,128)S(1)}, f32[2,8,16384]{2,1,0:T(8,128)}, u32[]{:S(2)}) %copy-start.3) | copy-done | bytes 1048600
  23.2 1.0 %copy-done.4 = f32[8,16384]{1,0:T(8,128)S(1)} copy-done((f32[8,16384]{1,0:T(8,128)S(1)}, f32[8,16384]{1,0:T(8,128)}, u32[]{:S(2)}) %copy-start.4) | copy-done | bytes 524312
  24.2 0.7 copy-done.6
  25.0 0.7 copy-done.7
  25.7 0.7 copy-done.8
  26.4 2.0 %prep.1 = (f32[8,16384]{1,0:T(8,128)S(1)}, f32[8,16384]{1,0:T(8,128)S(1)}, f32[8,16384]{1,0:T(8,128)S(1)}) custom-call(s32[2,2048]{1,0:T(2,128)S(1)} %copy-done.6, f32[2,2048]{1,0:T(2,128)S(1)} %copy-done.7, s32[2,128]{1,0:T(2,128)S(1)} %copy-done.8, f32[8,16384]{1,0:T(8,128)S(1)} %copy-done.4, f32[2,8,16384]{2,1,0:T(8,128)S(1)} %copy-done.3), custom_call_target="tpu_custom_call" | custom-call | flops 1000000000 | bytes 4000000 | tf_op jit(solution)/shard_map/prep/pallas_call | solution.py:100
  28.4 0.0 collective-permute-done.1.refs_4_
  28.4 0.1 collective-permute-start.2
  28.5 0.0 collective-permute-done.10.refs_7_
  28.5 2.7 %collective-permute-start.11 = (f32[8,8192]{1,0:T(8,128)S(1)}, f32[8,8192]{1,0:T(8,128)S(1)}, u32[]{:S(2)}, u32[]{:S(2)}) collective-permute-start(f32[8,8192]{1,0:T(8,128)S(1)} %collective-permute-done.10.refs_7_), channel_id=1, source_target_pairs={{0,224},{32,0},{64,32},{96,64},{128,96},{160,128},{192,160},{224,1... | collective-permute-start | bytes 786440 | tf_op jit(solution)/shard_map/ppermute | solution.py:257
  31.1 0.0 collective-permute-done.4.refs_5_
  31.2 0.0 collective-permute-start.5
  31.2 0.0 collective-permute-done.7.refs_6_
  31.2 2.7 %collective-permute-start.8 = (f32[8,8192]{1,0:T(8,128)S(1)}, f32[8,8192]{1,0:T(8,128)S(1)}, u32[]{:S(2)}, u32[]{:S(2)}) collective-permute-start(f32[8,8192]{1,0:T(8,128)S(1)} %collective-permute-done.7.refs_6_), channel_id=1, source_target_pairs={{0,224},{32,0},{64,32},{96,64},{128,96},{160,128},{192,160},{224,1... | collective-permute-start | bytes 786440 | tf_op jit(solution)/shard_map/ppermute | solution.py:257
  33.8 1.1 %collective-permute-done.2.refs_0_ = f32[8,8192]{1,0:T(8,128)S(1)} collective-permute-done((f32[8,8192]{1,0:T(8,128)S(1)}, f32[8,8192]{1,0:T(8,128)S(1)}, u32[]{:S(2)}, u32[]{:S(2)}) %collective-permute-start.2) | collective-permute-done | bytes 262176 | tf_op jit(solution)/shard_map/ppermute | solution.py:256
  34.9 0.0 collective-permute-start.12
  34.9 0.0 collective-permute-done.11.refs_3_
  34.9 2.7 %collective-permute-start.13 = (f32[8,8192]{1,0:T(8,128)S(1)}, f32[8,8192]{1,0:T(8,128)S(1)}, u32[]{:S(2)}, u32[]{:S(2)}) collective-permute-start(f32[8,8192]{1,0:T(8,128)S(1)} %collective-permute-done.11.refs_3_), channel_id=1, source_target_pairs={{0,224},{32,0},{64,32},{96,64},{128,96},{160,128},{192,160},{224,1... | collective-permute-start | bytes 786440 | tf_op jit(solution)/shard_map/ppermute | solution.py:262
  37.6 0.0 copy-done.2
  37.6 0.0 copy-done.5
  37.6 1.3 %early.1 = (f32[56,40]{1,0:T(8,128)S(1)}, bf16[112,16384]{1,0:T(8,128)(2,1)S(1)}) custom-call(f32[8,16384]{1,0:T(8,128)S(1)} %copy-done.2, f32[8,8192]{1,0:T(8,128)S(1)} %collective-permute-done.refs_0_, f32[8,8192]{1,0:T(8,128)S(1)} %collective-permute-done.3.refs_1_, f32[8,8192]{1,0:T(8,128)S(1)} %collective-permute-done.6.refs_2_, ...), custom_call_target="tpu_custom_call" | custom-call | flops 1000000000 | bytes 4000000 | tf_op jit(solution)/shard_map/early/pallas_call | solution.py:100
  38.9 1.5 %collective-permute-done.5.refs_1_ = f32[8,8192]{1,0:T(8,128)S(1)} collective-permute-done((f32[8,8192]{1,0:T(8,128)S(1)}, f32[8,8192]{1,0:T(8,128)S(1)}, u32[]{:S(2)}, u32[]{:S(2)}) %collective-permute-start.5) | collective-permute-done | bytes 262176 | tf_op jit(solution)/shard_map/ppermute | solution.py:256
  40.4 0.0 collective-permute-done.8.refs_2_
  40.4 5.6 %collective-permute-done.12.refs_4_ = f32[8,8192]{1,0:T(8,128)S(1)} collective-permute-done((f32[8,8192]{1,0:T(8,128)S(1)}, f32[8,8192]{1,0:T(8,128)S(1)}, u32[]{:S(2)}, u32[]{:S(2)}) %collective-permute-start.12) | collective-permute-done | bytes 262176 | tf_op jit(solution)/shard_map/ppermute | solution.py:262
  46.0 0.0 collective-permute-done.13.refs_5_
  46.0 2.1 %last.1 = (f32[80,64]{1,0:T(8,128)S(1)}, bf16[48,16384]{1,0:T(8,128)(2,1)S(1)}) custom-call(f32[8,8192]{1,0:T(8,128)S(1)} %collective-permute-done.2.refs_0_, f32[8,8192]{1,0:T(8,128)S(1)} %collective-permute-done.5.refs_1_, f32[8,8192]{1,0:T(8,128)S(1)} %collective-permute-done.8.refs_2_, f32[8,8192]{1,0:T(8,128)S(1)} %collective-permute-done.11.refs_3_, ...), custom_call_target="tpu_custom_call" | custom-call | flops 1000000000 | bytes 4000000 | tf_op jit(solution)/shard_map/last/pallas_call | solution.py:100
  48.0 1.8 %copy-done = bf16[112,16384]{1,0:T(8,128)(2,1)} copy-done((bf16[112,16384]{1,0:T(8,128)(2,1)}, bf16[112,16384]{1,0:T(8,128)(2,1)S(1)}, u32[]{:S(2)}) %copy-start) | copy-done | bytes 3670040
  49.8 3.7 %collective-permute-start.14 = (f32[80,64]{1,0:T(8,128)S(1)}, f32[80,64]{1,0:T(8,128)S(1)}, u32[]{:S(2)}, u32[]{:S(2)}) collective-permute-start(f32[80,64]{1,0:T(8,128)S(1)} %get-tuple-element.23), channel_id=1, source_target_pairs={{0,1},{1,0},{2,3},{3,2},{4,5},{5,4},{6,7},{7,6},{8,9},{9,8},{10,11... | collective-permute-start | bytes 61448 | tf_op jit(solution)/shard_map/ppermute | solution.py:265
  53.5 0.9 %collective-permute-done.14 = f32[80,64]{1,0:T(8,128)S(1)} collective-permute-done((f32[80,64]{1,0:T(8,128)S(1)}, f32[80,64]{1,0:T(8,128)S(1)}, u32[]{:S(2)}, u32[]{:S(2)}) %collective-permute-start.14) | collective-permute-done | bytes 20512 | tf_op jit(solution)/shard_map/ppermute | solution.py:265
  54.4 0.1 copy.7
  54.4 0.1 broadcast_in_dim.2
  54.5 17.0 %all_to_all.5 = f32[16,80,64]{1,2,0:T(8,128)} all-to-all(f32[16,80,64]{1,2,0:T(8,128)S(1)} %broadcast_in_dim.2), channel_id=1, replica_groups=mesh['member'=8,'x'=4,'y'=4,'core'=2] {'x','y'}, dimensions={0} | all-to-all | bytes 655360 | tf_op jit(solution)/shard_map/all_to_all | solution.py:267
  71.5 1.3 %copy.8.refs_0_ = f32[16,80,64]{2,1,0:T(8,128)S(1)} copy(f32[16,80,64]{1,2,0:T(8,128)} %all_to_all.5) | data formatting | bytes 655360 | tf_op jit(solution)/shard_map/all_to_all | solution.py:267
  72.8 2.0 %copy-done.1 = bf16[112,16384]{1,0:T(8,128)(2,1)S(1)} copy-done((bf16[112,16384]{1,0:T(8,128)(2,1)S(1)}, bf16[112,16384]{1,0:T(8,128)(2,1)}, u32[]{:S(2)}) %copy-start.1) | copy-done | bytes 3670040
  74.9 2.1 %final.1 = f32[8,16384]{1,0:T(8,128)} custom-call(f32[16,80,64]{2,1,0:T(8,128)S(1)} %copy.8.refs_0_, bf16[112,16384]{1,0:T(8,128)(2,1)S(1)} %copy-done.1, bf16[48,16384]{1,0:T(8,128)(2,1)S(1)} %get-tuple-element.24.refs_2_, f32[8,16384]{1,0:T(8,128)S(1)} %get-tuple-element.25.refs_3_, f32[8,16384]{1,0:T(8,128)S(1)} %get-tuple-element.26.refs_4_), custom_call_target="tpu_custom_call" | custom-call | flops 1000000000 | bytes 4000000 | tf_op jit(solution)/shard_map/final/pallas_call | solution.py:100
  (10 shorter events, 0.0 us)
Async XLA Ops:
  0.0 37.6 %copy-start.2 = (f32[8,16384]{1,0:T(8,128)S(1)}, f32[8,16384]{1,0:T(8,128)}, u32[]{:S(2)}) copy-start(f32[8,16384]{1,0:T(8,128)} %own.1) | copy-start | bytes 1572868
  0.0 37.6 %copy-start.5 = (f32[8,16384]{1,0:T(8,128)S(1)}, f32[8,16384]{1,0:T(8,128)}, u32[]{:S(2)}) copy-start(f32[8,16384]{1,0:T(8,128)} %refs_8_) | copy-start | bytes 1572868
  1.2 12.5 %collective-permute-start = (f32[8,8192]{1,0:T(8,128)S(1)}, f32[8,8192]{1,0:T(8,128)S(1)}, u32[]{:S(2)}, u32[]{:S(2)}) collective-permute-start(f32[8,8192]{1,0:T(8,128)S(1)} %get-tuple-element.28), channel_id=1, source_target_pairs={{0,32},{32,64},{64,96},{96,128},{128,160},{160,192},{192,224},{224... | collective-permute-start | bytes 786440 | tf_op jit(solution)/shard_map/ppermute | solution.py:256
  3.7 10.0 %collective-permute-start.9 = (f32[8,8192]{1,0:T(8,128)S(1)}, f32[8,8192]{1,0:T(8,128)S(1)}, u32[]{:S(2)}, u32[]{:S(2)}) collective-permute-start(f32[8,8192]{1,0:T(8,128)S(1)} %get-tuple-element.27), channel_id=1, source_target_pairs={{0,224},{32,0},{64,32},{96,64},{128,96},{160,128},{192,160},{224,1... | collective-permute-start | bytes 786440 | tf_op jit(solution)/shard_map/ppermute | solution.py:257
  7.7 11.6 %collective-permute-start.3 = (f32[8,8192]{1,0:T(8,128)S(1)}, f32[8,8192]{1,0:T(8,128)S(1)}, u32[]{:S(2)}, u32[]{:S(2)}) collective-permute-start(f32[8,8192]{1,0:T(8,128)S(1)} %get-tuple-element.27), channel_id=1, source_target_pairs={{0,32},{32,64},{64,96},{96,128},{128,160},{160,192},{192,224},{224... | collective-permute-start | bytes 786440 | tf_op jit(solution)/shard_map/ppermute | solution.py:256
  7.7 11.6 %collective-permute-start.6 = (f32[8,8192]{1,0:T(8,128)S(1)}, f32[8,8192]{1,0:T(8,128)S(1)}, u32[]{:S(2)}, u32[]{:S(2)}) collective-permute-start(f32[8,8192]{1,0:T(8,128)S(1)} %get-tuple-element.28), channel_id=1, source_target_pairs={{0,224},{32,0},{64,32},{96,64},{128,96},{160,128},{192,160},{224,1... | collective-permute-start | bytes 786440 | tf_op jit(solution)/shard_map/ppermute | solution.py:257
  13.7 14.7 %collective-permute-start.1 = (f32[8,8192]{1,0:T(8,128)S(1)}, f32[8,8192]{1,0:T(8,128)S(1)}, u32[]{:S(2)}, u32[]{:S(2)}) collective-permute-start(f32[8,8192]{1,0:T(8,128)S(1)} %collective-permute-done.refs_0_), channel_id=1, source_target_pairs={{0,32},{32,64},{64,96},{96,128},{128,160},{160,192},{192,224},{224... | collective-permute-start | bytes 786440 | tf_op jit(solution)/shard_map/ppermute | solution.py:256
  13.7 14.8 %collective-permute-start.10 = (f32[8,8192]{1,0:T(8,128)S(1)}, f32[8,8192]{1,0:T(8,128)S(1)}, u32[]{:S(2)}, u32[]{:S(2)}) collective-permute-start(f32[8,8192]{1,0:T(8,128)S(1)} %collective-permute-done.9.refs_3_), channel_id=1, source_target_pairs={{0,224},{32,0},{64,32},{96,64},{128,96},{160,128},{192,160},{224,1... | collective-permute-start | bytes 786440 | tf_op jit(solution)/shard_map/ppermute | solution.py:257
  19.3 11.9 %collective-permute-start.4 = (f32[8,8192]{1,0:T(8,128)S(1)}, f32[8,8192]{1,0:T(8,128)S(1)}, u32[]{:S(2)}, u32[]{:S(2)}) collective-permute-start(f32[8,8192]{1,0:T(8,128)S(1)} %collective-permute-done.3.refs_1_), channel_id=1, source_target_pairs={{0,32},{32,64},{64,96},{96,128},{128,160},{160,192},{192,224},{224... | collective-permute-start | bytes 786440 | tf_op jit(solution)/shard_map/ppermute | solution.py:256
  19.3 11.9 %collective-permute-start.7 = (f32[8,8192]{1,0:T(8,128)S(1)}, f32[8,8192]{1,0:T(8,128)S(1)}, u32[]{:S(2)}, u32[]{:S(2)}) collective-permute-start(f32[8,8192]{1,0:T(8,128)S(1)} %collective-permute-done.6.refs_2_), channel_id=1, source_target_pairs={{0,224},{32,0},{64,32},{96,64},{128,96},{160,128},{192,160},{224,1... | collective-permute-start | bytes 786440 | tf_op jit(solution)/shard_map/ppermute | solution.py:257
  22.0 1.2 %copy-start.3 = (f32[2,8,16384]{2,1,0:T(8,128)S(1)}, f32[2,8,16384]{2,1,0:T(8,128)}, u32[]{:S(2)}) copy-start(f32[2,8,16384]{2,1,0:T(8,128)} %noise.1) | copy-start | bytes 3145732
  23.2 1.0 %copy-start.4 = (f32[8,16384]{1,0:T(8,128)S(1)}, f32[8,16384]{1,0:T(8,128)}, u32[]{:S(2)}) copy-start(f32[8,16384]{1,0:T(8,128)} %refs_8_) | copy-start | bytes 1572868
  24.2 0.7 copy-start.6
  25.0 0.7 copy-start.7
  25.7 0.7 copy-start.8
  28.4 6.5 %collective-permute-start.2 = (f32[8,8192]{1,0:T(8,128)S(1)}, f32[8,8192]{1,0:T(8,128)S(1)}, u32[]{:S(2)}, u32[]{:S(2)}) collective-permute-start(f32[8,8192]{1,0:T(8,128)S(1)} %collective-permute-done.1.refs_4_), channel_id=1, source_target_pairs={{0,32},{32,64},{64,96},{96,128},{128,160},{160,192},{192,224},{224... | collective-permute-start | bytes 786440 | tf_op jit(solution)/shard_map/ppermute | solution.py:256
  28.5 6.4 %collective-permute-start.11 = (f32[8,8192]{1,0:T(8,128)S(1)}, f32[8,8192]{1,0:T(8,128)S(1)}, u32[]{:S(2)}, u32[]{:S(2)}) collective-permute-start(f32[8,8192]{1,0:T(8,128)S(1)} %collective-permute-done.10.refs_7_), channel_id=1, source_target_pairs={{0,224},{32,0},{64,32},{96,64},{128,96},{160,128},{192,160},{224,1... | collective-permute-start | bytes 786440 | tf_op jit(solution)/shard_map/ppermute | solution.py:257
  31.2 9.2 %collective-permute-start.5 = (f32[8,8192]{1,0:T(8,128)S(1)}, f32[8,8192]{1,0:T(8,128)S(1)}, u32[]{:S(2)}, u32[]{:S(2)}) collective-permute-start(f32[8,8192]{1,0:T(8,128)S(1)} %collective-permute-done.4.refs_5_), channel_id=1, source_target_pairs={{0,32},{32,64},{64,96},{96,128},{128,160},{160,192},{192,224},{224... | collective-permute-start | bytes 786440 | tf_op jit(solution)/shard_map/ppermute | solution.py:256
  31.2 9.2 %collective-permute-start.8 = (f32[8,8192]{1,0:T(8,128)S(1)}, f32[8,8192]{1,0:T(8,128)S(1)}, u32[]{:S(2)}, u32[]{:S(2)}) collective-permute-start(f32[8,8192]{1,0:T(8,128)S(1)} %collective-permute-done.7.refs_6_), channel_id=1, source_target_pairs={{0,224},{32,0},{64,32},{96,64},{128,96},{160,128},{192,160},{224,1... | collective-permute-start | bytes 786440 | tf_op jit(solution)/shard_map/ppermute | solution.py:257
  34.9 11.1 %collective-permute-start.12 = (f32[8,8192]{1,0:T(8,128)S(1)}, f32[8,8192]{1,0:T(8,128)S(1)}, u32[]{:S(2)}, u32[]{:S(2)}) collective-permute-start(f32[8,8192]{1,0:T(8,128)S(1)} %collective-permute-done.2.refs_0_), channel_id=1, source_target_pairs={{0,32},{32,64},{64,96},{96,128},{128,160},{160,192},{192,224},{224... | collective-permute-start | bytes 786440 | tf_op jit(solution)/shard_map/ppermute | solution.py:262
  34.9 11.1 %collective-permute-start.13 = (f32[8,8192]{1,0:T(8,128)S(1)}, f32[8,8192]{1,0:T(8,128)S(1)}, u32[]{:S(2)}, u32[]{:S(2)}) collective-permute-start(f32[8,8192]{1,0:T(8,128)S(1)} %collective-permute-done.11.refs_3_), channel_id=1, source_target_pairs={{0,224},{32,0},{64,32},{96,64},{128,96},{160,128},{192,160},{224,1... | collective-permute-start | bytes 786440 | tf_op jit(solution)/shard_map/ppermute | solution.py:262
  48.0 1.8 %copy-start = (bf16[112,16384]{1,0:T(8,128)(2,1)}, bf16[112,16384]{1,0:T(8,128)(2,1)S(1)}, u32[]{:S(2)}) copy-start(bf16[112,16384]{1,0:T(8,128)(2,1)S(1)} %get-tuple-element.22.refs_7_.refs_1_) | copy-start | bytes 11010052
  49.8 4.5 %collective-permute-start.14 = (f32[80,64]{1,0:T(8,128)S(1)}, f32[80,64]{1,0:T(8,128)S(1)}, u32[]{:S(2)}, u32[]{:S(2)}) collective-permute-start(f32[80,64]{1,0:T(8,128)S(1)} %get-tuple-element.23), channel_id=1, source_target_pairs={{0,1},{1,0},{2,3},{3,2},{4,5},{5,4},{6,7},{7,6},{8,9},{9,8},{10,11... | collective-permute-start | bytes 61448 | tf_op jit(solution)/shard_map/ppermute | solution.py:265
  72.8 2.0 %copy-start.1 = (bf16[112,16384]{1,0:T(8,128)(2,1)S(1)}, bf16[112,16384]{1,0:T(8,128)(2,1)}, u32[]{:S(2)}) copy-start(bf16[112,16384]{1,0:T(8,128)(2,1)} %copy-done) | copy-start | bytes 11010052

commit v3 on v2

v3 whole, which is shorter than its diff:
```python
import math

import jax
import jax.numpy as jnp
from jax import lax
from jax.experimental import pallas as pl
from jax.experimental.pallas import tpu as pltpu
from jax.sharding import PartitionSpec as P

STEPS = 2
RINGS = 8
ROWS = 8
BF = jnp.bfloat16
F32 = jnp.float32
NT = (((1,), (1,)), ((), ()))
NN = (((1,), (0,)), ((), ()))


def constants(step):
    t = 0.6 - 0.1 * step
    alpha = 1.0 - 0.95 * t
    drift = -0.95 / alpha
    diffusion = 1.0 - 2.0 * drift * t
    return dict(
        t=t,
        alpha=alpha,
        gain=1.0 - 0.1 * drift - 0.1 * diffusion / t,
        pull=0.1 * diffusion * (1.0 - t),
        lift=0.1 * diffusion * alpha / t,
        kick=math.sqrt(0.1 * diffusion),
    )


def split3(x):
    a = x.astype(BF).astype(F32)
    r = x - a
    b = r.astype(BF).astype(F32)
    return a, b, r - b


def fields_kernel(cells, vals, mask, prec, targ):
    width = prec.shape[0]
    obs = cells.shape[1]
    rows = lax.broadcasted_iota(jnp.int32, (width, obs), 0)
    eye = lax.broadcasted_iota(jnp.int32, (width, width), 0) == lax.broadcasted_iota(
        jnp.int32, (width, width), 1
    )
    p_sum = jnp.zeros((width, width), F32)
    t_sum = jnp.zeros((width, width), F32)
    for s in range(cells.shape[0]):
        local = cells[s : s + 1, :] & (width * width - 1)
        high = jnp.where(rows == (local >> 7), 1.0, 0.0).astype(BF)
        low = rows == (local & 127)
        pieces = [jnp.ones((1, obs), F32), *split3(vals[s : s + 1, :])]
        sums = [
            lax.dot_general(
                high, jnp.where(low, piece, 0.0).astype(BF), NT, preferred_element_type=F32
            )
            for piece in pieces
        ]
        flags = mask[s : s + 1, :].astype(F32)
        flags = jnp.sum(jnp.where(eye, flags, 0.0), axis=1, keepdims=True)
        p_sum += flags * sums[0]
        t_sum += flags * (sums[1] + sums[2] + sums[3])
    prec[...] = p_sum
    targ[...] = t_sum


def fields(*args):
    shape = jax.ShapeDtypeStruct((128, 128), F32)
    return call(fields_kernel, (shape, shape), args, 10**9, name="fields")


def per_row(prec, targ, body):
    width = prec.shape[1]

    def step(h, carry):
        where = pl.ds(pl.multiple_of(h * width, width), width)
        body(where, prec[pl.ds(h, 1), :], targ[pl.ds(h, 1), :])
        return carry

    lax.fori_loop(0, prec.shape[0], step, 0, unroll=8)


def first_step(where, p, t, samples, noise):
    k = constants(0)
    return (
        (k["gain"] - k["pull"] * p) * samples[:, where]
        + k["pull"] * t
        + k["kick"] * noise[0, :, where]
    )


def base_kernel(samples, noise, prec, targ, base_ref, ab_ref):
    k0, k1 = constants(0), constants(1)

    def body(where, p, t):
        u = first_step(where, p, t, samples, noise)
        a1 = k1["gain"] - k1["pull"] * p
        base_ref[:, where] = a1 * u + k1["pull"] * t + k1["kick"] * noise[1, :, where]
        ab_ref[:, where] = jnp.broadcast_to(k0["lift"] * a1, u.shape)

    per_row(prec, targ, body)


def base_of(*args):
    shape = jax.ShapeDtypeStruct(args[0].shape, F32)
    return call(base_kernel, (shape, shape), args, 10**9, name="base")


CHUNK = 4096
LIMIT = pltpu.CompilerParams(vmem_limit_bytes=16 << 20)


def call(kernel, out_shape, args, flops, scratch=(), space=pltpu.VMEM, **kw):
    vmem = pl.BlockSpec(memory_space=pltpu.VMEM)
    return pl.pallas_call(
        kernel,
        out_shape=out_shape,
        in_specs=[pl.BlockSpec(memory_space=space)] * len(args),
        out_specs=jax.tree.map(lambda _: vmem, out_shape),
        scratch_shapes=scratch,
        compiler_params=LIMIT,
        cost_estimate=pl.CostEstimate(flops=flops, bytes_accessed=4 * 10**6, transcendentals=0),
        **kw,
    )(*args)


def split2(x):
    high = x.astype(BF).astype(F32)
    return jnp.concatenate([high, x - high], axis=0).astype(BF)


def column_chunks(blocks, body, acc):
    done = 0
    for pieces in zip(*blocks, strict=True):
        width = pieces[0].shape[1]
        for start in range(0, width, CHUNK):
            x = jnp.concatenate([p[:, start : start + CHUNK] for p in pieces], axis=0)
            acc = body(slice(done + start, done + start + CHUNK), x, acc)
        done += width
    return acc


def halves(full):
    half = full.shape[1] // 2
    return [full.at[:, :half], full.at[:, half:]]


def fold(z, m, n):
    z = z[:m] + z[m:]
    return z[:, :n] + z[:, n:]


def early_kernel(own, *refs):
    blocks, samples, noise, prec, targ, z, stack, u = refs[:-7], *refs[-7:]

    def first(where, p, t):
        u[:, where] = first_step(where, p, t, samples, noise)

    per_row(prec, targ, first)
    blocks = [blocks[i : i + 2] for i in range(0, len(blocks), 2)]
    blocks = [halves(own), *blocks, halves(samples), halves(u)]

    def body(where, x, acc):
        y = split2(x)
        stack[:, where] = y
        return acc + lax.dot_general(y, y, NT, preferred_element_type=F32)

    rows = ROWS * len(blocks)
    acc = column_chunks(blocks, body, jnp.zeros((2 * rows, 2 * rows), F32))
    z[...] = fold(acc, rows, rows)[:, : rows - 2 * ROWS]


def early(samples, noise, prec, targ, own, blocks):
    rows = ROWS * (3 + len(blocks) // 2)
    shapes = (
        jax.ShapeDtypeStruct((rows, rows - 2 * ROWS), F32),
        jax.ShapeDtypeStruct((2 * rows, own.shape[1]), BF),
    )
    args = (own, *blocks, samples, noise, prec, targ)
    return call(
        early_kernel, shapes, args, 10**9, [pltpu.VMEM(own.shape, F32)], name="early"
    )


def last_kernel(*refs):
    blocks, z1, stack, z, tail, full = refs[:-5], *refs[-5:]
    blocks = [blocks[i : i + 2] for i in range(0, len(blocks), 2)]
    new, old = ROWS * len(blocks), stack.shape[0] // 2

    def body(where, x, acc):
        y = split2(x)
        tail[:, where] = y
        return (
            acc[0] + lax.dot_general(y, stack[:, where], NT, preferred_element_type=F32),
            acc[1] + lax.dot_general(y, y, NT, preferred_element_type=F32),
        )

    acc = jnp.zeros((2 * new, 2 * old), F32), jnp.zeros((2 * new, 2 * new), F32)
    left, right = column_chunks(blocks, body, acc)
    left, right = fold(left, new, old), fold(right, new, new)
    m, n = z1.shape
    full[:m, :n] = z1[...]
    full[:m, n:] = left.T
    full[m:, :n] = left[:, :n]
    full[m:, n:] = right
    rows = z.shape[0]
    z[:, : n + new] = full[:rows, :]
    z[:, n + new :] = full[rows:, :]


def last(blocks, z1, stack):
    new = ROWS * (len(blocks) // 2)
    m, n = z1.shape
    shapes = (
        jax.ShapeDtypeStruct(((m + new) // 2, 2 * (n + new)), F32),
        jax.ShapeDtypeStruct((2 * new, stack.shape[1]), BF),
    )
    scratch = [pltpu.VMEM((m + new, n + new), F32)]
    return call(last_kernel, shapes, (*blocks, z1, stack), 10**9, scratch, name="last")


def softmax(x):
    e = jnp.exp(x - jnp.max(x, axis=1, keepdims=True))
    return e / jnp.sum(e, axis=1, keepdims=True)


def final_kernel(ncell, z_ref, stack, tail, base, ab, out):
    n = z_ref.shape[2] // 2
    old, new = stack.shape[0] // 2, tail.shape[0] // 2
    first = old - 2 * ROWS
    k0, k1 = constants(0), constants(1)
    z = z_ref[0]
    for i in range(1, z_ref.shape[0]):
        z = z + z_ref[i]
    z = jnp.concatenate([z[:, :n], z[:, n:]], axis=0)
    pp = jnp.concatenate([z[:first], z[old:]], axis=0)
    eye = lax.broadcasted_iota(jnp.int32, (n, n), 0) == lax.broadcasted_iota(jnp.int32, (n, n), 1)
    norm = jnp.sum(jnp.where(eye, pp, 0.0), axis=0, keepdims=True)

    def weights(k, cross):
        dist = k["alpha"] * k["alpha"] * norm - 2.0 * k["alpha"] * cross
        return softmax(-dist / (2.0 * k["t"] * math.sqrt(ncell)))

    w0 = weights(k0, z[first : first + ROWS])
    cross = z[first + ROWS : old] + k0["lift"] * lax.dot_general(
        w0, pp, NN, precision=lax.Precision.HIGHEST, preferred_element_type=F32
    )
    w1 = k1["lift"] * weights(k1, cross)
    w = jnp.concatenate([w0, w1], axis=0)
    wh = w.astype(BF).astype(F32)
    w = jnp.concatenate([wh, w - wh], axis=0)
    none = jnp.zeros((4 * ROWS, 2 * ROWS), F32)
    left = jnp.concatenate([w[:, :first], none, w[:, :first], none], axis=1).astype(BF)
    right = jnp.concatenate([w[:, first:], w[:, first:]], axis=1).astype(BF)
    width = out.shape[1] // 2
    for start in range(0, out.shape[1], width):
        to = slice(start, start + width)
        m = lax.dot_general(left, stack[:, to], NN, preferred_element_type=F32)
        m += lax.dot_general(right, tail[:, to], NN, preferred_element_type=F32)
        m = m[: 2 * ROWS] + m[2 * ROWS :]
        out[:, to] = base[:, to] + ab[:, to] * m[:ROWS] + m[ROWS:]


def final(ncell, z, stack, tail, base, ab):
    def final(*refs):
        return final_kernel(ncell, *refs)

    shape = jax.ShapeDtypeStruct(base.shape, F32)
    return call(final, shape, (z, stack, tail, base, ab), 10**9, name="final")


def total(x):
    x = x + lax.ppermute(x, "core", [(0, 1), (1, 0)])
    x = jnp.broadcast_to(x[None], (lax.axis_size("x") * lax.axis_size("y"), *x.shape))
    return lax.all_to_all(x, ("x", "y"), split_axis=0, concat_axis=0, tiled=True)


def per_device(prior, samples, noise, obs_cells, obs_values, seismic_mask):
    cells = prior.shape[1]
    half = cells // 2
    ncell = cells * lax.axis_size("x") * lax.axis_size("y") * lax.axis_size("core")
    up = [(i, (i + 1) % RINGS) for i in range(RINGS)]
    down = [(i, (i - 1) % RINGS) for i in range(RINGS)]
    rising = [prior[:, :half], prior[:, half:]]
    falling = list(rising)
    blocks = []
    prec, targ = fields(obs_cells, obs_values, seismic_mask)
    base, ab = base_of(samples, noise, prec, targ)
    for hop in range(3):
        if hop == 1:
            rising[0], prec, targ = lax.optimization_barrier((rising[0], prec, targ))
        if hop == 2:
            rising[0], base, ab = lax.optimization_barrier((rising[0], base, ab))
        for c in range(2):
            rising[c] = lax.ppermute(rising[c], "member", up)
            falling[c] = lax.ppermute(falling[c], "member", down)
        blocks += [*rising, *falling]
    z1, stack = early(samples, noise, prec, targ, prior, blocks)
    far = [lax.ppermute(rising[0], "member", up), lax.ppermute(falling[1], "member", down)]
    z, tail = last(far, z1, stack)
    z = total(z)
    return final(ncell, z, stack, tail, base, ab)


def solution(mesh):
    mesh = jax.sharding.Mesh(mesh.devices.reshape(RINGS, 4, 4, 2), ("member", "x", "y", "core"))
    cell = ("x", "y", "core")
    in_specs = (
        P("member", cell),
        P("member", cell),
        P(None, "member", cell),
        P(None, cell),
        P(None, cell),
        P(None, cell),
    )
    return jax.shard_map(
        per_device, mesh=mesh, in_specs=in_specs, out_specs=P("member", cell), check_vma=False
    )
```

time: 78 us -> 69.5 us (0.89)
  local copies, waits for them, and re-layouts: 10.8 us -> 3.36 us
  waiting for transfers between devices: 15.3 us -> 18.3 us
  blocking collectives: 17 us -> 14.5 us
  starting transfers between devices: 26.4 us -> 24 us
  Pallas kernels: 7.44 us -> 8.32 us
    unnamed x18 -> x12, local copies, waits for them, and re-layouts: 8.21 us -> 2.12 us
    ppermute x6, waiting for transfers between devices: 8.75 us -> 13.8 us  [per_device(): rising[c] = lax.ppermute(rising[c], 'member', up)]
    all_to_all x1, blocking collectives: 17 us -> 14.5 us  [total(): lax.all_to_all(x, ('x', 'y'), split_axis=0, concat_axis=0, tiled=True)]
    ppermute x1, starting transfers between devices: 3.66 us -> 1.28 us  [total(): x = x + lax.ppermute(x, 'core', [(0, 1), (1, 0)])]
    ppermute x1, waiting for transfers between devices: 5.61 us -> 3.67 us  [per_device(): lax.ppermute(rising[0], 'member', up)]
    all_to_all x1 -> x0, local copies, waits for them, and re-layouts: 1.28 us -> none  [per_device(): z = lax.all_to_all(z, ('x', 'y'), split_axis=0, concat_axis=0, tiled=True)]
    pallas_call x4 -> x5, Pallas kernels: 7.44 us -> 8.32 us  [call(): pl.pallas_call(kernel, out_shape=out_shape, in_specs=[pl.BlockSpec(memory...]
  transfers between devices with their start and end apart: 15 -> 15, of which waited for: 6 -> 7; matrix products, arithmetic and copies ran while one was open for 0% -> 0% of each run, Pallas kernels for 4% -> 6%
where the time goes in v3:
time: 69.5 us; the launch traced here: 68.6 us
  starting transfers between devices  24 us (35%)
  waiting for transfers between devices  18.3 us (26%)
  blocking collectives  14.5 us (21%)
  Pallas kernels  8.32 us (12%)
  local copies, waits for them, and re-layouts  3.36 us (5%)
    ppermute x6, starting transfers between devices, per_device(): falling[c] = lax.ppermute(falling[c], 'member', down)  17.4 us
    all_to_all x1, blocking collectives, total(): lax.all_to_all(x, ('x', 'y'), split_axis=0, concat_axis=0, tiled=True)  14.5 us
    ppermute x6, waiting for transfers between devices, per_device(): rising[c] = lax.ppermute(rising[c], 'member', up)  13.8 us
    pallas_call x5, Pallas kernels, call(): pl.pallas_call(kernel, out_shape=out_shape, in_specs=[pl.BlockSpec(memory...  8.32 us
    ppermute x1, waiting for transfers between devices, per_device(): lax.ppermute(rising[0], 'member', up)  3.67 us
    ppermute x1, starting transfers between devices, per_device(): lax.ppermute(falling[1], 'member', down)  2.67 us
    ppermute x6, starting transfers between devices, per_device(): rising[c] = lax.ppermute(rising[c], 'member', up)  2.64 us
    unnamed x12, local copies, waits for them, and re-layouts  2.12 us
  transfers between devices with their start and end apart: 15, of which 7 were waited for; matrix products, arithmetic and copies ran while one was open for 0% of the time, Pallas kernels for 6%

profile of v3, /device:TPU:1, one launch (start us, length us, event | category | flops | bytes accessed | tf_op | source)
XLA Modules:
  0.0 68.6 jit_solution(15302525907009996126)
XLA Ops:
  0.0 0.0 copy-start
  0.0 0.0 copy-start.2
  0.0 0.0 copy-start.1
  0.0 1.2 %fusion = (f32[8,8192]{1,0:T(8,128)S(1)}, f32[8,8192]{1,0:T(8,128)S(1)}) fusion(f32[8,16384]{1,0:T(8,128)} %own.1), kind=kLoop, calls=%fused_computation | loop fusion | bytes 1048576 | tf_op jit(solution)/shard_map/slice | solution.py:286
  1.2 2.5 %collective-permute-start = (f32[8,8192]{1,0:T(8,128)S(1)}, f32[8,8192]{1,0:T(8,128)S(1)}, u32[]{:S(2)}, u32[]{:S(2)}) collective-permute-start(f32[8,8192]{1,0:T(8,128)S(1)} %get-tuple-element.34), channel_id=1, source_target_pairs={{0,32},{32,64},{64,96},{96,128},{128,160},{160,192},{192,224},{224... | collective-permute-start | bytes 786440 | tf_op jit(solution)/shard_map/ppermute | solution.py:297
  3.8 4.0 %collective-permute-start.4 = (f32[8,8192]{1,0:T(8,128)S(1)}, f32[8,8192]{1,0:T(8,128)S(1)}, u32[]{:S(2)}, u32[]{:S(2)}) collective-permute-start(f32[8,8192]{1,0:T(8,128)S(1)} %get-tuple-element.33), channel_id=1, source_target_pairs={{0,224},{32,0},{64,32},{96,64},{128,96},{160,128},{192,160},{224,1... | collective-permute-start | bytes 786440 | tf_op jit(solution)/shard_map/ppermute | solution.py:298
  7.8 0.0 collective-permute-start.8
  7.8 2.7 %collective-permute-start.9 = (f32[8,8192]{1,0:T(8,128)S(1)}, f32[8,8192]{1,0:T(8,128)S(1)}, u32[]{:S(2)}, u32[]{:S(2)}) collective-permute-start(f32[8,8192]{1,0:T(8,128)S(1)} %get-tuple-element.34), channel_id=1, source_target_pairs={{0,224},{32,0},{64,32},{96,64},{128,96},{160,128},{192,160},{224,1... | collective-permute-start | bytes 786440 | tf_op jit(solution)/shard_map/ppermute | solution.py:298
  10.5 0.0 copy-start.3
  10.5 0.7 %copy-done.3 = s32[2,2048]{1,0:T(2,128)S(1)} copy-done((s32[2,2048]{1,0:T(2,128)S(1)}, s32[2,2048]{1,0:T(2,128)}, u32[]{:S(2)}) %copy-start.3) | copy-done | bytes 16408
  11.2 0.0 copy-start.4
  11.2 0.7 %copy-done.4 = f32[2,2048]{1,0:T(2,128)S(1)} copy-done((f32[2,2048]{1,0:T(2,128)S(1)}, f32[2,2048]{1,0:T(2,128)}, u32[]{:S(2)}) %copy-start.4) | copy-done | bytes 16408
  11.9 0.7 copy-done.5
  12.6 1.4 %fields.1 = (f32[128,128]{1,0:T(8,128)S(1)}, f32[128,128]{1,0:T(8,128)S(1)}) custom-call(s32[2,2048]{1,0:T(2,128)S(1)} %copy-done.3, f32[2,2048]{1,0:T(2,128)S(1)} %copy-done.4, s32[2,128]{1,0:T(2,128)S(1)} %copy-done.5), custom_call_target="tpu_custom_call" | custom-call | flops 1000000000 | bytes 4000000 | tf_op jit(solution)/shard_map/fields/pallas_call | solution.py:117
  14.0 0.0 collective-permute-done.refs_0_
  14.0 0.1 collective-permute-start.1
  14.1 0.0 collective-permute-done.4.refs_3_
  14.1 2.7 %collective-permute-start.5 = (f32[8,8192]{1,0:T(8,128)S(1)}, f32[8,8192]{1,0:T(8,128)S(1)}, u32[]{:S(2)}, u32[]{:S(2)}) collective-permute-start(f32[8,8192]{1,0:T(8,128)S(1)} %collective-permute-done.4.refs_3_), channel_id=1, source_target_pairs={{0,224},{32,0},{64,32},{96,64},{128,96},{160,128},{192,160},{224,1... | collective-permute-start | bytes 786440 | tf_op jit(solution)/shard_map/ppermute | solution.py:298
  16.8 2.6 %collective-permute-done.8.refs_1_ = f32[8,8192]{1,0:T(8,128)S(1)} collective-permute-done((f32[8,8192]{1,0:T(8,128)S(1)}, f32[8,8192]{1,0:T(8,128)S(1)}, u32[]{:S(2)}, u32[]{:S(2)}) %collective-permute-start.8) | collective-permute-done | bytes 262176 | tf_op jit(solution)/shard_map/ppermute | solution.py:297
  19.4 0.0 collective-permute-start.10
  19.4 0.0 collective-permute-done.9.refs_2_
  19.4 2.7 %collective-permute-start.11 = (f32[8,8192]{1,0:T(8,128)S(1)}, f32[8,8192]{1,0:T(8,128)S(1)}, u32[]{:S(2)}, u32[]{:S(2)}) collective-permute-start(f32[8,8192]{1,0:T(8,128)S(1)} %collective-permute-done.9.refs_2_), channel_id=1, source_target_pairs={{0,224},{32,0},{64,32},{96,64},{128,96},{160,128},{192,160},{224,1... | collective-permute-start | bytes 786440 | tf_op jit(solution)/shard_map/ppermute | solution.py:298
  22.0 0.0 copy-done.2
  22.0 0.0 copy-done.1
  22.0 0.5 base.1
  22.6 2.4 %collective-permute-done.1.refs_4_ = f32[8,8192]{1,0:T(8,128)S(1)} collective-permute-done((f32[8,8192]{1,0:T(8,128)S(1)}, f32[8,8192]{1,0:T(8,128)S(1)}, u32[]{:S(2)}, u32[]{:S(2)}) %collective-permute-start.1) | collective-permute-done | bytes 262176 | tf_op jit(solution)/shard_map/ppermute | solution.py:297
  25.0 0.0 collective-permute-start.2
  25.0 0.0 collective-permute-done.5.refs_7_
  25.0 2.7 %collective-permute-start.6 = (f32[8,8192]{1,0:T(8,128)S(1)}, f32[8,8192]{1,0:T(8,128)S(1)}, u32[]{:S(2)}, u32[]{:S(2)}) collective-permute-start(f32[8,8192]{1,0:T(8,128)S(1)} %collective-permute-done.5.refs_7_), channel_id=1, source_target_pairs={{0,224},{32,0},{64,32},{96,64},{128,96},{160,128},{192,160},{224,1... | collective-permute-start | bytes 786440 | tf_op jit(solution)/shard_map/ppermute | solution.py:298
  27.7 2.9 %collective-permute-done.10.refs_5_ = f32[8,8192]{1,0:T(8,128)S(1)} collective-permute-done((f32[8,8192]{1,0:T(8,128)S(1)}, f32[8,8192]{1,0:T(8,128)S(1)}, u32[]{:S(2)}, u32[]{:S(2)}) %collective-permute-start.10) | collective-permute-done | bytes 262176 | tf_op jit(solution)/shard_map/ppermute | solution.py:297
  30.6 0.0 collective-permute-start.12
  30.6 0.0 collective-permute-done.11.refs_6_
  30.6 2.7 %collective-permute-start.13 = (f32[8,8192]{1,0:T(8,128)S(1)}, f32[8,8192]{1,0:T(8,128)S(1)}, u32[]{:S(2)}, u32[]{:S(2)}) collective-permute-start(f32[8,8192]{1,0:T(8,128)S(1)} %collective-permute-done.11.refs_6_), channel_id=1, source_target_pairs={{0,224},{32,0},{64,32},{96,64},{128,96},{160,128},{192,160},{224,1... | collective-permute-start | bytes 786440 | tf_op jit(solution)/shard_map/ppermute | solution.py:298
  33.3 2.9 %collective-permute-done.2.refs_8_ = f32[8,8192]{1,0:T(8,128)S(1)} collective-permute-done((f32[8,8192]{1,0:T(8,128)S(1)}, f32[8,8192]{1,0:T(8,128)S(1)}, u32[]{:S(2)}, u32[]{:S(2)}) %collective-permute-start.2) | collective-permute-done | bytes 262176 | tf_op jit(solution)/shard_map/ppermute | solution.py:297
  36.2 0.0 collective-permute-start.3
  36.2 0.0 collective-permute-done.6.refs_11_
  36.2 2.7 %collective-permute-start.7 = (f32[8,8192]{1,0:T(8,128)S(1)}, f32[8,8192]{1,0:T(8,128)S(1)}, u32[]{:S(2)}, u32[]{:S(2)}) collective-permute-start(f32[8,8192]{1,0:T(8,128)S(1)} %collective-permute-done.6.refs_11_), channel_id=1, source_target_pairs={{0,224},{32,0},{64,32},{96,64},{128,96},{160,128},{192,160},{224,1... | collective-permute-start | bytes 786440 | tf_op jit(solution)/shard_map/ppermute | solution.py:301
  38.9 2.9 %collective-permute-done.12.refs_9_ = f32[8,8192]{1,0:T(8,128)S(1)} collective-permute-done((f32[8,8192]{1,0:T(8,128)S(1)}, f32[8,8192]{1,0:T(8,128)S(1)}, u32[]{:S(2)}, u32[]{:S(2)}) %collective-permute-start.12) | collective-permute-done | bytes 262176 | tf_op jit(solution)/shard_map/ppermute | solution.py:297
  41.8 0.0 collective-permute-done.13.refs_10_
  41.8 0.0 copy-done
  41.8 1.9 %early.1 = (f32[72,56]{1,0:T(8,128)S(1)}, bf16[144,16384]{1,0:T(8,128)(2,1)S(1)}) custom-call(f32[8,16384]{1,0:T(8,128)S(1)} %copy-done, f32[8,8192]{1,0:T(8,128)S(1)} %collective-permute-done.refs_0_, f32[8,8192]{1,0:T(8,128)S(1)} %collective-permute-done.8.refs_1_, f32[8,8192]{1,0:T(8,128)S(1)} %collective-permute-done.9.refs_2_, ...), custom_call_target="tpu_custom_call" | custom-call | flops 1000000000 | bytes 4000000 | tf_op jit(solution)/shard_map/early/pallas_call | solution.py:117
  43.8 3.7 %collective-permute-done.3.refs_0_ = f32[8,8192]{1,0:T(8,128)S(1)} collective-permute-done((f32[8,8192]{1,0:T(8,128)S(1)}, f32[8,8192]{1,0:T(8,128)S(1)}, u32[]{:S(2)}, u32[]{:S(2)}) %collective-permute-start.3) | collective-permute-done | bytes 262176 | tf_op jit(solution)/shard_map/ppermute | solution.py:301
  47.4 0.0 collective-permute-done.7.refs_1_
  47.5 1.9 %last.1 = (f32[40,128]{1,0:T(8,128)S(1)}, bf16[16,16384]{1,0:T(8,128)(2,1)S(1)}) custom-call(f32[8,8192]{1,0:T(8,128)S(1)} %collective-permute-done.3.refs_0_, f32[8,8192]{1,0:T(8,128)S(1)} %collective-permute-done.7.refs_1_, f32[72,56]{1,0:T(8,128)S(1)} %get-tuple-element.27.refs_2_, bf16[144,16384]{1,0:T(8,128)(2,1)S(1)} %get-tuple-element.28.refs_3_.refs_1_), custom_call_target="tpu_custom_call" | custom-call | flops 1000000000 | bytes 4000000 | tf_op jit(solution)/shard_map/last/pallas_call | solution.py:117
  49.3 1.3 %collective-permute-start.14 = (f32[40,128]{1,0:T(8,128)S(1)}, f32[40,128]{1,0:T(8,128)S(1)}, u32[]{:S(2)}, u32[]{:S(2)}) collective-permute-start(f32[40,128]{1,0:T(8,128)S(1)} %get-tuple-element.29), channel_id=1, source_target_pairs={{0,1},{1,0},{2,3},{3,2},{4,5},{5,4},{6,7},{7,6},{8,9},{9,8},{10,11... | collective-permute-start | bytes 61448 | tf_op jit(solution)/shard_map/ppermute | solution.py:275
  50.6 0.8 %collective-permute-done.14 = f32[40,128]{1,0:T(8,128)S(1)} collective-permute-done((f32[40,128]{1,0:T(8,128)S(1)}, f32[40,128]{1,0:T(8,128)S(1)}, u32[]{:S(2)}, u32[]{:S(2)}) %collective-permute-start.14) | collective-permute-done | bytes 20512 | tf_op jit(solution)/shard_map/ppermute | solution.py:275
  51.5 14.5 %all_to_all.5.refs_0_ = f32[16,40,128]{2,1,0:T(8,128)S(1)} all-to-all(f32[16,40,128]{2,1,0:T(8,128)S(1)} %broadcast_in_dim.2), channel_id=1, replica_groups=mesh['member'=8,'x'=4,'y'=4,'core'=2] {'x','y'}, dimensions={0} | all-to-all | bytes 655360 | tf_op jit(solution)/shard_map/all_to_all | solution.py:277
  66.0 2.6 %final.1 = f32[8,16384]{1,0:T(8,128)} custom-call(f32[16,40,128]{2,1,0:T(8,128)S(1)} %all_to_all.5.refs_0_, bf16[144,16384]{1,0:T(8,128)(2,1)S(1)} %get-tuple-element.28.refs_3_.refs_1_, bf16[16,16384]{1,0:T(8,128)(2,1)S(1)} %get-tuple-element.30.refs_2_, f32[8,16384]{1,0:T(8,128)S(1)} %get-tuple-element.31.refs_3_, f32[8,16384]{1,0:T(8,128)S(1)} %get-tuple-element.32.refs_4_), custom_call_target="tpu_custom_call" | custom-call | flops 1000000000 | bytes 4000000 | tf_op jit(solution)/shard_map/final/pallas_call | solution.py:117
  (3 shorter events, 0.0 us)
Async XLA Ops:
  0.0 41.8 %copy-start = (f32[8,16384]{1,0:T(8,128)S(1)}, f32[8,16384]{1,0:T(8,128)}, u32[]{:S(2)}) copy-start(f32[8,16384]{1,0:T(8,128)} %own.1) | copy-start | bytes 1572868
  0.0 22.0 %copy-start.2 = (f32[8,16384]{1,0:T(8,128)S(1)}, f32[8,16384]{1,0:T(8,128)}, u32[]{:S(2)}) copy-start(f32[8,16384]{1,0:T(8,128)} %refs_12_.1) | copy-start | bytes 1572868
  0.0 22.0 %copy-start.1 = (f32[2,8,16384]{2,1,0:T(8,128)S(1)}, f32[2,8,16384]{2,1,0:T(8,128)}, u32[]{:S(2)}) copy-start(f32[2,8,16384]{2,1,0:T(8,128)} %refs_13_.1) | copy-start | bytes 3145732
  1.2 12.8 %collective-permute-start = (f32[8,8192]{1,0:T(8,128)S(1)}, f32[8,8192]{1,0:T(8,128)S(1)}, u32[]{:S(2)}, u32[]{:S(2)}) collective-permute-start(f32[8,8192]{1,0:T(8,128)S(1)} %get-tuple-element.34), channel_id=1, source_target_pairs={{0,32},{32,64},{64,96},{96,128},{128,160},{160,192},{192,224},{224... | collective-permute-start | bytes 786440 | tf_op jit(solution)/shard_map/ppermute | solution.py:297
  3.8 10.3 %collective-permute-start.4 = (f32[8,8192]{1,0:T(8,128)S(1)}, f32[8,8192]{1,0:T(8,128)S(1)}, u32[]{:S(2)}, u32[]{:S(2)}) collective-permute-start(f32[8,8192]{1,0:T(8,128)S(1)} %get-tuple-element.33), channel_id=1, source_target_pairs={{0,224},{32,0},{64,32},{96,64},{128,96},{160,128},{192,160},{224,1... | collective-permute-start | bytes 786440 | tf_op jit(solution)/shard_map/ppermute | solution.py:298
  7.8 11.6 %collective-permute-start.8 = (f32[8,8192]{1,0:T(8,128)S(1)}, f32[8,8192]{1,0:T(8,128)S(1)}, u32[]{:S(2)}, u32[]{:S(2)}) collective-permute-start(f32[8,8192]{1,0:T(8,128)S(1)} %get-tuple-element.33), channel_id=1, source_target_pairs={{0,32},{32,64},{64,96},{96,128},{128,160},{160,192},{192,224},{224... | collective-permute-start | bytes 786440 | tf_op jit(solution)/shard_map/ppermute | solution.py:297
  7.8 11.6 %collective-permute-start.9 = (f32[8,8192]{1,0:T(8,128)S(1)}, f32[8,8192]{1,0:T(8,128)S(1)}, u32[]{:S(2)}, u32[]{:S(2)}) collective-permute-start(f32[8,8192]{1,0:T(8,128)S(1)} %get-tuple-element.34), channel_id=1, source_target_pairs={{0,224},{32,0},{64,32},{96,64},{128,96},{160,128},{192,160},{224,1... | collective-permute-start | bytes 786440 | tf_op jit(solution)/shard_map/ppermute | solution.py:298
  10.5 0.7 %copy-start.3 = (s32[2,2048]{1,0:T(2,128)S(1)}, s32[2,2048]{1,0:T(2,128)}, u32[]{:S(2)}) copy-start(s32[2,2048]{1,0:T(2,128)} %cells.1) | copy-start | bytes 49156
  11.2 0.7 %copy-start.4 = (f32[2,2048]{1,0:T(2,128)S(1)}, f32[2,2048]{1,0:T(2,128)}, u32[]{:S(2)}) copy-start(f32[2,2048]{1,0:T(2,128)} %vals.1) | copy-start | bytes 49156
  11.9 0.7 copy-start.5
  14.0 11.0 %collective-permute-start.1 = (f32[8,8192]{1,0:T(8,128)S(1)}, f32[8,8192]{1,0:T(8,128)S(1)}, u32[]{:S(2)}, u32[]{:S(2)}) collective-permute-start(f32[8,8192]{1,0:T(8,128)S(1)} %collective-permute-done.refs_0_), channel_id=1, source_target_pairs={{0,32},{32,64},{64,96},{96,128},{128,160},{160,192},{192,224},{224... | collective-permute-start | bytes 786440 | tf_op jit(solution)/shard_map/ppermute | solution.py:297
  14.1 10.9 %collective-permute-start.5 = (f32[8,8192]{1,0:T(8,128)S(1)}, f32[8,8192]{1,0:T(8,128)S(1)}, u32[]{:S(2)}, u32[]{:S(2)}) collective-permute-start(f32[8,8192]{1,0:T(8,128)S(1)} %collective-permute-done.4.refs_3_), channel_id=1, source_target_pairs={{0,224},{32,0},{64,32},{96,64},{128,96},{160,128},{192,160},{224,1... | collective-permute-start | bytes 786440 | tf_op jit(solution)/shard_map/ppermute | solution.py:298
  19.4 11.2 %collective-permute-start.10 = (f32[8,8192]{1,0:T(8,128)S(1)}, f32[8,8192]{1,0:T(8,128)S(1)}, u32[]{:S(2)}, u32[]{:S(2)}) collective-permute-start(f32[8,8192]{1,0:T(8,128)S(1)} %collective-permute-done.8.refs_1_), channel_id=1, source_target_pairs={{0,32},{32,64},{64,96},{96,128},{128,160},{160,192},{192,224},{224... | collective-permute-start | bytes 786440 | tf_op jit(solution)/shard_map/ppermute | solution.py:297
  19.4 11.2 %collective-permute-start.11 = (f32[8,8192]{1,0:T(8,128)S(1)}, f32[8,8192]{1,0:T(8,128)S(1)}, u32[]{:S(2)}, u32[]{:S(2)}) collective-permute-start(f32[8,8192]{1,0:T(8,128)S(1)} %collective-permute-done.9.refs_2_), channel_id=1, source_target_pairs={{0,224},{32,0},{64,32},{96,64},{128,96},{160,128},{192,160},{224,1... | collective-permute-start | bytes 786440 | tf_op jit(solution)/shard_map/ppermute | solution.py:298
  25.0 11.2 %collective-permute-start.2 = (f32[8,8192]{1,0:T(8,128)S(1)}, f32[8,8192]{1,0:T(8,128)S(1)}, u32[]{:S(2)}, u32[]{:S(2)}) collective-permute-start(f32[8,8192]{1,0:T(8,128)S(1)} %collective-permute-done.1.refs_4_), channel_id=1, source_target_pairs={{0,32},{32,64},{64,96},{96,128},{128,160},{160,192},{192,224},{224... | collective-permute-start | bytes 786440 | tf_op jit(solution)/shard_map/ppermute | solution.py:297
  25.0 11.2 %collective-permute-start.6 = (f32[8,8192]{1,0:T(8,128)S(1)}, f32[8,8192]{1,0:T(8,128)S(1)}, u32[]{:S(2)}, u32[]{:S(2)}) collective-permute-start(f32[8,8192]{1,0:T(8,128)S(1)} %collective-permute-done.5.refs_7_), channel_id=1, source_target_pairs={{0,224},{32,0},{64,32},{96,64},{128,96},{160,128},{192,160},{224,1... | collective-permute-start | bytes 786440 | tf_op jit(solution)/shard_map/ppermute | solution.py:298
  30.6 11.2 %collective-permute-start.12 = (f32[8,8192]{1,0:T(8,128)S(1)}, f32[8,8192]{1,0:T(8,128)S(1)}, u32[]{:S(2)}, u32[]{:S(2)}) collective-permute-start(f32[8,8192]{1,0:T(8,128)S(1)} %collective-permute-done.10.refs_5_), channel_id=1, source_target_pairs={{0,32},{32,64},{64,96},{96,128},{128,160},{160,192},{192,224},{224... | collective-permute-start | bytes 786440 | tf_op jit(solution)/shard_map/ppermute | solution.py:297
  30.6 11.2 %collective-permute-start.13 = (f32[8,8192]{1,0:T(8,128)S(1)}, f32[8,8192]{1,0:T(8,128)S(1)}, u32[]{:S(2)}, u32[]{:S(2)}) collective-permute-start(f32[8,8192]{1,0:T(8,128)S(1)} %collective-permute-done.11.refs_6_), channel_id=1, source_target_pairs={{0,224},{32,0},{64,32},{96,64},{128,96},{160,128},{192,160},{224,1... | collective-permute-start | bytes 786440 | tf_op jit(solution)/shard_map/ppermute | solution.py:298
  36.2 11.2 %collective-permute-start.3 = (f32[8,8192]{1,0:T(8,128)S(1)}, f32[8,8192]{1,0:T(8,128)S(1)}, u32[]{:S(2)}, u32[]{:S(2)}) collective-permute-start(f32[8,8192]{1,0:T(8,128)S(1)} %collective-permute-done.2.refs_8_), channel_id=1, source_target_pairs={{0,32},{32,64},{64,96},{96,128},{128,160},{160,192},{192,224},{224... | collective-permute-start | bytes 786440 | tf_op jit(solution)/shard_map/ppermute | solution.py:301
  36.2 11.2 %collective-permute-start.7 = (f32[8,8192]{1,0:T(8,128)S(1)}, f32[8,8192]{1,0:T(8,128)S(1)}, u32[]{:S(2)}, u32[]{:S(2)}) collective-permute-start(f32[8,8192]{1,0:T(8,128)S(1)} %collective-permute-done.6.refs_11_), channel_id=1, source_target_pairs={{0,224},{32,0},{64,32},{96,64},{128,96},{160,128},{192,160},{224,1... | collective-permute-start | bytes 786440 | tf_op jit(solution)/shard_map/ppermute | solution.py:301
  49.3 2.1 %collective-permute-start.14 = (f32[40,128]{1,0:T(8,128)S(1)}, f32[40,128]{1,0:T(8,128)S(1)}, u32[]{:S(2)}, u32[]{:S(2)}) collective-permute-start(f32[40,128]{1,0:T(8,128)S(1)} %get-tuple-element.29), channel_id=1, source_target_pairs={{0,1},{1,0},{2,3},{3,2},{4,5},{5,4},{6,7},{7,6},{8,9},{9,8},{10,11... | collective-permute-start | bytes 61448 | tf_op jit(solution)/shard_map/ppermute | solution.py:275

commit v4 on v3

v4 whole, which is shorter than its diff:
```python
import math

import jax
import jax.numpy as jnp
from jax import lax
from jax.experimental import pallas as pl
from jax.experimental.pallas import tpu as pltpu
from jax.sharding import PartitionSpec as P

STEPS = 2
RINGS = 8
ROWS = 8
BF = jnp.bfloat16
F32 = jnp.float32
NT = (((1,), (1,)), ((), ()))
NN = (((1,), (0,)), ((), ()))


def constants(step):
    t = 0.6 - 0.1 * step
    alpha = 1.0 - 0.95 * t
    drift = -0.95 / alpha
    diffusion = 1.0 - 2.0 * drift * t
    return dict(
        t=t,
        alpha=alpha,
        gain=1.0 - 0.1 * drift - 0.1 * diffusion / t,
        pull=0.1 * diffusion * (1.0 - t),
        lift=0.1 * diffusion * alpha / t,
        kick=math.sqrt(0.1 * diffusion),
    )


def split3(x):
    a = x.astype(BF).astype(F32)
    r = x - a
    b = r.astype(BF).astype(F32)
    return a, b, r - b


def fields_kernel(cells, vals, mask, prec, targ):
    width = prec.shape[0]
    obs = cells.shape[1]
    rows = lax.broadcasted_iota(jnp.int32, (width, obs), 0)
    eye = lax.broadcasted_iota(jnp.int32, (width, width), 0) == lax.broadcasted_iota(
        jnp.int32, (width, width), 1
    )
    p_sum = jnp.zeros((width, width), F32)
    t_sum = jnp.zeros((width, width), F32)
    for s in range(cells.shape[0]):
        local = cells[s : s + 1, :] & (width * width - 1)
        high = jnp.where(rows == (local >> 7), 1.0, 0.0).astype(BF)
        low = rows == (local & 127)
        pieces = [jnp.ones((1, obs), F32), *split3(vals[s : s + 1, :])]
        sums = [
            lax.dot_general(
                high, jnp.where(low, piece, 0.0).astype(BF), NT, preferred_element_type=F32
            )
            for piece in pieces
        ]
        flags = mask[s : s + 1, :].astype(F32)
        flags = jnp.sum(jnp.where(eye, flags, 0.0), axis=1, keepdims=True)
        p_sum += flags * sums[0]
        t_sum += flags * (sums[1] + sums[2] + sums[3])
    prec[...] = p_sum
    targ[...] = t_sum


def fields(*args):
    shape = jax.ShapeDtypeStruct((128, 128), F32)
    return call(fields_kernel, (shape, shape), args, 10**9, name="fields")


def per_row(prec, targ, body):
    width = prec.shape[1]

    def step(h, carry):
        where = pl.ds(pl.multiple_of(h * width, width), width)
        body(where, prec[pl.ds(h, 1), :], targ[pl.ds(h, 1), :])
        return carry

    lax.fori_loop(0, prec.shape[0], step, 0, unroll=8)


CHUNK = 4096
LIMIT = pltpu.CompilerParams(vmem_limit_bytes=16 << 20)


def call(kernel, out_shape, args, flops, scratch=(), space=pltpu.VMEM, out_space=pltpu.VMEM, **kw):
    out_spec = pl.BlockSpec(memory_space=out_space)
    return pl.pallas_call(
        kernel,
        out_shape=out_shape,
        in_specs=[pl.BlockSpec(memory_space=space)] * len(args),
        out_specs=jax.tree.map(lambda _: out_spec, out_shape),
        scratch_shapes=scratch,
        compiler_params=LIMIT,
        cost_estimate=pl.CostEstimate(flops=flops, bytes_accessed=4 * 10**6, transcendentals=0),
        **kw,
    )(*args)


def split2(x):
    high = x.astype(BF).astype(F32)
    return jnp.concatenate([high, x - high], axis=0).astype(BF)


def column_chunks(blocks, body, acc):
    done = 0
    for pieces in zip(*blocks, strict=True):
        width = pieces[0].shape[1]
        for start in range(0, width, CHUNK):
            x = jnp.concatenate([p[:, start : start + CHUNK] for p in pieces], axis=0)
            acc = body(slice(done + start, done + start + CHUNK), x, acc)
        done += width
    return acc


def halves(full):
    half = full.shape[1] // 2
    return [full.at[:, :half], full.at[:, half:]]


def fold(z, m, n):
    z = z[:m] + z[m:]
    return z[:, :n] + z[:, n:]


def early_kernel(own, *refs):
    blocks, samples, noise, prec, targ, z, stack, base, ab, u = refs[:-9], *refs[-9:]
    k0, k1 = constants(0), constants(1)

    def local(where, p, t):
        a1 = k1["gain"] - k1["pull"] * p
        x = (k0["gain"] - k0["pull"] * p) * samples[:, where]
        x = x + k0["pull"] * t + k0["kick"] * noise[0, :, where]
        u[:, where] = x
        base[:, where] = a1 * x + k1["pull"] * t + k1["kick"] * noise[1, :, where]
        ab[:, where] = jnp.broadcast_to(k0["lift"] * a1, x.shape)

    per_row(prec, targ, local)
    blocks = [blocks[i : i + 2] for i in range(0, len(blocks), 2)]
    blocks = [halves(own), *blocks, halves(samples), halves(u)]

    def body(where, x, acc):
        y = split2(x)
        stack[: y.shape[0], where] = y
        return acc + lax.dot_general(y, y, NT, preferred_element_type=F32)

    rows = ROWS * len(blocks)
    acc = column_chunks(blocks, body, jnp.zeros((2 * rows, 2 * rows), F32))
    acc = fold(acc, rows, rows)
    near, q = rows - 2 * ROWS, z.shape[0]
    z[...] = jnp.zeros(z.shape, F32)
    z[:, :near] = acc[:q, :near]
    z[: near - q, 2 * q : q + near] = acc[q:near, q:near]
    z[: 2 * ROWS, 3 * q :] = acc[near:, :q]
    z[2 * ROWS :, 3 * q : 2 * q + near] = acc[near:, q:near]


def early(samples, noise, prec, targ, own, blocks):
    rows = ROWS * (3 + len(blocks) // 2)
    shapes = (
        jax.ShapeDtypeStruct((ROWS * RINGS // 2, 2 * ROWS * RINGS), F32),
        jax.ShapeDtypeStruct((2 * (rows + ROWS), own.shape[1]), BF),
        jax.ShapeDtypeStruct(own.shape, F32),
        jax.ShapeDtypeStruct(own.shape, F32),
    )
    args = (own, *blocks, samples, noise, prec, targ)
    return call(
        early_kernel, shapes, args, 10**9, [pltpu.VMEM(own.shape, F32)], name="early"
    )


def last_kernel(*refs):
    far, z1, _, z, stack = refs[:-4], *refs[-4:]
    new, old = ROWS, stack.shape[0] // 2 - ROWS

    def body(where, x, acc):
        y = split2(x)
        stack[2 * old :, where] = y
        return acc + lax.dot_general(y, stack[:, where], NT, preferred_element_type=F32)

    acc = column_chunks([far], body, jnp.zeros((2 * new, 2 * (old + new)), F32))
    left, right = fold(acc[:, : 2 * old], new, old), fold(acc[:, 2 * old :], new, new)
    near, q = old - 2 * ROWS, z.shape[0]
    column = left.T
    z[...] = z1[...]
    z[:, near : 2 * q] = column[:q]
    z[: near - q, q + near : 3 * q] = column[q:near]
    z[near - q :, 2 * q : q + near] = left[:, q:near]
    z[near - q :, q + near : 3 * q] = right
    z[2 * ROWS :, 2 * q + near :] = column[near:]


def last(far, z1, stack):
    shapes = (jax.ShapeDtypeStruct(z1.shape, F32), jax.ShapeDtypeStruct(stack.shape, BF))
    args = (*far, z1, stack)
    places = {len(args) - 1: 1}
    return call(last_kernel, shapes, args, 10**9, input_output_aliases=places, name="last")


def exponentials(x):
    e = jnp.exp(x - jnp.max(x, axis=1, keepdims=True))
    return e, 1.0 / jnp.sum(e, axis=1, keepdims=True)


def final_kernel(ncell, z_ref, stack, base, ab, out, buffer, sems):
    first = stack.shape[0] // 2 - 3 * ROWS
    k0, k1 = constants(0), constants(1)
    z = z_ref[0]
    for i in range(1, z_ref.shape[0]):
        z = z + z_ref[i]
    q = z.shape[0]
    corner, side, other, rest = [z[:, i * q : (i + 1) * q] for i in range(4)]
    eye = lax.broadcasted_iota(jnp.int32, (q, q), 0) == lax.broadcasted_iota(jnp.int32, (q, q), 1)
    norm = [jnp.sum(jnp.where(eye, x, 0.0), axis=0, keepdims=True) for x in (corner, other)]
    norm = jnp.concatenate(norm, axis=1)
    members = jnp.concatenate([z[:, : 2 * q], jnp.concatenate([side.T, other], axis=1)], axis=0)
    cross = jnp.concatenate([rest[: 2 * ROWS], rest[2 * ROWS :]], axis=1)

    def terms(k, cross):
        dist = k["alpha"] * k["alpha"] * norm - 2.0 * k["alpha"] * cross
        return exponentials(dist * (-1.0 / (2.0 * k["t"] * math.sqrt(ncell))))

    def dot(x, y):
        return lax.dot_general(
            x, y, NN, precision=lax.Precision.HIGHEST, preferred_element_type=F32
        )

    e0, scale0 = terms(k0, cross[:ROWS])
    lift = dot(e0, members)
    e1, scale1 = terms(k1, cross[ROWS:] + k0["lift"] * (scale0 * lift))
    scale1 = k1["lift"] * scale1
    w = jnp.concatenate([e0, e1], axis=0)
    wh = w.astype(BF).astype(F32)
    w = jnp.concatenate([wh, w - wh], axis=0)
    none = jnp.zeros((4 * ROWS, 2 * ROWS), F32)
    near = jnp.concatenate([w[:, :first], none], axis=1)
    w = jnp.concatenate([near, near, w[:, first:], w[:, first:]], axis=1).astype(BF)
    pieces = sems.shape[0]
    width = out.shape[1] // pieces
    copies = []
    for i in range(pieces):
        to = slice(i * width, (i + 1) * width)
        m = lax.dot_general(w, stack[:, to], NN, preferred_element_type=F32)
        m = m[: 2 * ROWS] + m[2 * ROWS :]
        buffer[:, to] = base[:, to] + ab[:, to] * (scale0 * m[:ROWS]) + scale1 * m[ROWS:]
        copies.append(pltpu.make_async_copy(buffer.at[:, to], out.at[:, to], sems.at[i]))
        copies[-1].start()
    for copy in copies:
        copy.wait()


def final(ncell, z, stack, base, ab):
    def final(*refs):
        return final_kernel(ncell, *refs)

    shape = jax.ShapeDtypeStruct(base.shape, F32)
    scratch = [pltpu.VMEM(base.shape, F32), pltpu.SemaphoreType.DMA((4,))]
    args = (z, stack, base, ab)
    return call(final, shape, args, 10**9, scratch, out_space=pltpu.HBM, name="final")


def total(x):
    x = x + lax.ppermute(x, "core", [(0, 1), (1, 0)])
    x = jnp.broadcast_to(x[None], (lax.axis_size("x") * lax.axis_size("y"), *x.shape))
    return lax.all_to_all(x, ("x", "y"), split_axis=0, concat_axis=0, tiled=True)


def per_device(prior, samples, noise, obs_cells, obs_values, seismic_mask):
    cells = prior.shape[1]
    half = cells // 2
    ncell = cells * lax.axis_size("x") * lax.axis_size("y") * lax.axis_size("core")
    up = [(i, (i + 1) % RINGS) for i in range(RINGS)]
    down = [(i, (i - 1) % RINGS) for i in range(RINGS)]
    rising = [prior[:, :half], prior[:, half:]]
    falling = list(rising)
    blocks = []
    prec, targ = fields(obs_cells, obs_values, seismic_mask)
    for hop in range(3):
        if hop == 1:
            rising[0], prec, targ = lax.optimization_barrier((rising[0], prec, targ))
        for c in range(2):
            rising[c] = lax.ppermute(rising[c], "member", up)
            falling[c] = lax.ppermute(falling[c], "member", down)
        blocks += [*rising, *falling]
    z1, stack, base, ab = early(samples, noise, prec, targ, prior, blocks)
    far = [lax.ppermute(rising[0], "member", up), lax.ppermute(falling[1], "member", down)]
    z, stack = last(far, z1, stack)
    z = total(z)
    return final(ncell, z, stack, base, ab)


def solution(mesh):
    mesh = jax.sharding.Mesh(mesh.devices.reshape(RINGS, 4, 4, 2), ("member", "x", "y", "core"))
    cell = ("x", "y", "core")
    in_specs = (
        P("member", cell),
        P("member", cell),
        P(None, "member", cell),
        P(None, cell),
        P(None, cell),
        P(None, cell),
    )
    return jax.shard_map(
        per_device, mesh=mesh, in_specs=in_specs, out_specs=P("member", cell), check_vma=False
    )
```

time: 69.5 us -> 68.7 us (0.988)
  waiting for transfers between devices: 18.3 us -> 13.9 us
  starting transfers between devices: 24 us -> 27.2 us
  local copies, waits for them, and re-layouts: 3.36 us -> 5.37 us
  Pallas kernels: 8.32 us -> 7.52 us
    ppermute x6, waiting for transfers between devices: 13.8 us -> 5.53 us  [per_device(): rising[c] = lax.ppermute(rising[c], 'member', up)]
    ppermute x6, waiting for transfers between devices: 0.02 us -> 6.23 us  [per_device(): falling[c] = lax.ppermute(falling[c], 'member', down)]
    ppermute x1, waiting for transfers between devices: 3.67 us -> 0.01 us  [per_device(): lax.ppermute(rising[0], 'member', up)]
    unnamed x12, local copies, waits for them, and re-layouts: 2.12 us -> 4.2 us
    ppermute x1, starting transfers between devices: 1.28 us -> 2.82 us  [total(): x = x + lax.ppermute(x, 'core', [(0, 1), (1, 0)])]
    ppermute x1, waiting for transfers between devices: 0.01 us -> 1.35 us  [per_device(): lax.ppermute(falling[1], 'member', down)]
    ppermute x6, starting transfers between devices: 17.4 us -> 18.4 us  [per_device(): falling[c] = lax.ppermute(falling[c], 'member', down)]
    pallas_call x5 -> x4, Pallas kernels: 8.32 us -> 7.52 us  [call(): pl.pallas_call(kernel, out_shape=out_shape, in_specs=[pl.BlockSpec(memory...]
  transfers between devices with their start and end apart: 15 -> 15, of which waited for: 7 -> 9; matrix products, arithmetic and copies ran while one was open for 0% -> 0% of each run, Pallas kernels for 6% -> 5%
where the time goes in v4:
time: 68.7 us; the launch traced here: 68.4 us
  starting transfers between devices  27.2 us (40%)
  blocking collectives  14.1 us (21%)
  waiting for transfers between devices  13.9 us (20%)
  Pallas kernels  7.52 us (11%)
  local copies, waits for them, and re-layouts  5.37 us (8%)
    ppermute x6, starting transfers between devices, per_device(): falling[c] = lax.ppermute(falling[c], 'member', down)  18.4 us
    all_to_all x1, blocking collectives, total(): lax.all_to_all(x, ('x', 'y'), split_axis=0, concat_axis=0, tiled=True)  14.1 us
    pallas_call x4, Pallas kernels, call(): pl.pallas_call(kernel, out_shape=out_shape, in_specs=[pl.BlockSpec(memory...  7.52 us
    ppermute x6, waiting for transfers between devices, per_device(): falling[c] = lax.ppermute(falling[c], 'member', down)  6.23 us
    ppermute x6, waiting for transfers between devices, per_device(): rising[c] = lax.ppermute(rising[c], 'member', up)  5.53 us
    unnamed x12, local copies, waits for them, and re-layouts  4.2 us
    ppermute x1, starting transfers between devices, per_device(): lax.ppermute(falling[1], 'member', down)  3.41 us
    ppermute x1, starting transfers between devices, total(): x = x + lax.ppermute(x, 'core', [(0, 1), (1, 0)])  2.82 us
  transfers between devices with their start and end apart: 15, of which 9 were waited for; matrix products, arithmetic and copies ran while one was open for 0% of the time, Pallas kernels for 5%

profile of v4, /device:TPU:1, one launch (start us, length us, event | category | flops | bytes accessed | tf_op | source)
XLA Modules:
  0.0 68.4 jit_solution(13199560738587584315)
XLA Ops:
  0.0 0.0 copy-start.1
  0.0 1.2 %fusion = (f32[8,8192]{1,0:T(8,128)S(1)}, f32[8,8192]{1,0:T(8,128)S(1)}) fusion(f32[8,16384]{1,0:T(8,128)} %own.1), kind=kLoop, calls=%fused_computation | loop fusion | bytes 1048576 | tf_op jit(solution)/shard_map/slice | solution.py:277
  1.2 2.5 %collective-permute-start = (f32[8,8192]{1,0:T(8,128)S(1)}, f32[8,8192]{1,0:T(8,128)S(1)}, u32[]{:S(2)}, u32[]{:S(2)}) collective-permute-start(f32[8,8192]{1,0:T(8,128)S(1)} %get-tuple-element.28), channel_id=1, source_target_pairs={{0,32},{32,64},{64,96},{96,128},{128,160},{160,192},{192,224},{224... | collective-permute-start | bytes 786440 | tf_op jit(solution)/shard_map/ppermute | solution.py:285
  3.7 4.0 %collective-permute-start.4 = (f32[8,8192]{1,0:T(8,128)S(1)}, f32[8,8192]{1,0:T(8,128)S(1)}, u32[]{:S(2)}, u32[]{:S(2)}) collective-permute-start(f32[8,8192]{1,0:T(8,128)S(1)} %get-tuple-element.27), channel_id=1, source_target_pairs={{0,224},{32,0},{64,32},{96,64},{128,96},{160,128},{192,160},{224,1... | collective-permute-start | bytes 786440 | tf_op jit(solution)/shard_map/ppermute | solution.py:286
  7.7 0.0 collective-permute-start.8
  7.7 2.7 %collective-permute-start.9 = (f32[8,8192]{1,0:T(8,128)S(1)}, f32[8,8192]{1,0:T(8,128)S(1)}, u32[]{:S(2)}, u32[]{:S(2)}) collective-permute-start(f32[8,8192]{1,0:T(8,128)S(1)} %get-tuple-element.28), channel_id=1, source_target_pairs={{0,224},{32,0},{64,32},{96,64},{128,96},{160,128},{192,160},{224,1... | collective-permute-start | bytes 786440 | tf_op jit(solution)/shard_map/ppermute | solution.py:286
  10.4 0.0 copy-start.3
  10.4 0.7 %copy-done.3 = s32[2,2048]{1,0:T(2,128)S(1)} copy-done((s32[2,2048]{1,0:T(2,128)S(1)}, s32[2,2048]{1,0:T(2,128)}, u32[]{:S(2)}) %copy-start.3) | copy-done | bytes 16408
  11.1 0.0 copy-start.4
  11.1 0.7 %copy-done.4 = f32[2,2048]{1,0:T(2,128)S(1)} copy-done((f32[2,2048]{1,0:T(2,128)S(1)}, f32[2,2048]{1,0:T(2,128)}, u32[]{:S(2)}) %copy-start.4) | copy-done | bytes 16408
  11.8 0.0 copy-start.5
  11.8 0.7 copy-done.5
  12.5 1.4 %fields.1 = (f32[128,128]{1,0:T(8,128)S(1)}, f32[128,128]{1,0:T(8,128)S(1)}) custom-call(s32[2,2048]{1,0:T(2,128)S(1)} %copy-done.3, f32[2,2048]{1,0:T(2,128)S(1)} %copy-done.4, s32[2,128]{1,0:T(2,128)S(1)} %copy-done.5), custom_call_target="tpu_custom_call" | custom-call | flops 1000000000 | bytes 4000000 | tf_op jit(solution)/shard_map/fields/pallas_call | solution.py:91
  13.9 0.0 collective-permute-done.refs_0_
  13.9 0.0 collective-permute-done.4.refs_3_
  13.9 2.2 %collective-permute-start.5 = (f32[8,8192]{1,0:T(8,128)S(1)}, f32[8,8192]{1,0:T(8,128)S(1)}, u32[]{:S(2)}, u32[]{:S(2)}) collective-permute-start(f32[8,8192]{1,0:T(8,128)S(1)} %collective-permute-done.4.refs_3_), channel_id=1, source_target_pairs={{0,224},{32,0},{64,32},{96,64},{128,96},{160,128},{192,160},{224,1... | collective-permute-start | bytes 786440 | tf_op jit(solution)/shard_map/ppermute | solution.py:286
  16.1 0.0 collective-permute-start.1
  16.1 3.2 %collective-permute-done.8.refs_1_ = f32[8,8192]{1,0:T(8,128)S(1)} collective-permute-done((f32[8,8192]{1,0:T(8,128)S(1)}, f32[8,8192]{1,0:T(8,128)S(1)}, u32[]{:S(2)}, u32[]{:S(2)}) %collective-permute-start.8) | collective-permute-done | bytes 262176 | tf_op jit(solution)/shard_map/ppermute | solution.py:285
  19.3 0.0 collective-permute-start.10
  19.3 0.0 collective-permute-done.9.refs_2_
  19.3 2.7 %collective-permute-start.11 = (f32[8,8192]{1,0:T(8,128)S(1)}, f32[8,8192]{1,0:T(8,128)S(1)}, u32[]{:S(2)}, u32[]{:S(2)}) collective-permute-start(f32[8,8192]{1,0:T(8,128)S(1)} %collective-permute-done.9.refs_2_), channel_id=1, source_target_pairs={{0,224},{32,0},{64,32},{96,64},{128,96},{160,128},{192,160},{224,1... | collective-permute-start | bytes 786440 | tf_op jit(solution)/shard_map/ppermute | solution.py:286
  22.0 2.0 %collective-permute-done.5.refs_7_ = f32[8,8192]{1,0:T(8,128)S(1)} collective-permute-done((f32[8,8192]{1,0:T(8,128)S(1)}, f32[8,8192]{1,0:T(8,128)S(1)}, u32[]{:S(2)}, u32[]{:S(2)}) %collective-permute-start.5) | collective-permute-done | bytes 262176 | tf_op jit(solution)/shard_map/ppermute | solution.py:286
  23.9 3.4 %collective-permute-start.6 = (f32[8,8192]{1,0:T(8,128)S(1)}, f32[8,8192]{1,0:T(8,128)S(1)}, u32[]{:S(2)}, u32[]{:S(2)}) collective-permute-start(f32[8,8192]{1,0:T(8,128)S(1)} %collective-permute-done.5.refs_7_), channel_id=1, source_target_pairs={{0,224},{32,0},{64,32},{96,64},{128,96},{160,128},{192,160},{224,1... | collective-permute-start | bytes 786440 | tf_op jit(solution)/shard_map/ppermute | solution.py:286
  27.4 0.0 collective-permute-done.1.refs_4_
  27.4 0.0 collective-permute-start.2
  27.4 1.2 %collective-permute-done.10.refs_5_ = f32[8,8192]{1,0:T(8,128)S(1)} collective-permute-done((f32[8,8192]{1,0:T(8,128)S(1)}, f32[8,8192]{1,0:T(8,128)S(1)}, u32[]{:S(2)}, u32[]{:S(2)}) %collective-permute-start.10) | collective-permute-done | bytes 262176 | tf_op jit(solution)/shard_map/ppermute | solution.py:285
  28.6 0.0 collective-permute-start.12
  28.6 1.0 %collective-permute-done.11.refs_6_ = f32[8,8192]{1,0:T(8,128)S(1)} collective-permute-done((f32[8,8192]{1,0:T(8,128)S(1)}, f32[8,8192]{1,0:T(8,128)S(1)}, u32[]{:S(2)}, u32[]{:S(2)}) %collective-permute-start.11) | collective-permute-done | bytes 262176 | tf_op jit(solution)/shard_map/ppermute | solution.py:286
  29.6 3.4 %collective-permute-start.13 = (f32[8,8192]{1,0:T(8,128)S(1)}, f32[8,8192]{1,0:T(8,128)S(1)}, u32[]{:S(2)}, u32[]{:S(2)}) collective-permute-start(f32[8,8192]{1,0:T(8,128)S(1)} %collective-permute-done.11.refs_6_), channel_id=1, source_target_pairs={{0,224},{32,0},{64,32},{96,64},{128,96},{160,128},{192,160},{224,1... | collective-permute-start | bytes 786440 | tf_op jit(solution)/shard_map/ppermute | solution.py:286
  33.0 2.2 %collective-permute-done.6.refs_11_ = f32[8,8192]{1,0:T(8,128)S(1)} collective-permute-done((f32[8,8192]{1,0:T(8,128)S(1)}, f32[8,8192]{1,0:T(8,128)S(1)}, u32[]{:S(2)}, u32[]{:S(2)}) %collective-permute-start.6) | collective-permute-done | bytes 262176 | tf_op jit(solution)/shard_map/ppermute | solution.py:286
  35.2 3.4 %collective-permute-start.7 = (f32[8,8192]{1,0:T(8,128)S(1)}, f32[8,8192]{1,0:T(8,128)S(1)}, u32[]{:S(2)}, u32[]{:S(2)}) collective-permute-start(f32[8,8192]{1,0:T(8,128)S(1)} %collective-permute-done.6.refs_11_), channel_id=1, source_target_pairs={{0,224},{32,0},{64,32},{96,64},{128,96},{160,128},{192,160},{224,1... | collective-permute-start | bytes 786440 | tf_op jit(solution)/shard_map/ppermute | solution.py:289
  38.6 0.0 collective-permute-done.2.refs_8_
  38.6 0.0 collective-permute-start.3
  38.6 1.1 %collective-permute-done.12.refs_9_ = f32[8,8192]{1,0:T(8,128)S(1)} collective-permute-done((f32[8,8192]{1,0:T(8,128)S(1)}, f32[8,8192]{1,0:T(8,128)S(1)}, u32[]{:S(2)}, u32[]{:S(2)}) %collective-permute-start.12) | collective-permute-done | bytes 262176 | tf_op jit(solution)/shard_map/ppermute | solution.py:285
  39.7 1.1 %collective-permute-done.13.refs_10_ = f32[8,8192]{1,0:T(8,128)S(1)} collective-permute-done((f32[8,8192]{1,0:T(8,128)S(1)}, f32[8,8192]{1,0:T(8,128)S(1)}, u32[]{:S(2)}, u32[]{:S(2)}) %collective-permute-start.13) | collective-permute-done | bytes 262176 | tf_op jit(solution)/shard_map/ppermute | solution.py:286
  40.8 0.0 copy-done.1
  40.8 0.0 copy-start
  40.8 1.0 %copy-done = f32[8,16384]{1,0:T(8,128)S(1)} copy-done((f32[8,16384]{1,0:T(8,128)S(1)}, f32[8,16384]{1,0:T(8,128)}, u32[]{:S(2)}) %copy-start) | copy-done | bytes 524312
  41.8 0.0 copy-start.2
  41.8 1.0 %copy-done.2 = f32[8,16384]{1,0:T(8,128)S(1)} copy-done((f32[8,16384]{1,0:T(8,128)S(1)}, f32[8,16384]{1,0:T(8,128)}, u32[]{:S(2)}) %copy-start.2) | copy-done | bytes 524312
  42.9 2.2 %early.1 = (f32[32,128]{1,0:T(8,128)S(1)}, bf16[160,16384]{1,0:T(8,128)(2,1)S(1)}, f32[8,16384]{1,0:T(8,128)S(1)}, f32[8,16384]{1,0:T(8,128)S(1)}) custom-call(f32[8,16384]{1,0:T(8,128)S(1)} %copy-done, f32[8,8192]{1,0:T(8,128)S(1)} %collective-permute-done.refs_0_, f32[8,8192]{1,0:T(8,128)S(1)} %collective-permute-done.8.refs_1_, ...), custom_call_target="tpu_custom_call" | custom-call | flops 1000000000 | bytes 4000000 | tf_op jit(solution)/shard_map/early/pallas_call | solution.py:91
  45.1 1.3 %collective-permute-done.7.refs_1_ = f32[8,8192]{1,0:T(8,128)S(1)} collective-permute-done((f32[8,8192]{1,0:T(8,128)S(1)}, f32[8,8192]{1,0:T(8,128)S(1)}, u32[]{:S(2)}, u32[]{:S(2)}) %collective-permute-start.7) | collective-permute-done | bytes 262176 | tf_op jit(solution)/shard_map/ppermute | solution.py:289
  46.4 0.0 collective-permute-done.3.refs_0_
  46.4 1.7 %last.1 = (f32[32,128]{1,0:T(8,128)S(1)}, bf16[160,16384]{1,0:T(8,128)(2,1)S(1)}) custom-call(f32[8,8192]{1,0:T(8,128)S(1)} %collective-permute-done.3.refs_0_, f32[8,8192]{1,0:T(8,128)S(1)} %collective-permute-done.7.refs_1_, f32[32,128]{1,0:T(8,128)S(1)} %get-tuple-element.21.refs_2_, ...), custom_call_target="tpu_custom_call", output_to_operand_aliasing={{1}: (3, {})} | custom-call | flops 1000000000 | bytes 4000000 | tf_op jit(solution)/shard_map/last/pallas_call | solution.py:91
  48.1 2.8 %collective-permute-start.14 = (f32[32,128]{1,0:T(8,128)S(1)}, f32[32,128]{1,0:T(8,128)S(1)}, u32[]{:S(2)}, u32[]{:S(2)}) collective-permute-start(f32[32,128]{1,0:T(8,128)S(1)} %get-tuple-element.23), channel_id=1, source_target_pairs={{0,1},{1,0},{2,3},{3,2},{4,5},{5,4},{6,7},{7,6},{8,9},{9,8},{10,11... | collective-permute-start | bytes 49160 | tf_op jit(solution)/shard_map/ppermute | solution.py:266
  50.9 0.8 %collective-permute-done.14 = f32[32,128]{1,0:T(8,128)S(1)} collective-permute-done((f32[32,128]{1,0:T(8,128)S(1)}, f32[32,128]{1,0:T(8,128)S(1)}, u32[]{:S(2)}, u32[]{:S(2)}) %collective-permute-start.14) | collective-permute-done | bytes 16416 | tf_op jit(solution)/shard_map/ppermute | solution.py:266
  51.8 14.1 %all_to_all.5.refs_0_ = f32[16,32,128]{2,1,0:T(8,128)S(1)} all-to-all(f32[16,32,128]{2,1,0:T(8,128)S(1)} %broadcast_in_dim.2), channel_id=1, replica_groups=mesh['member'=8,'x'=4,'y'=4,'core'=2] {'x','y'}, dimensions={0} | all-to-all | bytes 524288 | tf_op jit(solution)/shard_map/all_to_all | solution.py:268
  65.9 2.3 %final.1 = f32[8,16384]{1,0:T(8,128)} custom-call(f32[16,32,128]{2,1,0:T(8,128)S(1)} %all_to_all.5.refs_0_, bf16[160,16384]{1,0:T(8,128)(2,1)S(1)} %get-tuple-element.24.refs_1_, f32[8,16384]{1,0:T(8,128)S(1)} %get-tuple-element.25.refs_2_, f32[8,16384]{1,0:T(8,128)S(1)} %get-tuple-element.26.refs_3_), custom_call_target="tpu_custom_call" | custom-call | flops 1000000000 | bytes 4000000 | tf_op jit(solution)/shard_map/final/pallas_call | solution.py:91
  (2 shorter events, 0.0 us)
Async XLA Ops:
  0.0 40.8 %copy-start.1 = (f32[2,8,16384]{2,1,0:T(8,128)S(1)}, f32[2,8,16384]{2,1,0:T(8,128)}, u32[]{:S(2)}) copy-start(f32[2,8,16384]{2,1,0:T(8,128)} %refs_13_.1) | copy-start | bytes 3145732
  1.2 12.8 %collective-permute-start = (f32[8,8192]{1,0:T(8,128)S(1)}, f32[8,8192]{1,0:T(8,128)S(1)}, u32[]{:S(2)}, u32[]{:S(2)}) collective-permute-start(f32[8,8192]{1,0:T(8,128)S(1)} %get-tuple-element.28), channel_id=1, source_target_pairs={{0,32},{32,64},{64,96},{96,128},{128,160},{160,192},{192,224},{224... | collective-permute-start | bytes 786440 | tf_op jit(solution)/shard_map/ppermute | solution.py:285
  3.7 10.2 %collective-permute-start.4 = (f32[8,8192]{1,0:T(8,128)S(1)}, f32[8,8192]{1,0:T(8,128)S(1)}, u32[]{:S(2)}, u32[]{:S(2)}) collective-permute-start(f32[8,8192]{1,0:T(8,128)S(1)} %get-tuple-element.27), channel_id=1, source_target_pairs={{0,224},{32,0},{64,32},{96,64},{128,96},{160,128},{192,160},{224,1... | collective-permute-start | bytes 786440 | tf_op jit(solution)/shard_map/ppermute | solution.py:286
  7.7 11.6 %collective-permute-start.8 = (f32[8,8192]{1,0:T(8,128)S(1)}, f32[8,8192]{1,0:T(8,128)S(1)}, u32[]{:S(2)}, u32[]{:S(2)}) collective-permute-start(f32[8,8192]{1,0:T(8,128)S(1)} %get-tuple-element.27), channel_id=1, source_target_pairs={{0,32},{32,64},{64,96},{96,128},{128,160},{160,192},{192,224},{224... | collective-permute-start | bytes 786440 | tf_op jit(solution)/shard_map/ppermute | solution.py:285
  7.7 11.6 %collective-permute-start.9 = (f32[8,8192]{1,0:T(8,128)S(1)}, f32[8,8192]{1,0:T(8,128)S(1)}, u32[]{:S(2)}, u32[]{:S(2)}) collective-permute-start(f32[8,8192]{1,0:T(8,128)S(1)} %get-tuple-element.28), channel_id=1, source_target_pairs={{0,224},{32,0},{64,32},{96,64},{128,96},{160,128},{192,160},{224,1... | collective-permute-start | bytes 786440 | tf_op jit(solution)/shard_map/ppermute | solution.py:286
  10.4 0.7 %copy-start.3 = (s32[2,2048]{1,0:T(2,128)S(1)}, s32[2,2048]{1,0:T(2,128)}, u32[]{:S(2)}) copy-start(s32[2,2048]{1,0:T(2,128)} %cells.1) | copy-start | bytes 49156
  11.1 0.7 %copy-start.4 = (f32[2,2048]{1,0:T(2,128)S(1)}, f32[2,2048]{1,0:T(2,128)}, u32[]{:S(2)}) copy-start(f32[2,2048]{1,0:T(2,128)} %vals.1) | copy-start | bytes 49156
  11.8 0.7 copy-start.5
  13.9 10.0 %collective-permute-start.5 = (f32[8,8192]{1,0:T(8,128)S(1)}, f32[8,8192]{1,0:T(8,128)S(1)}, u32[]{:S(2)}, u32[]{:S(2)}) collective-permute-start(f32[8,8192]{1,0:T(8,128)S(1)} %collective-permute-done.4.refs_3_), channel_id=1, source_target_pairs={{0,224},{32,0},{64,32},{96,64},{128,96},{160,128},{192,160},{224,1... | collective-permute-start | bytes 786440 | tf_op jit(solution)/shard_map/ppermute | solution.py:286
  16.1 11.2 %collective-permute-start.1 = (f32[8,8192]{1,0:T(8,128)S(1)}, f32[8,8192]{1,0:T(8,128)S(1)}, u32[]{:S(2)}, u32[]{:S(2)}) collective-permute-start(f32[8,8192]{1,0:T(8,128)S(1)} %collective-permute-done.refs_0_), channel_id=1, source_target_pairs={{0,32},{32,64},{64,96},{96,128},{128,160},{160,192},{192,224},{224... | collective-permute-start | bytes 786440 | tf_op jit(solution)/shard_map/ppermute | solution.py:285
  19.3 9.3 %collective-permute-start.10 = (f32[8,8192]{1,0:T(8,128)S(1)}, f32[8,8192]{1,0:T(8,128)S(1)}, u32[]{:S(2)}, u32[]{:S(2)}) collective-permute-start(f32[8,8192]{1,0:T(8,128)S(1)} %collective-permute-done.8.refs_1_), channel_id=1, source_target_pairs={{0,32},{32,64},{64,96},{96,128},{128,160},{160,192},{192,224},{224... | collective-permute-start | bytes 786440 | tf_op jit(solution)/shard_map/ppermute | solution.py:285
  19.3 10.3 %collective-permute-start.11 = (f32[8,8192]{1,0:T(8,128)S(1)}, f32[8,8192]{1,0:T(8,128)S(1)}, u32[]{:S(2)}, u32[]{:S(2)}) collective-permute-start(f32[8,8192]{1,0:T(8,128)S(1)} %collective-permute-done.9.refs_2_), channel_id=1, source_target_pairs={{0,224},{32,0},{64,32},{96,64},{128,96},{160,128},{192,160},{224,1... | collective-permute-start | bytes 786440 | tf_op jit(solution)/shard_map/ppermute | solution.py:286
  23.9 11.2 %collective-permute-start.6 = (f32[8,8192]{1,0:T(8,128)S(1)}, f32[8,8192]{1,0:T(8,128)S(1)}, u32[]{:S(2)}, u32[]{:S(2)}) collective-permute-start(f32[8,8192]{1,0:T(8,128)S(1)} %collective-permute-done.5.refs_7_), channel_id=1, source_target_pairs={{0,224},{32,0},{64,32},{96,64},{128,96},{160,128},{192,160},{224,1... | collective-permute-start | bytes 786440 | tf_op jit(solution)/shard_map/ppermute | solution.py:286
  27.4 11.2 %collective-permute-start.2 = (f32[8,8192]{1,0:T(8,128)S(1)}, f32[8,8192]{1,0:T(8,128)S(1)}, u32[]{:S(2)}, u32[]{:S(2)}) collective-permute-start(f32[8,8192]{1,0:T(8,128)S(1)} %collective-permute-done.1.refs_4_), channel_id=1, source_target_pairs={{0,32},{32,64},{64,96},{96,128},{128,160},{160,192},{192,224},{224... | collective-permute-start | bytes 786440 | tf_op jit(solution)/shard_map/ppermute | solution.py:285
  28.6 11.2 %collective-permute-start.12 = (f32[8,8192]{1,0:T(8,128)S(1)}, f32[8,8192]{1,0:T(8,128)S(1)}, u32[]{:S(2)}, u32[]{:S(2)}) collective-permute-start(f32[8,8192]{1,0:T(8,128)S(1)} %collective-permute-done.10.refs_5_), channel_id=1, source_target_pairs={{0,32},{32,64},{64,96},{96,128},{128,160},{160,192},{192,224},{224... | collective-permute-start | bytes 786440 | tf_op jit(solution)/shard_map/ppermute | solution.py:285
  29.6 11.2 %collective-permute-start.13 = (f32[8,8192]{1,0:T(8,128)S(1)}, f32[8,8192]{1,0:T(8,128)S(1)}, u32[]{:S(2)}, u32[]{:S(2)}) collective-permute-start(f32[8,8192]{1,0:T(8,128)S(1)} %collective-permute-done.11.refs_6_), channel_id=1, source_target_pairs={{0,224},{32,0},{64,32},{96,64},{128,96},{160,128},{192,160},{224,1... | collective-permute-start | bytes 786440 | tf_op jit(solution)/shard_map/ppermute | solution.py:286
  35.2 11.2 %collective-permute-start.7 = (f32[8,8192]{1,0:T(8,128)S(1)}, f32[8,8192]{1,0:T(8,128)S(1)}, u32[]{:S(2)}, u32[]{:S(2)}) collective-permute-start(f32[8,8192]{1,0:T(8,128)S(1)} %collective-permute-done.6.refs_11_), channel_id=1, source_target_pairs={{0,224},{32,0},{64,32},{96,64},{128,96},{160,128},{192,160},{224,1... | collective-permute-start | bytes 786440 | tf_op jit(solution)/shard_map/ppermute | solution.py:289
  38.6 7.8 %collective-permute-start.3 = (f32[8,8192]{1,0:T(8,128)S(1)}, f32[8,8192]{1,0:T(8,128)S(1)}, u32[]{:S(2)}, u32[]{:S(2)}) collective-permute-start(f32[8,8192]{1,0:T(8,128)S(1)} %collective-permute-done.2.refs_8_), channel_id=1, source_target_pairs={{0,32},{32,64},{64,96},{96,128},{128,160},{160,192},{192,224},{224... | collective-permute-start | bytes 786440 | tf_op jit(solution)/shard_map/ppermute | solution.py:289
  40.8 1.0 %copy-start = (f32[8,16384]{1,0:T(8,128)S(1)}, f32[8,16384]{1,0:T(8,128)}, u32[]{:S(2)}) copy-start(f32[8,16384]{1,0:T(8,128)} %own.1) | copy-start | bytes 1572868
  41.8 1.0 %copy-start.2 = (f32[8,16384]{1,0:T(8,128)S(1)}, f32[8,16384]{1,0:T(8,128)}, u32[]{:S(2)}) copy-start(f32[8,16384]{1,0:T(8,128)} %refs_12_.1) | copy-start | bytes 1572868
  48.1 3.7 %collective-permute-start.14 = (f32[32,128]{1,0:T(8,128)S(1)}, f32[32,128]{1,0:T(8,128)S(1)}, u32[]{:S(2)}, u32[]{:S(2)}) collective-permute-start(f32[32,128]{1,0:T(8,128)S(1)} %get-tuple-element.23), channel_id=1, source_target_pairs={{0,1},{1,0},{2,3},{3,2},{4,5},{5,4},{6,7},{7,6},{8,9},{9,8},{10,11... | collective-permute-start | bytes 49160 | tf_op jit(solution)/shard_map/ppermute | solution.py:266

commit v5 on v4

--- a/solution.py
+++ b/solution.py
@@ -229,8 +229,7 @@
         )
 
     e0, scale0 = terms(k0, cross[:ROWS])
-    lift = dot(e0, members)
-    e1, scale1 = terms(k1, cross[ROWS:] + k0["lift"] * (scale0 * lift))
+    e1, scale1 = terms(k1, cross[ROWS:] + k0["lift"] * dot(e0 * scale0, members))
     scale1 = k1["lift"] * scale1
     w = jnp.concatenate([e0, e1], axis=0)
     wh = w.astype(BF).astype(F32)
@@ -279,12 +278,13 @@
     blocks = []
     prec, targ = fields(obs_cells, obs_values, seismic_mask)
     for hop in range(3):
-        if hop == 1:
+        if hop > 0:
             rising[0], prec, targ = lax.optimization_barrier((rising[0], prec, targ))
         for c in range(2):
             rising[c] = lax.ppermute(rising[c], "member", up)
             falling[c] = lax.ppermute(falling[c], "member", down)
         blocks += [*rising, *falling]
+    rising[0], prec, targ = lax.optimization_barrier((rising[0], prec, targ))
     z1, stack, base, ab = early(samples, noise, prec, targ, prior, blocks)
     far = [lax.ppermute(rising[0], "member", up), lax.ppermute(falling[1], "member", down)]
     z, stack = last(far, z1, stack)

time: 68.7 us -> 68.7 us (level)
  waiting for transfers between devices: 13.9 us -> 15.8 us
  starting transfers between devices: 27.2 us -> 25.3 us
    ppermute x6, waiting for transfers between devices: 5.53 us -> 14.6 us  [per_device(): rising[c] = lax.ppermute(rising[c], 'member', up)]
    ppermute x6, waiting for transfers between devices: 6.23 us -> 0.02 us  [per_device(): falling[c] = lax.ppermute(falling[c], 'member', down)]
    ppermute x6, starting transfers between devices: 18.4 us -> 17.4 us  [per_device(): falling[c] = lax.ppermute(falling[c], 'member', down)]
    ppermute x1, waiting for transfers between devices: 1.35 us -> 0.37 us  [per_device(): lax.ppermute(falling[1], 'member', down)]
    ppermute x1, starting transfers between devices: 3.41 us -> 2.44 us  [per_device(): lax.ppermute(falling[1], 'member', down)]
  transfers between devices with their start and end apart: 15 -> 15, of which waited for: 9 -> 7; matrix products, arithmetic and copies ran while one was open for 0% -> 0% of each run, Pallas kernels for 5% -> 5%
where the time goes in v5:
time: 68.7 us; the launch traced here: 68.3 us
  starting transfers between devices  25.3 us (37%)
  waiting for transfers between devices  15.8 us (23%)
  blocking collectives  14.1 us (21%)
  Pallas kernels  7.5 us (11%)
  local copies, waits for them, and re-layouts  5.37 us (8%)
    ppermute x6, starting transfers between devices, per_device(): falling[c] = lax.ppermute(falling[c], 'member', down)  17.4 us
    ppermute x6, waiting for transfers between devices, per_device(): rising[c] = lax.ppermute(rising[c], 'member', up)  14.6 us
    all_to_all x1, blocking collectives, total(): lax.all_to_all(x, ('x', 'y'), split_axis=0, concat_axis=0, tiled=True)  14.1 us
    pallas_call x4, Pallas kernels, call(): pl.pallas_call(kernel, out_shape=out_shape, in_specs=[pl.BlockSpec(memory...  7.5 us
    unnamed x12, local copies, waits for them, and re-layouts  4.2 us
    ppermute x1, starting transfers between devices, total(): x = x + lax.ppermute(x, 'core', [(0, 1), (1, 0)])  2.82 us
    ppermute x6, starting transfers between devices, per_device(): rising[c] = lax.ppermute(rising[c], 'member', up)  2.64 us
    ppermute x1, starting transfers between devices, per_device(): lax.ppermute(falling[1], 'member', down)  2.44 us
  transfers between devices with their start and end apart: 15, of which 7 were waited for; matrix products, arithmetic and copies ran while one was open for 0% of the time, Pallas kernels for 5%

profile of v5, /device:TPU:1, one launch (start us, length us, event | category | flops | bytes accessed | tf_op | source)
XLA Modules:
  0.0 68.3 jit_solution(7711521740913369701)
XLA Ops:
  0.0 0.0 copy-start.1
  0.0 1.2 %fusion = (f32[8,8192]{1,0:T(8,128)S(1)}, f32[8,8192]{1,0:T(8,128)S(1)}) fusion(f32[8,16384]{1,0:T(8,128)} %own.1), kind=kLoop, calls=%fused_computation | loop fusion | bytes 1048576 | tf_op jit(solution)/shard_map/slice | solution.py:276
  1.2 2.5 %collective-permute-start = (f32[8,8192]{1,0:T(8,128)S(1)}, f32[8,8192]{1,0:T(8,128)S(1)}, u32[]{:S(2)}, u32[]{:S(2)}) collective-permute-start(f32[8,8192]{1,0:T(8,128)S(1)} %get-tuple-element.40), channel_id=1, source_target_pairs={{0,32},{32,64},{64,96},{96,128},{128,160},{160,192},{192,224},{224... | collective-permute-start | bytes 786440 | tf_op jit(solution)/shard_map/ppermute | solution.py:284
  3.7 4.0 %collective-permute-start.4 = (f32[8,8192]{1,0:T(8,128)S(1)}, f32[8,8192]{1,0:T(8,128)S(1)}, u32[]{:S(2)}, u32[]{:S(2)}) collective-permute-start(f32[8,8192]{1,0:T(8,128)S(1)} %get-tuple-element.39), channel_id=1, source_target_pairs={{0,224},{32,0},{64,32},{96,64},{128,96},{160,128},{192,160},{224,1... | collective-permute-start | bytes 786440 | tf_op jit(solution)/shard_map/ppermute | solution.py:285
  7.7 0.0 collective-permute-start.8
  7.7 2.7 %collective-permute-start.9 = (f32[8,8192]{1,0:T(8,128)S(1)}, f32[8,8192]{1,0:T(8,128)S(1)}, u32[]{:S(2)}, u32[]{:S(2)}) collective-permute-start(f32[8,8192]{1,0:T(8,128)S(1)} %get-tuple-element.40), channel_id=1, source_target_pairs={{0,224},{32,0},{64,32},{96,64},{128,96},{160,128},{192,160},{224,1... | collective-permute-start | bytes 786440 | tf_op jit(solution)/shard_map/ppermute | solution.py:285
  10.4 0.0 copy-start.3
  10.4 0.7 %copy-done.3 = s32[2,2048]{1,0:T(2,128)S(1)} copy-done((s32[2,2048]{1,0:T(2,128)S(1)}, s32[2,2048]{1,0:T(2,128)}, u32[]{:S(2)}) %copy-start.3) | copy-done | bytes 16408
  11.1 0.0 copy-start.4
  11.1 0.7 %copy-done.4 = f32[2,2048]{1,0:T(2,128)S(1)} copy-done((f32[2,2048]{1,0:T(2,128)S(1)}, f32[2,2048]{1,0:T(2,128)}, u32[]{:S(2)}) %copy-start.4) | copy-done | bytes 16408
  11.8 0.0 copy-start.5
  11.8 0.7 copy-done.5
  12.5 1.4 %fields.1 = (f32[128,128]{1,0:T(8,128)S(1)}, f32[128,128]{1,0:T(8,128)S(1)}) custom-call(s32[2,2048]{1,0:T(2,128)S(1)} %copy-done.3, f32[2,2048]{1,0:T(2,128)S(1)} %copy-done.4, s32[2,128]{1,0:T(2,128)S(1)} %copy-done.5), custom_call_target="tpu_custom_call" | custom-call | flops 1000000000 | bytes 4000000 | tf_op jit(solution)/shard_map/fields/pallas_call | solution.py:91
  13.9 0.0 collective-permute-done.refs_0_
  13.9 0.1 collective-permute-start.1
  14.0 0.0 collective-permute-done.4.refs_3_
  14.0 2.7 %collective-permute-start.5 = (f32[8,8192]{1,0:T(8,128)S(1)}, f32[8,8192]{1,0:T(8,128)S(1)}, u32[]{:S(2)}, u32[]{:S(2)}) collective-permute-start(f32[8,8192]{1,0:T(8,128)S(1)} %collective-permute-done.4.refs_3_), channel_id=1, source_target_pairs={{0,224},{32,0},{64,32},{96,64},{128,96},{160,128},{192,160},{224,1... | collective-permute-start | bytes 786440 | tf_op jit(solution)/shard_map/ppermute | solution.py:285
  16.7 2.6 %collective-permute-done.8.refs_1_ = f32[8,8192]{1,0:T(8,128)S(1)} collective-permute-done((f32[8,8192]{1,0:T(8,128)S(1)}, f32[8,8192]{1,0:T(8,128)S(1)}, u32[]{:S(2)}, u32[]{:S(2)}) %collective-permute-start.8) | collective-permute-done | bytes 262176 | tf_op jit(solution)/shard_map/ppermute | solution.py:284
  19.3 0.0 collective-permute-start.10
  19.3 0.0 collective-permute-done.9.refs_2_
  19.3 2.7 %collective-permute-start.11 = (f32[8,8192]{1,0:T(8,128)S(1)}, f32[8,8192]{1,0:T(8,128)S(1)}, u32[]{:S(2)}, u32[]{:S(2)}) collective-permute-start(f32[8,8192]{1,0:T(8,128)S(1)} %collective-permute-done.9.refs_2_), channel_id=1, source_target_pairs={{0,224},{32,0},{64,32},{96,64},{128,96},{160,128},{192,160},{224,1... | collective-permute-start | bytes 786440 | tf_op jit(solution)/shard_map/ppermute | solution.py:285
  22.0 2.9 %collective-permute-done.1.refs_4_ = f32[8,8192]{1,0:T(8,128)S(1)} collective-permute-done((f32[8,8192]{1,0:T(8,128)S(1)}, f32[8,8192]{1,0:T(8,128)S(1)}, u32[]{:S(2)}, u32[]{:S(2)}) %collective-permute-start.1) | collective-permute-done | bytes 262176 | tf_op jit(solution)/shard_map/ppermute | solution.py:284
  24.9 0.0 collective-permute-start.2
  24.9 0.0 collective-permute-done.5.refs_7_
  24.9 2.7 %collective-permute-start.6 = (f32[8,8192]{1,0:T(8,128)S(1)}, f32[8,8192]{1,0:T(8,128)S(1)}, u32[]{:S(2)}, u32[]{:S(2)}) collective-permute-start(f32[8,8192]{1,0:T(8,128)S(1)} %collective-permute-done.5.refs_7_), channel_id=1, source_target_pairs={{0,224},{32,0},{64,32},{96,64},{128,96},{160,128},{192,160},{224,1... | collective-permute-start | bytes 786440 | tf_op jit(solution)/shard_map/ppermute | solution.py:285
  27.6 2.9 %collective-permute-done.10.refs_5_ = f32[8,8192]{1,0:T(8,128)S(1)} collective-permute-done((f32[8,8192]{1,0:T(8,128)S(1)}, f32[8,8192]{1,0:T(8,128)S(1)}, u32[]{:S(2)}, u32[]{:S(2)}) %collective-permute-start.10) | collective-permute-done | bytes 262176 | tf_op jit(solution)/shard_map/ppermute | solution.py:284
  30.5 0.0 collective-permute-start.12
  30.5 0.0 collective-permute-done.11.refs_6_
  30.5 2.7 %collective-permute-start.13 = (f32[8,8192]{1,0:T(8,128)S(1)}, f32[8,8192]{1,0:T(8,128)S(1)}, u32[]{:S(2)}, u32[]{:S(2)}) collective-permute-start(f32[8,8192]{1,0:T(8,128)S(1)} %collective-permute-done.11.refs_6_), channel_id=1, source_target_pairs={{0,224},{32,0},{64,32},{96,64},{128,96},{160,128},{192,160},{224,1... | collective-permute-start | bytes 786440 | tf_op jit(solution)/shard_map/ppermute | solution.py:285
  33.2 2.9 %collective-permute-done.2.refs_8_ = f32[8,8192]{1,0:T(8,128)S(1)} collective-permute-done((f32[8,8192]{1,0:T(8,128)S(1)}, f32[8,8192]{1,0:T(8,128)S(1)}, u32[]{:S(2)}, u32[]{:S(2)}) %collective-permute-start.2) | collective-permute-done | bytes 262176 | tf_op jit(solution)/shard_map/ppermute | solution.py:284
  36.1 0.0 collective-permute-done.6.refs_11_
  36.1 2.4 %collective-permute-start.7 = (f32[8,8192]{1,0:T(8,128)S(1)}, f32[8,8192]{1,0:T(8,128)S(1)}, u32[]{:S(2)}, u32[]{:S(2)}) collective-permute-start(f32[8,8192]{1,0:T(8,128)S(1)} %collective-permute-done.6.refs_11_), channel_id=1, source_target_pairs={{0,224},{32,0},{64,32},{96,64},{128,96},{160,128},{192,160},{224,1... | collective-permute-start | bytes 786440 | tf_op jit(solution)/shard_map/ppermute | solution.py:289
  38.6 0.0 collective-permute-start.3
  38.6 3.2 %collective-permute-done.12.refs_9_ = f32[8,8192]{1,0:T(8,128)S(1)} collective-permute-done((f32[8,8192]{1,0:T(8,128)S(1)}, f32[8,8192]{1,0:T(8,128)S(1)}, u32[]{:S(2)}, u32[]{:S(2)}) %collective-permute-start.12) | collective-permute-done | bytes 262176 | tf_op jit(solution)/shard_map/ppermute | solution.py:284
  41.8 0.0 collective-permute-done.13.refs_10_
  41.8 0.0 copy-done.1
  41.8 0.0 copy-start
  41.8 1.0 %copy-done = f32[8,16384]{1,0:T(8,128)S(1)} copy-done((f32[8,16384]{1,0:T(8,128)S(1)}, f32[8,16384]{1,0:T(8,128)}, u32[]{:S(2)}) %copy-start) | copy-done | bytes 524312
  42.8 0.0 copy-start.2
  42.8 1.0 %copy-done.2 = f32[8,16384]{1,0:T(8,128)S(1)} copy-done((f32[8,16384]{1,0:T(8,128)S(1)}, f32[8,16384]{1,0:T(8,128)}, u32[]{:S(2)}) %copy-start.2) | copy-done | bytes 524312
  43.9 2.2 %early.1 = (f32[32,128]{1,0:T(8,128)S(1)}, bf16[160,16384]{1,0:T(8,128)(2,1)S(1)}, f32[8,16384]{1,0:T(8,128)S(1)}, f32[8,16384]{1,0:T(8,128)S(1)}) custom-call(f32[8,16384]{1,0:T(8,128)S(1)} %copy-done, f32[8,8192]{1,0:T(8,128)S(1)} %collective-permute-done.refs_0_, f32[8,8192]{1,0:T(8,128)S(1)} %collective-permute-done.8.refs_1_, ...), custom_call_target="tpu_custom_call" | custom-call | flops 1000000000 | bytes 4000000 | tf_op jit(solution)/shard_map/early/pallas_call | solution.py:91
  46.0 0.4 collective-permute-done.7.refs_1_
  46.4 0.0 collective-permute-done.3.refs_0_
  46.4 1.7 %last.1 = (f32[32,128]{1,0:T(8,128)S(1)}, bf16[160,16384]{1,0:T(8,128)(2,1)S(1)}) custom-call(f32[8,8192]{1,0:T(8,128)S(1)} %collective-permute-done.3.refs_0_, f32[8,8192]{1,0:T(8,128)S(1)} %collective-permute-done.7.refs_1_, f32[32,128]{1,0:T(8,128)S(1)} %get-tuple-element.33.refs_2_, ...), custom_call_target="tpu_custom_call", output_to_operand_aliasing={{1}: (3, {})} | custom-call | flops 1000000000 | bytes 4000000 | tf_op jit(solution)/shard_map/last/pallas_call | solution.py:91
  48.1 2.8 %collective-permute-start.14 = (f32[32,128]{1,0:T(8,128)S(1)}, f32[32,128]{1,0:T(8,128)S(1)}, u32[]{:S(2)}, u32[]{:S(2)}) collective-permute-start(f32[32,128]{1,0:T(8,128)S(1)} %get-tuple-element.35), channel_id=1, source_target_pairs={{0,1},{1,0},{2,3},{3,2},{4,5},{5,4},{6,7},{7,6},{8,9},{9,8},{10,11... | collective-permute-start | bytes 49160 | tf_op jit(solution)/shard_map/ppermute | solution.py:265
  50.9 0.8 %collective-permute-done.14 = f32[32,128]{1,0:T(8,128)S(1)} collective-permute-done((f32[32,128]{1,0:T(8,128)S(1)}, f32[32,128]{1,0:T(8,128)S(1)}, u32[]{:S(2)}, u32[]{:S(2)}) %collective-permute-start.14) | collective-permute-done | bytes 16416 | tf_op jit(solution)/shard_map/ppermute | solution.py:265
  51.8 14.1 %all_to_all.5.refs_0_ = f32[16,32,128]{2,1,0:T(8,128)S(1)} all-to-all(f32[16,32,128]{2,1,0:T(8,128)S(1)} %broadcast_in_dim.2), channel_id=1, replica_groups=mesh['member'=8,'x'=4,'y'=4,'core'=2] {'x','y'}, dimensions={0} | all-to-all | bytes 524288 | tf_op jit(solution)/shard_map/all_to_all | solution.py:267
  65.9 2.2 %final.1 = f32[8,16384]{1,0:T(8,128)} custom-call(f32[16,32,128]{2,1,0:T(8,128)S(1)} %all_to_all.5.refs_0_, bf16[160,16384]{1,0:T(8,128)(2,1)S(1)} %get-tuple-element.36.refs_1_, f32[8,16384]{1,0:T(8,128)S(1)} %get-tuple-element.37.refs_2_, f32[8,16384]{1,0:T(8,128)S(1)} %get-tuple-element.38.refs_3_), custom_call_target="tpu_custom_call" | custom-call | flops 1000000000 | bytes 4000000 | tf_op jit(solution)/shard_map/final/pallas_call | solution.py:91
  (2 shorter events, 0.0 us)
Async XLA Ops:
  0.0 41.8 %copy-start.1 = (f32[2,8,16384]{2,1,0:T(8,128)S(1)}, f32[2,8,16384]{2,1,0:T(8,128)}, u32[]{:S(2)}) copy-start(f32[2,8,16384]{2,1,0:T(8,128)} %refs_13_.1) | copy-start | bytes 3145732
  1.2 12.8 %collective-permute-start = (f32[8,8192]{1,0:T(8,128)S(1)}, f32[8,8192]{1,0:T(8,128)S(1)}, u32[]{:S(2)}, u32[]{:S(2)}) collective-permute-start(f32[8,8192]{1,0:T(8,128)S(1)} %get-tuple-element.40), channel_id=1, source_target_pairs={{0,32},{32,64},{64,96},{96,128},{128,160},{160,192},{192,224},{224... | collective-permute-start | bytes 786440 | tf_op jit(solution)/shard_map/ppermute | solution.py:284
  3.7 10.3 %collective-permute-start.4 = (f32[8,8192]{1,0:T(8,128)S(1)}, f32[8,8192]{1,0:T(8,128)S(1)}, u32[]{:S(2)}, u32[]{:S(2)}) collective-permute-start(f32[8,8192]{1,0:T(8,128)S(1)} %get-tuple-element.39), channel_id=1, source_target_pairs={{0,224},{32,0},{64,32},{96,64},{128,96},{160,128},{192,160},{224,1... | collective-permute-start | bytes 786440 | tf_op jit(solution)/shard_map/ppermute | solution.py:285
  7.7 11.6 %collective-permute-start.8 = (f32[8,8192]{1,0:T(8,128)S(1)}, f32[8,8192]{1,0:T(8,128)S(1)}, u32[]{:S(2)}, u32[]{:S(2)}) collective-permute-start(f32[8,8192]{1,0:T(8,128)S(1)} %get-tuple-element.39), channel_id=1, source_target_pairs={{0,32},{32,64},{64,96},{96,128},{128,160},{160,192},{192,224},{224... | collective-permute-start | bytes 786440 | tf_op jit(solution)/shard_map/ppermute | solution.py:284
  7.7 11.6 %collective-permute-start.9 = (f32[8,8192]{1,0:T(8,128)S(1)}, f32[8,8192]{1,0:T(8,128)S(1)}, u32[]{:S(2)}, u32[]{:S(2)}) collective-permute-start(f32[8,8192]{1,0:T(8,128)S(1)} %get-tuple-element.40), channel_id=1, source_target_pairs={{0,224},{32,0},{64,32},{96,64},{128,96},{160,128},{192,160},{224,1... | collective-permute-start | bytes 786440 | tf_op jit(solution)/shard_map/ppermute | solution.py:285
  10.4 0.7 %copy-start.3 = (s32[2,2048]{1,0:T(2,128)S(1)}, s32[2,2048]{1,0:T(2,128)}, u32[]{:S(2)}) copy-start(s32[2,2048]{1,0:T(2,128)} %cells.1) | copy-start | bytes 49156
  11.1 0.7 %copy-start.4 = (f32[2,2048]{1,0:T(2,128)S(1)}, f32[2,2048]{1,0:T(2,128)}, u32[]{:S(2)}) copy-start(f32[2,2048]{1,0:T(2,128)} %vals.1) | copy-start | bytes 49156
  11.8 0.7 copy-start.5
  13.9 11.0 %collective-permute-start.1 = (f32[8,8192]{1,0:T(8,128)S(1)}, f32[8,8192]{1,0:T(8,128)S(1)}, u32[]{:S(2)}, u32[]{:S(2)}) collective-permute-start(f32[8,8192]{1,0:T(8,128)S(1)} %collective-permute-done.refs_0_), channel_id=1, source_target_pairs={{0,32},{32,64},{64,96},{96,128},{128,160},{160,192},{192,224},{224... | collective-permute-start | bytes 786440 | tf_op jit(solution)/shard_map/ppermute | solution.py:284
  14.0 10.9 %collective-permute-start.5 = (f32[8,8192]{1,0:T(8,128)S(1)}, f32[8,8192]{1,0:T(8,128)S(1)}, u32[]{:S(2)}, u32[]{:S(2)}) collective-permute-start(f32[8,8192]{1,0:T(8,128)S(1)} %collective-permute-done.4.refs_3_), channel_id=1, source_target_pairs={{0,224},{32,0},{64,32},{96,64},{128,96},{160,128},{192,160},{224,1... | collective-permute-start | bytes 786440 | tf_op jit(solution)/shard_map/ppermute | solution.py:285
  19.3 11.2 %collective-permute-start.10 = (f32[8,8192]{1,0:T(8,128)S(1)}, f32[8,8192]{1,0:T(8,128)S(1)}, u32[]{:S(2)}, u32[]{:S(2)}) collective-permute-start(f32[8,8192]{1,0:T(8,128)S(1)} %collective-permute-done.8.refs_1_), channel_id=1, source_target_pairs={{0,32},{32,64},{64,96},{96,128},{128,160},{160,192},{192,224},{224... | collective-permute-start | bytes 786440 | tf_op jit(solution)/shard_map/ppermute | solution.py:284
  19.3 11.2 %collective-permute-start.11 = (f32[8,8192]{1,0:T(8,128)S(1)}, f32[8,8192]{1,0:T(8,128)S(1)}, u32[]{:S(2)}, u32[]{:S(2)}) collective-permute-start(f32[8,8192]{1,0:T(8,128)S(1)} %collective-permute-done.9.refs_2_), channel_id=1, source_target_pairs={{0,224},{32,0},{64,32},{96,64},{128,96},{160,128},{192,160},{224,1... | collective-permute-start | bytes 786440 | tf_op jit(solution)/shard_map/ppermute | solution.py:285
  24.9 11.2 %collective-permute-start.2 = (f32[8,8192]{1,0:T(8,128)S(1)}, f32[8,8192]{1,0:T(8,128)S(1)}, u32[]{:S(2)}, u32[]{:S(2)}) collective-permute-start(f32[8,8192]{1,0:T(8,128)S(1)} %collective-permute-done.1.refs_4_), channel_id=1, source_target_pairs={{0,32},{32,64},{64,96},{96,128},{128,160},{160,192},{192,224},{224... | collective-permute-start | bytes 786440 | tf_op jit(solution)/shard_map/ppermute | solution.py:284
  24.9 11.2 %collective-permute-start.6 = (f32[8,8192]{1,0:T(8,128)S(1)}, f32[8,8192]{1,0:T(8,128)S(1)}, u32[]{:S(2)}, u32[]{:S(2)}) collective-permute-start(f32[8,8192]{1,0:T(8,128)S(1)} %collective-permute-done.5.refs_7_), channel_id=1, source_target_pairs={{0,224},{32,0},{64,32},{96,64},{128,96},{160,128},{192,160},{224,1... | collective-permute-start | bytes 786440 | tf_op jit(solution)/shard_map/ppermute | solution.py:285
  30.5 11.2 %collective-permute-start.12 = (f32[8,8192]{1,0:T(8,128)S(1)}, f32[8,8192]{1,0:T(8,128)S(1)}, u32[]{:S(2)}, u32[]{:S(2)}) collective-permute-start(f32[8,8192]{1,0:T(8,128)S(1)} %collective-permute-done.10.refs_5_), channel_id=1, source_target_pairs={{0,32},{32,64},{64,96},{96,128},{128,160},{160,192},{192,224},{224... | collective-permute-start | bytes 786440 | tf_op jit(solution)/shard_map/ppermute | solution.py:284
  30.5 11.2 %collective-permute-start.13 = (f32[8,8192]{1,0:T(8,128)S(1)}, f32[8,8192]{1,0:T(8,128)S(1)}, u32[]{:S(2)}, u32[]{:S(2)}) collective-permute-start(f32[8,8192]{1,0:T(8,128)S(1)} %collective-permute-done.11.refs_6_), channel_id=1, source_target_pairs={{0,224},{32,0},{64,32},{96,64},{128,96},{160,128},{192,160},{224,1... | collective-permute-start | bytes 786440 | tf_op jit(solution)/shard_map/ppermute | solution.py:285
  36.1 10.3 %collective-permute-start.7 = (f32[8,8192]{1,0:T(8,128)S(1)}, f32[8,8192]{1,0:T(8,128)S(1)}, u32[]{:S(2)}, u32[]{:S(2)}) collective-permute-start(f32[8,8192]{1,0:T(8,128)S(1)} %collective-permute-done.6.refs_11_), channel_id=1, source_target_pairs={{0,224},{32,0},{64,32},{96,64},{128,96},{160,128},{192,160},{224,1... | collective-permute-start | bytes 786440 | tf_op jit(solution)/shard_map/ppermute | solution.py:289
  38.6 7.8 %collective-permute-start.3 = (f32[8,8192]{1,0:T(8,128)S(1)}, f32[8,8192]{1,0:T(8,128)S(1)}, u32[]{:S(2)}, u32[]{:S(2)}) collective-permute-start(f32[8,8192]{1,0:T(8,128)S(1)} %collective-permute-done.2.refs_8_), channel_id=1, source_target_pairs={{0,32},{32,64},{64,96},{96,128},{128,160},{160,192},{192,224},{224... | collective-permute-start | bytes 786440 | tf_op jit(solution)/shard_map/ppermute | solution.py:289
  41.8 1.0 %copy-start = (f32[8,16384]{1,0:T(8,128)S(1)}, f32[8,16384]{1,0:T(8,128)}, u32[]{:S(2)}) copy-start(f32[8,16384]{1,0:T(8,128)} %own.1) | copy-start | bytes 1572868
  42.8 1.0 %copy-start.2 = (f32[8,16384]{1,0:T(8,128)S(1)}, f32[8,16384]{1,0:T(8,128)}, u32[]{:S(2)}) copy-start(f32[8,16384]{1,0:T(8,128)} %refs_12_.1) | copy-start | bytes 1572868
  48.1 3.7 %collective-permute-start.14 = (f32[32,128]{1,0:T(8,128)S(1)}, f32[32,128]{1,0:T(8,128)S(1)}, u32[]{:S(2)}, u32[]{:S(2)}) collective-permute-start(f32[32,128]{1,0:T(8,128)S(1)} %get-tuple-element.35), channel_id=1, source_target_pairs={{0,1},{1,0},{2,3},{3,2},{4,5},{5,4},{6,7},{7,6},{8,9},{9,8},{10,11... | collective-permute-start | bytes 49160 | tf_op jit(solution)/shard_map/ppermute | solution.py:265

commit v6 on v5

--- a/solution.py
+++ b/solution.py
@@ -82,6 +82,25 @@
     lax.fori_loop(0, prec.shape[0], step, 0, unroll=8)
 
 
+def local_kernel(samples, noise, prec, targ, u, base, ab):
+    k0, k1 = constants(0), constants(1)
+
+    def local(where, p, t):
+        a1 = k1["gain"] - k1["pull"] * p
+        x = (k0["gain"] - k0["pull"] * p) * samples[:, where]
+        x = x + k0["pull"] * t + k0["kick"] * noise[0, :, where]
+        u[:, where] = x
+        base[:, where] = a1 * x + k1["pull"] * t + k1["kick"] * noise[1, :, where]
+        ab[:, where] = jnp.broadcast_to(k0["lift"] * a1, x.shape)
+
+    per_row(prec, targ, local)
+
+
+def local_terms(*args):
+    shape = jax.ShapeDtypeStruct(args[0].shape, F32)
+    return call(local_kernel, (shape, shape, shape), args, 10**9, name="local")
+
+
 CHUNK = 4096
 LIMIT = pltpu.CompilerParams(vmem_limit_bytes=16 << 20)
 
@@ -127,18 +146,7 @@
 
 
 def early_kernel(own, *refs):
-    blocks, samples, noise, prec, targ, z, stack, base, ab, u = refs[:-9], *refs[-9:]
-    k0, k1 = constants(0), constants(1)
-
-    def local(where, p, t):
-        a1 = k1["gain"] - k1["pull"] * p
-        x = (k0["gain"] - k0["pull"] * p) * samples[:, where]
-        x = x + k0["pull"] * t + k0["kick"] * noise[0, :, where]
-        u[:, where] = x
-        base[:, where] = a1 * x + k1["pull"] * t + k1["kick"] * noise[1, :, where]
-        ab[:, where] = jnp.broadcast_to(k0["lift"] * a1, x.shape)
-
-    per_row(prec, targ, local)
+    blocks, samples, u, z, stack = refs[:-4], *refs[-4:]
     blocks = [blocks[i : i + 2] for i in range(0, len(blocks), 2)]
     blocks = [halves(own), *blocks, halves(samples), halves(u)]
 
@@ -158,30 +166,31 @@
     z[2 * ROWS :, 3 * q : 2 * q + near] = acc[near:, q:near]
 
 
-def early(samples, noise, prec, targ, own, blocks):
+def early(samples, u, own, blocks):
     rows = ROWS * (3 + len(blocks) // 2)
     shapes = (
         jax.ShapeDtypeStruct((ROWS * RINGS // 2, 2 * ROWS * RINGS), F32),
         jax.ShapeDtypeStruct((2 * (rows + ROWS), own.shape[1]), BF),
-        jax.ShapeDtypeStruct(own.shape, F32),
-        jax.ShapeDtypeStruct(own.shape, F32),
-    )
-    args = (own, *blocks, samples, noise, prec, targ)
-    return call(
-        early_kernel, shapes, args, 10**9, [pltpu.VMEM(own.shape, F32)], name="early"
-    )
-
-
-def last_kernel(*refs):
-    far, z1, _, z, stack = refs[:-4], *refs[-4:]
+    )
+    return call(early_kernel, shapes, (own, *blocks, samples, u), 10**9, name="early")
+
+
+def far_products(pieces, places, stack, acc):
+    for piece, start in zip(pieces, places, strict=True):
+        where = slice(start, start + piece.shape[1])
+        y = split2(piece[...])
+        stack[stack.shape[0] - 2 * ROWS :, where] = y
+        acc = acc + lax.dot_general(y, stack[:, where], NT, preferred_element_type=F32)
+    return acc
+
+
+def far_kernel(places, first, second, _, acc, stack):
+    acc[...] = far_products((first, second), places, stack, jnp.zeros(acc.shape, F32))
+
+
+def last_kernel(places, first, second, acc, z1, _, z, stack):
     new, old = ROWS, stack.shape[0] // 2 - ROWS
-
-    def body(where, x, acc):
-        y = split2(x)
-        stack[2 * old :, where] = y
-        return acc + lax.dot_general(y, stack[:, where], NT, preferred_element_type=F32)
-
-    acc = column_chunks([far], body, jnp.zeros((2 * new, 2 * (old + new)), F32))
+    acc = far_products((first, second), places, stack, acc[...])
     left, right = fold(acc[:, : 2 * old], new, old), fold(acc[:, 2 * old :], new, new)
     near, q = old - 2 * ROWS, z.shape[0]
     column = left.T
@@ -193,11 +202,23 @@
     z[2 * ROWS :, 2 * q + near :] = column[near:]
 
 
+def in_place(kernel, places, shape, args, name):
+    shapes = (shape, jax.ShapeDtypeStruct(args[-1].shape, BF))
+
+    def body(*refs):
+        kernel(places, *refs)
+
+    alias = {len(args) - 1: 1}
+    return call(body, shapes, args, 10**9, input_output_aliases=alias, name=name)
+
+
 def last(far, z1, stack):
-    shapes = (jax.ShapeDtypeStruct(z1.shape, F32), jax.ShapeDtypeStruct(stack.shape, BF))
-    args = (*far, z1, stack)
-    places = {len(args) - 1: 1}
-    return call(last_kernel, shapes, args, 10**9, input_output_aliases=places, name="last")
+    quarter = far[0].shape[1]
+    acc = jax.ShapeDtypeStruct((2 * ROWS, stack.shape[0]), F32)
+    acc, stack = in_place(far_kernel, (0, 2 * quarter), acc, (far[0], far[2], stack), "far")
+    z = jax.ShapeDtypeStruct(z1.shape, F32)
+    args = (far[1], far[3], acc, z1, stack)
+    return in_place(last_kernel, (quarter, 3 * quarter), z, args, "last")
 
 
 def exponentials(x):
@@ -278,15 +299,23 @@
     blocks = []
     prec, targ = fields(obs_cells, obs_values, seismic_mask)
     for hop in range(3):
-        if hop > 0:
+        if hop == 1:
             rising[0], prec, targ = lax.optimization_barrier((rising[0], prec, targ))
+            u, base, ab = local_terms(samples, noise, prec, targ)
+        if hop == 2:
+            rising[0], u, base, ab = lax.optimization_barrier((rising[0], u, base, ab))
         for c in range(2):
             rising[c] = lax.ppermute(rising[c], "member", up)
             falling[c] = lax.ppermute(falling[c], "member", down)
         blocks += [*rising, *falling]
-    rising[0], prec, targ = lax.optimization_barrier((rising[0], prec, targ))
-    z1, stack, base, ab = early(samples, noise, prec, targ, prior, blocks)
-    far = [lax.ppermute(rising[0], "member", up), lax.ppermute(falling[1], "member", down)]
+    z1, stack = early(samples, u, prior, blocks)
+    quarter = half // 2
+    rising[0], falling[1] = lax.optimization_barrier((rising[0], falling[1]))
+    far = [
+        lax.ppermute(x[:, i * quarter : (i + 1) * quarter], "member", way)
+        for x, way in ((rising[0], up), (falling[1], down))
+        for i in range(2)
+    ]
     z, stack = last(far, z1, stack)
     z = total(z)
     return final(ncell, z, stack, base, ab)

time: 68.7 us -> 69.9 us (1.017)
  starting transfers between devices: 25.3 us -> 31.9 us
  waiting for transfers between devices: 15.8 us -> 10.1 us
    ppermute x6, waiting for transfers between devices: 14.6 us -> 6.89 us  [per_device(): rising[c] = lax.ppermute(rising[c], 'member', up)]
    ppermute x2 -> x4, starting transfers between devices: 2.44 us -> 6.6 us  [per_device(): lax.ppermute(x[:, i * quarter:(i + 1) * quarter], 'member', way)]
    ppermute x1, starting transfers between devices: 2.82 us -> 5.51 us  [total(): x = x + lax.ppermute(x, 'core', [(0, 1), (1, 0)])]
    ppermute x6, waiting for transfers between devices: 0.02 us -> 1.98 us  [per_device(): falling[c] = lax.ppermute(falling[c], 'member', down)]
    unnamed x12 -> x14, local copies, waits for them, and re-layouts: 4.2 us -> 4.38 us
    pallas_call x4 -> x6, Pallas kernels: 7.5 us -> 7.55 us  [call(): pl.pallas_call(kernel, out_shape=out_shape, in_specs=[pl.BlockSpec(memory...]
  transfers between devices with their start and end apart: 15 -> 17, of which waited for: 7 -> 7; matrix products, arithmetic and copies ran while one was open for 0% -> 0% of each run, Pallas kernels for 5% -> 6%
where the time goes in v6:
time: 69.9 us; the launch traced here: 69.6 us
  starting transfers between devices  31.9 us (46%)
  blocking collectives  14.1 us (20%)
  waiting for transfers between devices  10.1 us (14%)
  Pallas kernels  7.55 us (11%)
  local copies, waits for them, and re-layouts  5.6 us (8%)
    ppermute x6, starting transfers between devices, per_device(): falling[c] = lax.ppermute(falling[c], 'member', down)  17.1 us
    all_to_all x1, blocking collectives, total(): lax.all_to_all(x, ('x', 'y'), split_axis=0, concat_axis=0, tiled=True)  14.1 us
    pallas_call x6, Pallas kernels, call(): pl.pallas_call(kernel, out_shape=out_shape, in_specs=[pl.BlockSpec(memory...  7.55 us
    ppermute x6, waiting for transfers between devices, per_device(): rising[c] = lax.ppermute(rising[c], 'member', up)  6.89 us
    ppermute x4, starting transfers between devices, per_device(): lax.ppermute(x[:, i * quarter:(i + 1) * quarter], 'member', way)  6.6 us
    ppermute x1, starting transfers between devices, total(): x = x + lax.ppermute(x, 'core', [(0, 1), (1, 0)])  5.51 us
    unnamed x14, local copies, waits for them, and re-layouts  4.38 us
    ppermute x6, starting transfers between devices, per_device(): rising[c] = lax.ppermute(rising[c], 'member', up)  2.64 us
  transfers between devices with their start and end apart: 17, of which 7 were waited for; matrix products, arithmetic and copies ran while one was open for 0% of the time, Pallas kernels for 6%

profile of v6, /device:TPU:1, one launch (start us, length us, event | category | flops | bytes accessed | tf_op | source)
XLA Modules:
  0.0 69.6 jit_solution(11695068725946565515)
XLA Ops:
  0.0 1.2 %fusion = (f32[8,8192]{1,0:T(8,128)S(1)}, f32[8,8192]{1,0:T(8,128)S(1)}) fusion(f32[8,16384]{1,0:T(8,128)} %own.1), kind=kLoop, calls=%fused_computation | loop fusion | bytes 1048576 | tf_op jit(solution)/shard_map/slice | solution.py:297
  1.2 2.5 %collective-permute-start = (f32[8,8192]{1,0:T(8,128)S(1)}, f32[8,8192]{1,0:T(8,128)S(1)}, u32[]{:S(2)}, u32[]{:S(2)}) collective-permute-start(f32[8,8192]{1,0:T(8,128)S(1)} %get-tuple-element.46), channel_id=1, source_target_pairs={{0,32},{32,64},{64,96},{96,128},{128,160},{160,192},{192,224},{224... | collective-permute-start | bytes 786440 | tf_op jit(solution)/shard_map/ppermute | solution.py:308
  3.7 4.0 %collective-permute-start.3 = (f32[8,8192]{1,0:T(8,128)S(1)}, f32[8,8192]{1,0:T(8,128)S(1)}, u32[]{:S(2)}, u32[]{:S(2)}) collective-permute-start(f32[8,8192]{1,0:T(8,128)S(1)} %get-tuple-element.45), channel_id=1, source_target_pairs={{0,224},{32,0},{64,32},{96,64},{128,96},{160,128},{192,160},{224,1... | collective-permute-start | bytes 786440 | tf_op jit(solution)/shard_map/ppermute | solution.py:309
  7.7 0.0 collective-permute-start.10
  7.7 2.7 %collective-permute-start.11 = (f32[8,8192]{1,0:T(8,128)S(1)}, f32[8,8192]{1,0:T(8,128)S(1)}, u32[]{:S(2)}, u32[]{:S(2)}) collective-permute-start(f32[8,8192]{1,0:T(8,128)S(1)} %get-tuple-element.46), channel_id=1, source_target_pairs={{0,224},{32,0},{64,32},{96,64},{128,96},{160,128},{192,160},{224,1... | collective-permute-start | bytes 786440 | tf_op jit(solution)/shard_map/ppermute | solution.py:309
  10.4 0.7 %copy-done.4 = s32[2,2048]{1,0:T(2,128)S(1)} copy-done((s32[2,2048]{1,0:T(2,128)S(1)}, s32[2,2048]{1,0:T(2,128)}, u32[]{:S(2)}) %copy-start.4) | copy-done | bytes 16408
  11.1 0.7 %copy-done.5 = f32[2,2048]{1,0:T(2,128)S(1)} copy-done((f32[2,2048]{1,0:T(2,128)S(1)}, f32[2,2048]{1,0:T(2,128)}, u32[]{:S(2)}) %copy-start.5) | copy-done | bytes 16408
  11.8 0.7 copy-done.6
  12.5 1.4 %fields.1 = (f32[128,128]{1,0:T(8,128)S(1)}, f32[128,128]{1,0:T(8,128)S(1)}) custom-call(s32[2,2048]{1,0:T(2,128)S(1)} %copy-done.4, f32[2,2048]{1,0:T(2,128)S(1)} %copy-done.5, s32[2,128]{1,0:T(2,128)S(1)} %copy-done.6), custom_call_target="tpu_custom_call" | custom-call | flops 1000000000 | bytes 4000000 | tf_op jit(solution)/shard_map/fields/pallas_call | solution.py:110
  13.9 0.0 collective-permute-done.refs_0_
  13.9 0.1 collective-permute-start.1
  14.0 0.0 collective-permute-done.3.refs_3_
  14.0 2.7 %collective-permute-start.4 = (f32[8,8192]{1,0:T(8,128)S(1)}, f32[8,8192]{1,0:T(8,128)S(1)}, u32[]{:S(2)}, u32[]{:S(2)}) collective-permute-start(f32[8,8192]{1,0:T(8,128)S(1)} %collective-permute-done.3.refs_3_), channel_id=1, source_target_pairs={{0,224},{32,0},{64,32},{96,64},{128,96},{160,128},{192,160},{224,1... | collective-permute-start | bytes 786440 | tf_op jit(solution)/shard_map/ppermute | solution.py:309
  16.7 2.6 %collective-permute-done.10.refs_1_ = f32[8,8192]{1,0:T(8,128)S(1)} collective-permute-done((f32[8,8192]{1,0:T(8,128)S(1)}, f32[8,8192]{1,0:T(8,128)S(1)}, u32[]{:S(2)}, u32[]{:S(2)}) %collective-permute-start.10) | collective-permute-done | bytes 262176 | tf_op jit(solution)/shard_map/ppermute | solution.py:308
  19.3 0.0 collective-permute-start.12
  19.3 0.0 collective-permute-done.11.refs_2_
  19.3 2.7 %collective-permute-start.13 = (f32[8,8192]{1,0:T(8,128)S(1)}, f32[8,8192]{1,0:T(8,128)S(1)}, u32[]{:S(2)}, u32[]{:S(2)}) collective-permute-start(f32[8,8192]{1,0:T(8,128)S(1)} %collective-permute-done.11.refs_2_), channel_id=1, source_target_pairs={{0,224},{32,0},{64,32},{96,64},{128,96},{160,128},{192,160},{224,1... | collective-permute-start | bytes 786440 | tf_op jit(solution)/shard_map/ppermute | solution.py:309
  22.0 1.0 %copy-done.1 = f32[8,16384]{1,0:T(8,128)S(1)} copy-done((f32[8,16384]{1,0:T(8,128)S(1)}, f32[8,16384]{1,0:T(8,128)}, u32[]{:S(2)}) %copy-start.1) | copy-done | bytes 524312
  23.0 1.2 %copy-done.3 = f32[2,8,16384]{2,1,0:T(8,128)S(1)} copy-done((f32[2,8,16384]{2,1,0:T(8,128)S(1)}, f32[2,8,16384]{2,1,0:T(8,128)}, u32[]{:S(2)}) %copy-start.3) | copy-done | bytes 1048600
  24.2 0.5 local.1
  24.8 0.1 collective-permute-done.1.refs_4_
  24.9 0.0 collective-permute-done.4.refs_7_
  24.9 2.4 %collective-permute-start.5 = (f32[8,8192]{1,0:T(8,128)S(1)}, f32[8,8192]{1,0:T(8,128)S(1)}, u32[]{:S(2)}, u32[]{:S(2)}) collective-permute-start(f32[8,8192]{1,0:T(8,128)S(1)} %collective-permute-done.4.refs_7_), channel_id=1, source_target_pairs={{0,224},{32,0},{64,32},{96,64},{128,96},{160,128},{192,160},{224,1... | collective-permute-start | bytes 786440 | tf_op jit(solution)/shard_map/ppermute | solution.py:309
  27.4 0.0 collective-permute-start.2
  27.4 3.2 %collective-permute-done.12.refs_5_ = f32[8,8192]{1,0:T(8,128)S(1)} collective-permute-done((f32[8,8192]{1,0:T(8,128)S(1)}, f32[8,8192]{1,0:T(8,128)S(1)}, u32[]{:S(2)}, u32[]{:S(2)}) %collective-permute-start.12) | collective-permute-done | bytes 262176 | tf_op jit(solution)/shard_map/ppermute | solution.py:308
  30.5 0.0 collective-permute-start.14
  30.5 0.0 collective-permute-done.13.refs_6_
  30.5 2.7 %collective-permute-start.15 = (f32[8,8192]{1,0:T(8,128)S(1)}, f32[8,8192]{1,0:T(8,128)S(1)}, u32[]{:S(2)}, u32[]{:S(2)}) collective-permute-start(f32[8,8192]{1,0:T(8,128)S(1)} %collective-permute-done.13.refs_6_), channel_id=1, source_target_pairs={{0,224},{32,0},{64,32},{96,64},{128,96},{160,128},{192,160},{224,1... | collective-permute-start | bytes 786440 | tf_op jit(solution)/shard_map/ppermute | solution.py:309
  33.2 2.0 %collective-permute-done.5.refs_11_ = f32[8,8192]{1,0:T(8,128)S(1)} collective-permute-done((f32[8,8192]{1,0:T(8,128)S(1)}, f32[8,8192]{1,0:T(8,128)S(1)}, u32[]{:S(2)}, u32[]{:S(2)}) %collective-permute-start.5) | collective-permute-done | bytes 262176 | tf_op jit(solution)/shard_map/ppermute | solution.py:309
  35.2 0.0 collective-permute-done.2.refs_8_
  35.2 0.1 collective-permute-start.8
  35.3 3.5 %collective-permute-start.9 = (f32[8,4096]{1,0:T(8,128)S(1)}, f32[8,4096]{1,0:T(8,128)S(1)}, u32[]{:S(2)}, u32[]{:S(2)}) collective-permute-start(f32[8,4096]{1,0:T(8,128)S(1)} %get-tuple-element.47), channel_id=1, source_target_pairs={{0,224},{32,0},{64,32},{96,64},{128,96},{160,128},{192,160},{224,1... | collective-permute-start | bytes 393224 | tf_op jit(solution)/shard_map/ppermute | solution.py:315
  38.8 0.0 collective-permute-start.6
  38.8 1.0 %collective-permute-done.14.refs_9_ = f32[8,8192]{1,0:T(8,128)S(1)} collective-permute-done((f32[8,8192]{1,0:T(8,128)S(1)}, f32[8,8192]{1,0:T(8,128)S(1)}, u32[]{:S(2)}, u32[]{:S(2)}) %collective-permute-start.14) | collective-permute-done | bytes 262176 | tf_op jit(solution)/shard_map/ppermute | solution.py:308
  39.8 3.0 %collective-permute-start.7 = (f32[8,4096]{1,0:T(8,128)S(1)}, f32[8,4096]{1,0:T(8,128)S(1)}, u32[]{:S(2)}, u32[]{:S(2)}) collective-permute-start(f32[8,4096]{1,0:T(8,128)S(1)} %get-tuple-element.48), channel_id=1, source_target_pairs={{0,224},{32,0},{64,32},{96,64},{128,96},{160,128},{192,160},{224,1... | collective-permute-start | bytes 393224 | tf_op jit(solution)/shard_map/ppermute | solution.py:315
  42.8 0.0 collective-permute-done.15.refs_10_
  42.8 0.0 copy-done
  42.8 1.6 %early.1 = (f32[32,128]{1,0:T(8,128)S(1)}, bf16[160,16384]{1,0:T(8,128)(2,1)S(1)}) custom-call(f32[8,16384]{1,0:T(8,128)S(1)} %copy-done, f32[8,8192]{1,0:T(8,128)S(1)} %collective-permute-done.refs_0_, f32[8,8192]{1,0:T(8,128)S(1)} %collective-permute-done.10.refs_1_, f32[8,8192]{1,0:T(8,128)S(1)} %collective-permute-done.11.refs_2_, ...), custom_call_target="tpu_custom_call" | custom-call | flops 1000000000 | bytes 4000000 | tf_op jit(solution)/shard_map/early/pallas_call | solution.py:110
  44.4 0.0 collective-permute-done.8.refs_0_
  44.4 0.0 collective-permute-done.9.refs_1_
  44.5 0.8 %far.1 = (f32[16,160]{1,0:T(8,128)S(1)}, bf16[160,16384]{1,0:T(8,128)(2,1)S(1)}) custom-call(f32[8,4096]{1,0:T(8,128)S(1)} %collective-permute-done.8.refs_0_, f32[8,4096]{1,0:T(8,128)S(1)} %collective-permute-done.9.refs_1_, bf16[160,16384]{1,0:T(8,128)(2,1)S(1)} %get-tuple-element.37.refs_2_), custom_call_target="tpu_custom_call", output_to_operand_aliasing={{1}: (2, {})} | custom-call | flops 1000000000 | bytes 4000000 | tf_op jit(solution)/shard_map/far/pallas_call | solution.py:110
  45.2 0.4 collective-permute-done.6.refs_0_
  45.6 0.0 collective-permute-done.7.refs_1_
  45.6 1.0 %last.1 = (f32[32,128]{1,0:T(8,128)S(1)}, bf16[160,16384]{1,0:T(8,128)(2,1)S(1)}) custom-call(f32[8,4096]{1,0:T(8,128)S(1)} %collective-permute-done.6.refs_0_, f32[8,4096]{1,0:T(8,128)S(1)} %collective-permute-done.7.refs_1_, f32[16,160]{1,0:T(8,128)S(1)} %get-tuple-element.38.refs_2_, ...), custom_call_target="tpu_custom_call", output_to_operand_aliasing={{1}: (4, {})} | custom-call | flops 1000000000 | bytes 4000000 | tf_op jit(solution)/shard_map/last/pallas_call | solution.py:110
  46.6 5.5 %collective-permute-start.16 = (f32[32,128]{1,0:T(8,128)S(1)}, f32[32,128]{1,0:T(8,128)S(1)}, u32[]{:S(2)}, u32[]{:S(2)}) collective-permute-start(f32[32,128]{1,0:T(8,128)S(1)} %get-tuple-element.41), channel_id=1, source_target_pairs={{0,1},{1,0},{2,3},{3,2},{4,5},{5,4},{6,7},{7,6},{8,9},{9,8},{10,11... | collective-permute-start | bytes 49160 | tf_op jit(solution)/shard_map/ppermute | solution.py:286
  52.1 0.8 %collective-permute-done.16 = f32[32,128]{1,0:T(8,128)S(1)} collective-permute-done((f32[32,128]{1,0:T(8,128)S(1)}, f32[32,128]{1,0:T(8,128)S(1)}, u32[]{:S(2)}, u32[]{:S(2)}) %collective-permute-start.16) | collective-permute-done | bytes 16416 | tf_op jit(solution)/shard_map/ppermute | solution.py:286
  53.0 14.1 %all_to_all.5.refs_0_ = f32[16,32,128]{2,1,0:T(8,128)S(1)} all-to-all(f32[16,32,128]{2,1,0:T(8,128)S(1)} %broadcast_in_dim.2), channel_id=1, replica_groups=mesh['member'=8,'x'=4,'y'=4,'core'=2] {'x','y'}, dimensions={0} | all-to-all | bytes 524288 | tf_op jit(solution)/shard_map/all_to_all | solution.py:288
  67.2 2.2 %final.1 = f32[8,16384]{1,0:T(8,128)} custom-call(f32[16,32,128]{2,1,0:T(8,128)S(1)} %all_to_all.5.refs_0_, bf16[160,16384]{1,0:T(8,128)(2,1)S(1)} %get-tuple-element.42.refs_1_, f32[8,16384]{1,0:T(8,128)S(1)} %get-tuple-element.43.refs_2_, f32[8,16384]{1,0:T(8,128)S(1)} %get-tuple-element.44.refs_3_), custom_call_target="tpu_custom_call" | custom-call | flops 1000000000 | bytes 4000000 | tf_op jit(solution)/shard_map/final/pallas_call | solution.py:110
  (12 shorter events, 0.1 us)
Async XLA Ops:
  0.0 42.8 %copy-start = (f32[8,16384]{1,0:T(8,128)S(1)}, f32[8,16384]{1,0:T(8,128)}, u32[]{:S(2)}) copy-start(f32[8,16384]{1,0:T(8,128)} %own.1) | copy-start | bytes 1572868
  0.0 42.8 %copy-start.2 = (f32[8,16384]{1,0:T(8,128)S(1)}, f32[8,16384]{1,0:T(8,128)}, u32[]{:S(2)}) copy-start(f32[8,16384]{1,0:T(8,128)} %refs_12_.1) | copy-start | bytes 1572868
  1.2 12.8 %collective-permute-start = (f32[8,8192]{1,0:T(8,128)S(1)}, f32[8,8192]{1,0:T(8,128)S(1)}, u32[]{:S(2)}, u32[]{:S(2)}) collective-permute-start(f32[8,8192]{1,0:T(8,128)S(1)} %get-tuple-element.46), channel_id=1, source_target_pairs={{0,32},{32,64},{64,96},{96,128},{128,160},{160,192},{192,224},{224... | collective-permute-start | bytes 786440 | tf_op jit(solution)/shard_map/ppermute | solution.py:308
  3.7 10.3 %collective-permute-start.3 = (f32[8,8192]{1,0:T(8,128)S(1)}, f32[8,8192]{1,0:T(8,128)S(1)}, u32[]{:S(2)}, u32[]{:S(2)}) collective-permute-start(f32[8,8192]{1,0:T(8,128)S(1)} %get-tuple-element.45), channel_id=1, source_target_pairs={{0,224},{32,0},{64,32},{96,64},{128,96},{160,128},{192,160},{224,1... | collective-permute-start | bytes 786440 | tf_op jit(solution)/shard_map/ppermute | solution.py:309
  7.7 11.6 %collective-permute-start.10 = (f32[8,8192]{1,0:T(8,128)S(1)}, f32[8,8192]{1,0:T(8,128)S(1)}, u32[]{:S(2)}, u32[]{:S(2)}) collective-permute-start(f32[8,8192]{1,0:T(8,128)S(1)} %get-tuple-element.45), channel_id=1, source_target_pairs={{0,32},{32,64},{64,96},{96,128},{128,160},{160,192},{192,224},{224... | collective-permute-start | bytes 786440 | tf_op jit(solution)/shard_map/ppermute | solution.py:308
  7.7 11.6 %collective-permute-start.11 = (f32[8,8192]{1,0:T(8,128)S(1)}, f32[8,8192]{1,0:T(8,128)S(1)}, u32[]{:S(2)}, u32[]{:S(2)}) collective-permute-start(f32[8,8192]{1,0:T(8,128)S(1)} %get-tuple-element.46), channel_id=1, source_target_pairs={{0,224},{32,0},{64,32},{96,64},{128,96},{160,128},{192,160},{224,1... | collective-permute-start | bytes 786440 | tf_op jit(solution)/shard_map/ppermute | solution.py:309
  10.4 0.7 %copy-start.4 = (s32[2,2048]{1,0:T(2,128)S(1)}, s32[2,2048]{1,0:T(2,128)}, u32[]{:S(2)}) copy-start(s32[2,2048]{1,0:T(2,128)} %cells.1) | copy-start | bytes 49156
  11.1 0.7 %copy-start.5 = (f32[2,2048]{1,0:T(2,128)S(1)}, f32[2,2048]{1,0:T(2,128)}, u32[]{:S(2)}) copy-start(f32[2,2048]{1,0:T(2,128)} %vals.1) | copy-start | bytes 49156
  11.8 0.7 copy-start.6
  13.9 11.0 %collective-permute-start.1 = (f32[8,8192]{1,0:T(8,128)S(1)}, f32[8,8192]{1,0:T(8,128)S(1)}, u32[]{:S(2)}, u32[]{:S(2)}) collective-permute-start(f32[8,8192]{1,0:T(8,128)S(1)} %collective-permute-done.refs_0_), channel_id=1, source_target_pairs={{0,32},{32,64},{64,96},{96,128},{128,160},{160,192},{192,224},{224... | collective-permute-start | bytes 786440 | tf_op jit(solution)/shard_map/ppermute | solution.py:308
  14.0 10.9 %collective-permute-start.4 = (f32[8,8192]{1,0:T(8,128)S(1)}, f32[8,8192]{1,0:T(8,128)S(1)}, u32[]{:S(2)}, u32[]{:S(2)}) collective-permute-start(f32[8,8192]{1,0:T(8,128)S(1)} %collective-permute-done.3.refs_3_), channel_id=1, source_target_pairs={{0,224},{32,0},{64,32},{96,64},{128,96},{160,128},{192,160},{224,1... | collective-permute-start | bytes 786440 | tf_op jit(solution)/shard_map/ppermute | solution.py:309
  19.3 11.2 %collective-permute-start.12 = (f32[8,8192]{1,0:T(8,128)S(1)}, f32[8,8192]{1,0:T(8,128)S(1)}, u32[]{:S(2)}, u32[]{:S(2)}) collective-permute-start(f32[8,8192]{1,0:T(8,128)S(1)} %collective-permute-done.10.refs_1_), channel_id=1, source_target_pairs={{0,32},{32,64},{64,96},{96,128},{128,160},{160,192},{192,224},{224... | collective-permute-start | bytes 786440 | tf_op jit(solution)/shard_map/ppermute | solution.py:308
  19.3 11.2 %collective-permute-start.13 = (f32[8,8192]{1,0:T(8,128)S(1)}, f32[8,8192]{1,0:T(8,128)S(1)}, u32[]{:S(2)}, u32[]{:S(2)}) collective-permute-start(f32[8,8192]{1,0:T(8,128)S(1)} %collective-permute-done.11.refs_2_), channel_id=1, source_target_pairs={{0,224},{32,0},{64,32},{96,64},{128,96},{160,128},{192,160},{224,1... | collective-permute-start | bytes 786440 | tf_op jit(solution)/shard_map/ppermute | solution.py:309
  22.0 1.0 %copy-start.1 = (f32[8,16384]{1,0:T(8,128)S(1)}, f32[8,16384]{1,0:T(8,128)}, u32[]{:S(2)}) copy-start(f32[8,16384]{1,0:T(8,128)} %refs_12_.1) | copy-start | bytes 1572868
  23.0 1.2 %copy-start.3 = (f32[2,8,16384]{2,1,0:T(8,128)S(1)}, f32[2,8,16384]{2,1,0:T(8,128)}, u32[]{:S(2)}) copy-start(f32[2,8,16384]{2,1,0:T(8,128)} %noise.1) | copy-start | bytes 3145732
  24.9 10.3 %collective-permute-start.5 = (f32[8,8192]{1,0:T(8,128)S(1)}, f32[8,8192]{1,0:T(8,128)S(1)}, u32[]{:S(2)}, u32[]{:S(2)}) collective-permute-start(f32[8,8192]{1,0:T(8,128)S(1)} %collective-permute-done.4.refs_7_), channel_id=1, source_target_pairs={{0,224},{32,0},{64,32},{96,64},{128,96},{160,128},{192,160},{224,1... | collective-permute-start | bytes 786440 | tf_op jit(solution)/shard_map/ppermute | solution.py:309
  27.4 7.8 %collective-permute-start.2 = (f32[8,8192]{1,0:T(8,128)S(1)}, f32[8,8192]{1,0:T(8,128)S(1)}, u32[]{:S(2)}, u32[]{:S(2)}) collective-permute-start(f32[8,8192]{1,0:T(8,128)S(1)} %collective-permute-done.1.refs_4_), channel_id=1, source_target_pairs={{0,32},{32,64},{64,96},{96,128},{128,160},{160,192},{192,224},{224... | collective-permute-start | bytes 786440 | tf_op jit(solution)/shard_map/ppermute | solution.py:308
  30.5 9.3 %collective-permute-start.14 = (f32[8,8192]{1,0:T(8,128)S(1)}, f32[8,8192]{1,0:T(8,128)S(1)}, u32[]{:S(2)}, u32[]{:S(2)}) collective-permute-start(f32[8,8192]{1,0:T(8,128)S(1)} %collective-permute-done.12.refs_5_), channel_id=1, source_target_pairs={{0,32},{32,64},{64,96},{96,128},{128,160},{160,192},{192,224},{224... | collective-permute-start | bytes 786440 | tf_op jit(solution)/shard_map/ppermute | solution.py:308
  30.5 12.3 %collective-permute-start.15 = (f32[8,8192]{1,0:T(8,128)S(1)}, f32[8,8192]{1,0:T(8,128)S(1)}, u32[]{:S(2)}, u32[]{:S(2)}) collective-permute-start(f32[8,8192]{1,0:T(8,128)S(1)} %collective-permute-done.13.refs_6_), channel_id=1, source_target_pairs={{0,224},{32,0},{64,32},{96,64},{128,96},{160,128},{192,160},{224,1... | collective-permute-start | bytes 786440 | tf_op jit(solution)/shard_map/ppermute | solution.py:309
  35.2 9.2 %collective-permute-start.8 = (f32[8,4096]{1,0:T(8,128)S(1)}, f32[8,4096]{1,0:T(8,128)S(1)}, u32[]{:S(2)}, u32[]{:S(2)}) collective-permute-start(f32[8,4096]{1,0:T(8,128)S(1)} %get-tuple-element.49), channel_id=1, source_target_pairs={{0,32},{32,64},{64,96},{96,128},{128,160},{160,192},{192,224},{224... | collective-permute-start | bytes 393224 | tf_op jit(solution)/shard_map/ppermute | solution.py:315
  35.3 9.1 %collective-permute-start.9 = (f32[8,4096]{1,0:T(8,128)S(1)}, f32[8,4096]{1,0:T(8,128)S(1)}, u32[]{:S(2)}, u32[]{:S(2)}) collective-permute-start(f32[8,4096]{1,0:T(8,128)S(1)} %get-tuple-element.47), channel_id=1, source_target_pairs={{0,224},{32,0},{64,32},{96,64},{128,96},{160,128},{192,160},{224,1... | collective-permute-start | bytes 393224 | tf_op jit(solution)/shard_map/ppermute | solution.py:315
  38.8 6.8 %collective-permute-start.6 = (f32[8,4096]{1,0:T(8,128)S(1)}, f32[8,4096]{1,0:T(8,128)S(1)}, u32[]{:S(2)}, u32[]{:S(2)}) collective-permute-start(f32[8,4096]{1,0:T(8,128)S(1)} %get-tuple-element.50), channel_id=1, source_target_pairs={{0,32},{32,64},{64,96},{96,128},{128,160},{160,192},{192,224},{224... | collective-permute-start | bytes 393224 | tf_op jit(solution)/shard_map/ppermute | solution.py:315
  39.8 5.8 %collective-permute-start.7 = (f32[8,4096]{1,0:T(8,128)S(1)}, f32[8,4096]{1,0:T(8,128)S(1)}, u32[]{:S(2)}, u32[]{:S(2)}) collective-permute-start(f32[8,4096]{1,0:T(8,128)S(1)} %get-tuple-element.48), channel_id=1, source_target_pairs={{0,224},{32,0},{64,32},{96,64},{128,96},{160,128},{192,160},{224,1... | collective-permute-start | bytes 393224 | tf_op jit(solution)/shard_map/ppermute | solution.py:315
  46.6 6.3 %collective-permute-start.16 = (f32[32,128]{1,0:T(8,128)S(1)}, f32[32,128]{1,0:T(8,128)S(1)}, u32[]{:S(2)}, u32[]{:S(2)}) collective-permute-start(f32[32,128]{1,0:T(8,128)S(1)} %get-tuple-element.41), channel_id=1, source_target_pairs={{0,1},{1,0},{2,3},{3,2},{4,5},{5,4},{6,7},{7,6},{8,9},{9,8},{10,11... | collective-permute-start | bytes 49160 | tf_op jit(solution)/shard_map/ppermute | solution.py:286

commit v7 on v5

--- a/solution.py
+++ b/solution.py
@@ -82,6 +82,25 @@
     lax.fori_loop(0, prec.shape[0], step, 0, unroll=8)
 
 
+def local_kernel(samples, noise, prec, targ, u, base, ab):
+    k0, k1 = constants(0), constants(1)
+
+    def local(where, p, t):
+        a1 = k1["gain"] - k1["pull"] * p
+        x = (k0["gain"] - k0["pull"] * p) * samples[:, where]
+        x = x + k0["pull"] * t + k0["kick"] * noise[0, :, where]
+        u[:, where] = x
+        base[:, where] = a1 * x + k1["pull"] * t + k1["kick"] * noise[1, :, where]
+        ab[:, where] = jnp.broadcast_to(k0["lift"] * a1, x.shape)
+
+    per_row(prec, targ, local)
+
+
+def local_terms(*args):
+    shape = jax.ShapeDtypeStruct(args[0].shape, F32)
+    return call(local_kernel, (shape, shape, shape), args, 10**9, name="local")
+
+
 CHUNK = 4096
 LIMIT = pltpu.CompilerParams(vmem_limit_bytes=16 << 20)
 
@@ -127,18 +146,7 @@
 
 
 def early_kernel(own, *refs):
-    blocks, samples, noise, prec, targ, z, stack, base, ab, u = refs[:-9], *refs[-9:]
-    k0, k1 = constants(0), constants(1)
-
-    def local(where, p, t):
-        a1 = k1["gain"] - k1["pull"] * p
-        x = (k0["gain"] - k0["pull"] * p) * samples[:, where]
-        x = x + k0["pull"] * t + k0["kick"] * noise[0, :, where]
-        u[:, where] = x
-        base[:, where] = a1 * x + k1["pull"] * t + k1["kick"] * noise[1, :, where]
-        ab[:, where] = jnp.broadcast_to(k0["lift"] * a1, x.shape)
-
-    per_row(prec, targ, local)
+    blocks, samples, u, z, stack = refs[:-4], *refs[-4:]
     blocks = [blocks[i : i + 2] for i in range(0, len(blocks), 2)]
     blocks = [halves(own), *blocks, halves(samples), halves(u)]
 
@@ -158,18 +166,13 @@
     z[2 * ROWS :, 3 * q : 2 * q + near] = acc[near:, q:near]
 
 
-def early(samples, noise, prec, targ, own, blocks):
+def early(samples, u, own, blocks):
     rows = ROWS * (3 + len(blocks) // 2)
     shapes = (
         jax.ShapeDtypeStruct((ROWS * RINGS // 2, 2 * ROWS * RINGS), F32),
         jax.ShapeDtypeStruct((2 * (rows + ROWS), own.shape[1]), BF),
-        jax.ShapeDtypeStruct(own.shape, F32),
-        jax.ShapeDtypeStruct(own.shape, F32),
-    )
-    args = (own, *blocks, samples, noise, prec, targ)
-    return call(
-        early_kernel, shapes, args, 10**9, [pltpu.VMEM(own.shape, F32)], name="early"
-    )
+    )
+    return call(early_kernel, shapes, (own, *blocks, samples, u), 10**9, name="early")
 
 
 def last_kernel(*refs):
@@ -278,14 +281,16 @@
     blocks = []
     prec, targ = fields(obs_cells, obs_values, seismic_mask)
     for hop in range(3):
-        if hop > 0:
+        if hop == 1:
             rising[0], prec, targ = lax.optimization_barrier((rising[0], prec, targ))
+            u, base, ab = local_terms(samples, noise, prec, targ)
+        if hop == 2:
+            rising[0], u, base, ab = lax.optimization_barrier((rising[0], u, base, ab))
         for c in range(2):
             rising[c] = lax.ppermute(rising[c], "member", up)
             falling[c] = lax.ppermute(falling[c], "member", down)
         blocks += [*rising, *falling]
-    rising[0], prec, targ = lax.optimization_barrier((rising[0], prec, targ))
-    z1, stack, base, ab = early(samples, noise, prec, targ, prior, blocks)
+    z1, stack = early(samples, u, prior, blocks)
     far = [lax.ppermute(rising[0], "member", up), lax.ppermute(falling[1], "member", down)]
     z, stack = last(far, z1, stack)
     z = total(z)

time: 68.7 us -> 68.7 us (level)
  waiting for transfers between devices: 15.8 us -> 14.9 us
  starting transfers between devices: 25.3 us -> 26 us
    ppermute x6, waiting for transfers between devices: 14.6 us -> 7.11 us  [per_device(): rising[c] = lax.ppermute(rising[c], 'member', up)]
    ppermute x1, waiting for transfers between devices: 0.37 us -> 4.02 us  [per_device(): lax.ppermute(falling[1], 'member', down)]
    ppermute x6, waiting for transfers between devices: 0.02 us -> 2.97 us  [per_device(): falling[c] = lax.ppermute(falling[c], 'member', down)]
    ppermute x1, starting transfers between devices: 2.44 us -> 3.41 us  [per_device(): lax.ppermute(falling[1], 'member', down)]
    unnamed x12 -> x14, local copies, waits for them, and re-layouts: 4.2 us -> 4.38 us
    pallas_call x4 -> x5, Pallas kernels: 7.5 us -> 7.44 us  [call(): pl.pallas_call(kernel, out_shape=out_shape, in_specs=[pl.BlockSpec(memory...]
  transfers between devices with their start and end apart: 15 -> 15, of which waited for: 7 -> 8; matrix products, arithmetic and copies ran while one was open for 0% -> 0% of each run, Pallas kernels for 5% -> 5%
where the time goes in v7:
time: 68.7 us; the launch traced here: 68.3 us
  starting transfers between devices  26 us (38%)
  waiting for transfers between devices  14.9 us (22%)
  blocking collectives  14.1 us (21%)
  Pallas kernels  7.44 us (11%)
  local copies, waits for them, and re-layouts  5.56 us (8%)
    ppermute x6, starting transfers between devices, per_device(): falling[c] = lax.ppermute(falling[c], 'member', down)  17.1 us
    all_to_all x1, blocking collectives, total(): lax.all_to_all(x, ('x', 'y'), split_axis=0, concat_axis=0, tiled=True)  14.1 us
    pallas_call x5, Pallas kernels, call(): pl.pallas_call(kernel, out_shape=out_shape, in_specs=[pl.BlockSpec(memory...  7.44 us
    ppermute x6, waiting for transfers between devices, per_device(): rising[c] = lax.ppermute(rising[c], 'member', up)  7.11 us
    unnamed x14, local copies, waits for them, and re-layouts  4.38 us
    ppermute x1, waiting for transfers between devices, per_device(): lax.ppermute(falling[1], 'member', down)  4.02 us
    ppermute x1, starting transfers between devices, per_device(): lax.ppermute(falling[1], 'member', down)  3.41 us
    ppermute x6, waiting for transfers between devices, per_device(): falling[c] = lax.ppermute(falling[c], 'member', down)  2.97 us
  transfers between devices with their start and end apart: 15, of which 8 were waited for; matrix products, arithmetic and copies ran while one was open for 0% of the time, Pallas kernels for 5%

profile of v7, /device:TPU:1, one launch (start us, length us, event | category | flops | bytes accessed | tf_op | source)
XLA Modules:
  0.0 68.3 jit_solution(9218741056716575748)
XLA Ops:
  0.0 0.0 copy-start
  0.0 0.0 copy-start.2
  0.0 1.2 %fusion = (f32[8,8192]{1,0:T(8,128)S(1)}, f32[8,8192]{1,0:T(8,128)S(1)}) fusion(f32[8,16384]{1,0:T(8,128)} %own.1), kind=kLoop, calls=%fused_computation | loop fusion | bytes 1048576 | tf_op jit(solution)/shard_map/slice | solution.py:279
  1.2 2.5 %collective-permute-start = (f32[8,8192]{1,0:T(8,128)S(1)}, f32[8,8192]{1,0:T(8,128)S(1)}, u32[]{:S(2)}, u32[]{:S(2)}) collective-permute-start(f32[8,8192]{1,0:T(8,128)S(1)} %get-tuple-element.38), channel_id=1, source_target_pairs={{0,32},{32,64},{64,96},{96,128},{128,160},{160,192},{192,224},{224... | collective-permute-start | bytes 786440 | tf_op jit(solution)/shard_map/ppermute | solution.py:290
  3.7 4.0 %collective-permute-start.4 = (f32[8,8192]{1,0:T(8,128)S(1)}, f32[8,8192]{1,0:T(8,128)S(1)}, u32[]{:S(2)}, u32[]{:S(2)}) collective-permute-start(f32[8,8192]{1,0:T(8,128)S(1)} %get-tuple-element.37), channel_id=1, source_target_pairs={{0,224},{32,0},{64,32},{96,64},{128,96},{160,128},{192,160},{224,1... | collective-permute-start | bytes 786440 | tf_op jit(solution)/shard_map/ppermute | solution.py:291
  7.7 0.0 collective-permute-start.8
  7.7 2.7 %collective-permute-start.9 = (f32[8,8192]{1,0:T(8,128)S(1)}, f32[8,8192]{1,0:T(8,128)S(1)}, u32[]{:S(2)}, u32[]{:S(2)}) collective-permute-start(f32[8,8192]{1,0:T(8,128)S(1)} %get-tuple-element.38), channel_id=1, source_target_pairs={{0,224},{32,0},{64,32},{96,64},{128,96},{160,128},{192,160},{224,1... | collective-permute-start | bytes 786440 | tf_op jit(solution)/shard_map/ppermute | solution.py:291
  10.4 0.0 copy-start.4
  10.4 0.7 %copy-done.4 = s32[2,2048]{1,0:T(2,128)S(1)} copy-done((s32[2,2048]{1,0:T(2,128)S(1)}, s32[2,2048]{1,0:T(2,128)}, u32[]{:S(2)}) %copy-start.4) | copy-done | bytes 16408
  11.1 0.0 copy-start.5
  11.1 0.7 %copy-done.5 = f32[2,2048]{1,0:T(2,128)S(1)} copy-done((f32[2,2048]{1,0:T(2,128)S(1)}, f32[2,2048]{1,0:T(2,128)}, u32[]{:S(2)}) %copy-start.5) | copy-done | bytes 16408
  11.8 0.7 copy-done.6
  12.5 1.4 %fields.1 = (f32[128,128]{1,0:T(8,128)S(1)}, f32[128,128]{1,0:T(8,128)S(1)}) custom-call(s32[2,2048]{1,0:T(2,128)S(1)} %copy-done.4, f32[2,2048]{1,0:T(2,128)S(1)} %copy-done.5, s32[2,128]{1,0:T(2,128)S(1)} %copy-done.6), custom_call_target="tpu_custom_call" | custom-call | flops 1000000000 | bytes 4000000 | tf_op jit(solution)/shard_map/fields/pallas_call | solution.py:110
  13.9 0.0 collective-permute-done.refs_0_
  13.9 0.1 collective-permute-start.1
  14.0 0.0 collective-permute-done.4.refs_3_
  14.0 2.7 %collective-permute-start.5 = (f32[8,8192]{1,0:T(8,128)S(1)}, f32[8,8192]{1,0:T(8,128)S(1)}, u32[]{:S(2)}, u32[]{:S(2)}) collective-permute-start(f32[8,8192]{1,0:T(8,128)S(1)} %collective-permute-done.4.refs_3_), channel_id=1, source_target_pairs={{0,224},{32,0},{64,32},{96,64},{128,96},{160,128},{192,160},{224,1... | collective-permute-start | bytes 786440 | tf_op jit(solution)/shard_map/ppermute | solution.py:291
  16.7 2.6 %collective-permute-done.8.refs_1_ = f32[8,8192]{1,0:T(8,128)S(1)} collective-permute-done((f32[8,8192]{1,0:T(8,128)S(1)}, f32[8,8192]{1,0:T(8,128)S(1)}, u32[]{:S(2)}, u32[]{:S(2)}) %collective-permute-start.8) | collective-permute-done | bytes 262176 | tf_op jit(solution)/shard_map/ppermute | solution.py:290
  19.3 0.0 collective-permute-start.10
  19.3 0.0 collective-permute-done.9.refs_2_
  19.3 2.7 %collective-permute-start.11 = (f32[8,8192]{1,0:T(8,128)S(1)}, f32[8,8192]{1,0:T(8,128)S(1)}, u32[]{:S(2)}, u32[]{:S(2)}) collective-permute-start(f32[8,8192]{1,0:T(8,128)S(1)} %collective-permute-done.9.refs_2_), channel_id=1, source_target_pairs={{0,224},{32,0},{64,32},{96,64},{128,96},{160,128},{192,160},{224,1... | collective-permute-start | bytes 786440 | tf_op jit(solution)/shard_map/ppermute | solution.py:291
  22.0 1.0 %copy-done.1 = f32[8,16384]{1,0:T(8,128)S(1)} copy-done((f32[8,16384]{1,0:T(8,128)S(1)}, f32[8,16384]{1,0:T(8,128)}, u32[]{:S(2)}) %copy-start.1) | copy-done | bytes 524312
  23.0 1.2 %copy-done.3 = f32[2,8,16384]{2,1,0:T(8,128)S(1)} copy-done((f32[2,8,16384]{2,1,0:T(8,128)S(1)}, f32[2,8,16384]{2,1,0:T(8,128)}, u32[]{:S(2)}) %copy-start.3) | copy-done | bytes 1048600
  24.2 0.5 local.1
  24.8 0.1 collective-permute-done.1.refs_4_
  24.9 0.0 collective-permute-done.5.refs_7_
  24.9 2.4 %collective-permute-start.6 = (f32[8,8192]{1,0:T(8,128)S(1)}, f32[8,8192]{1,0:T(8,128)S(1)}, u32[]{:S(2)}, u32[]{:S(2)}) collective-permute-start(f32[8,8192]{1,0:T(8,128)S(1)} %collective-permute-done.5.refs_7_), channel_id=1, source_target_pairs={{0,224},{32,0},{64,32},{96,64},{128,96},{160,128},{192,160},{224,1... | collective-permute-start | bytes 786440 | tf_op jit(solution)/shard_map/ppermute | solution.py:291
  27.4 0.0 collective-permute-start.2
  27.4 3.2 %collective-permute-done.10.refs_5_ = f32[8,8192]{1,0:T(8,128)S(1)} collective-permute-done((f32[8,8192]{1,0:T(8,128)S(1)}, f32[8,8192]{1,0:T(8,128)S(1)}, u32[]{:S(2)}, u32[]{:S(2)}) %collective-permute-start.10) | collective-permute-done | bytes 262176 | tf_op jit(solution)/shard_map/ppermute | solution.py:290
  30.5 0.0 collective-permute-start.12
  30.5 0.0 collective-permute-done.11.refs_6_
  30.5 2.7 %collective-permute-start.13 = (f32[8,8192]{1,0:T(8,128)S(1)}, f32[8,8192]{1,0:T(8,128)S(1)}, u32[]{:S(2)}, u32[]{:S(2)}) collective-permute-start(f32[8,8192]{1,0:T(8,128)S(1)} %collective-permute-done.11.refs_6_), channel_id=1, source_target_pairs={{0,224},{32,0},{64,32},{96,64},{128,96},{160,128},{192,160},{224,1... | collective-permute-start | bytes 786440 | tf_op jit(solution)/shard_map/ppermute | solution.py:291
  33.2 2.0 %collective-permute-done.6.refs_11_ = f32[8,8192]{1,0:T(8,128)S(1)} collective-permute-done((f32[8,8192]{1,0:T(8,128)S(1)}, f32[8,8192]{1,0:T(8,128)S(1)}, u32[]{:S(2)}, u32[]{:S(2)}) %collective-permute-start.6) | collective-permute-done | bytes 262176 | tf_op jit(solution)/shard_map/ppermute | solution.py:291
  35.2 3.4 %collective-permute-start.7 = (f32[8,8192]{1,0:T(8,128)S(1)}, f32[8,8192]{1,0:T(8,128)S(1)}, u32[]{:S(2)}, u32[]{:S(2)}) collective-permute-start(f32[8,8192]{1,0:T(8,128)S(1)} %collective-permute-done.6.refs_11_), channel_id=1, source_target_pairs={{0,224},{32,0},{64,32},{96,64},{128,96},{160,128},{192,160},{224,1... | collective-permute-start | bytes 786440 | tf_op jit(solution)/shard_map/ppermute | solution.py:294
  38.6 0.0 collective-permute-done.2.refs_8_
  38.6 0.0 collective-permute-start.3
  38.6 1.2 %collective-permute-done.12.refs_9_ = f32[8,8192]{1,0:T(8,128)S(1)} collective-permute-done((f32[8,8192]{1,0:T(8,128)S(1)}, f32[8,8192]{1,0:T(8,128)S(1)}, u32[]{:S(2)}, u32[]{:S(2)}) %collective-permute-start.12) | collective-permute-done | bytes 262176 | tf_op jit(solution)/shard_map/ppermute | solution.py:290
  39.8 1.0 %collective-permute-done.13.refs_10_ = f32[8,8192]{1,0:T(8,128)S(1)} collective-permute-done((f32[8,8192]{1,0:T(8,128)S(1)}, f32[8,8192]{1,0:T(8,128)S(1)}, u32[]{:S(2)}, u32[]{:S(2)}) %collective-permute-start.13) | collective-permute-done | bytes 262176 | tf_op jit(solution)/shard_map/ppermute | solution.py:291
  40.8 0.0 copy-done
  40.8 0.0 copy-done.2
  40.8 1.6 %early.1 = (f32[32,128]{1,0:T(8,128)S(1)}, bf16[160,16384]{1,0:T(8,128)(2,1)S(1)}) custom-call(f32[8,16384]{1,0:T(8,128)S(1)} %copy-done, f32[8,8192]{1,0:T(8,128)S(1)} %collective-permute-done.refs_0_, f32[8,8192]{1,0:T(8,128)S(1)} %collective-permute-done.8.refs_1_, f32[8,8192]{1,0:T(8,128)S(1)} %collective-permute-done.9.refs_2_, ...), custom_call_target="tpu_custom_call" | custom-call | flops 1000000000 | bytes 4000000 | tf_op jit(solution)/shard_map/early/pallas_call | solution.py:110
  42.4 4.0 %collective-permute-done.7.refs_1_ = f32[8,8192]{1,0:T(8,128)S(1)} collective-permute-done((f32[8,8192]{1,0:T(8,128)S(1)}, f32[8,8192]{1,0:T(8,128)S(1)}, u32[]{:S(2)}, u32[]{:S(2)}) %collective-permute-start.7) | collective-permute-done | bytes 262176 | tf_op jit(solution)/shard_map/ppermute | solution.py:294
  46.4 0.0 collective-permute-done.3.refs_0_
  46.4 1.7 %last.1 = (f32[32,128]{1,0:T(8,128)S(1)}, bf16[160,16384]{1,0:T(8,128)(2,1)S(1)}) custom-call(f32[8,8192]{1,0:T(8,128)S(1)} %collective-permute-done.3.refs_0_, f32[8,8192]{1,0:T(8,128)S(1)} %collective-permute-done.7.refs_1_, f32[32,128]{1,0:T(8,128)S(1)} %get-tuple-element.31.refs_2_, ...), custom_call_target="tpu_custom_call", output_to_operand_aliasing={{1}: (3, {})} | custom-call | flops 1000000000 | bytes 4000000 | tf_op jit(solution)/shard_map/last/pallas_call | solution.py:110
  48.1 2.8 %collective-permute-start.14 = (f32[32,128]{1,0:T(8,128)S(1)}, f32[32,128]{1,0:T(8,128)S(1)}, u32[]{:S(2)}, u32[]{:S(2)}) collective-permute-start(f32[32,128]{1,0:T(8,128)S(1)} %get-tuple-element.33), channel_id=1, source_target_pairs={{0,1},{1,0},{2,3},{3,2},{4,5},{5,4},{6,7},{7,6},{8,9},{9,8},{10,11... | collective-permute-start | bytes 49160 | tf_op jit(solution)/shard_map/ppermute | solution.py:268
  50.9 0.8 %collective-permute-done.14 = f32[32,128]{1,0:T(8,128)S(1)} collective-permute-done((f32[32,128]{1,0:T(8,128)S(1)}, f32[32,128]{1,0:T(8,128)S(1)}, u32[]{:S(2)}, u32[]{:S(2)}) %collective-permute-start.14) | collective-permute-done | bytes 16416 | tf_op jit(solution)/shard_map/ppermute | solution.py:268
  51.8 14.1 %all_to_all.5.refs_0_ = f32[16,32,128]{2,1,0:T(8,128)S(1)} all-to-all(f32[16,32,128]{2,1,0:T(8,128)S(1)} %broadcast_in_dim.2), channel_id=1, replica_groups=mesh['member'=8,'x'=4,'y'=4,'core'=2] {'x','y'}, dimensions={0} | all-to-all | bytes 524288 | tf_op jit(solution)/shard_map/all_to_all | solution.py:270
  65.9 2.2 %final.1 = f32[8,16384]{1,0:T(8,128)} custom-call(f32[16,32,128]{2,1,0:T(8,128)S(1)} %all_to_all.5.refs_0_, bf16[160,16384]{1,0:T(8,128)(2,1)S(1)} %get-tuple-element.34.refs_1_, f32[8,16384]{1,0:T(8,128)S(1)} %get-tuple-element.35.refs_2_, f32[8,16384]{1,0:T(8,128)S(1)} %get-tuple-element.36.refs_3_), custom_call_target="tpu_custom_call" | custom-call | flops 1000000000 | bytes 4000000 | tf_op jit(solution)/shard_map/final/pallas_call | solution.py:110
  (5 shorter events, 0.0 us)
Async XLA Ops:
  0.0 40.8 %copy-start = (f32[8,16384]{1,0:T(8,128)S(1)}, f32[8,16384]{1,0:T(8,128)}, u32[]{:S(2)}) copy-start(f32[8,16384]{1,0:T(8,128)} %own.1) | copy-start | bytes 1572868
  0.0 40.8 %copy-start.2 = (f32[8,16384]{1,0:T(8,128)S(1)}, f32[8,16384]{1,0:T(8,128)}, u32[]{:S(2)}) copy-start(f32[8,16384]{1,0:T(8,128)} %refs_12_.1) | copy-start | bytes 1572868
  1.2 12.8 %collective-permute-start = (f32[8,8192]{1,0:T(8,128)S(1)}, f32[8,8192]{1,0:T(8,128)S(1)}, u32[]{:S(2)}, u32[]{:S(2)}) collective-permute-start(f32[8,8192]{1,0:T(8,128)S(1)} %get-tuple-element.38), channel_id=1, source_target_pairs={{0,32},{32,64},{64,96},{96,128},{128,160},{160,192},{192,224},{224... | collective-permute-start | bytes 786440 | tf_op jit(solution)/shard_map/ppermute | solution.py:290
  3.7 10.3 %collective-permute-start.4 = (f32[8,8192]{1,0:T(8,128)S(1)}, f32[8,8192]{1,0:T(8,128)S(1)}, u32[]{:S(2)}, u32[]{:S(2)}) collective-permute-start(f32[8,8192]{1,0:T(8,128)S(1)} %get-tuple-element.37), channel_id=1, source_target_pairs={{0,224},{32,0},{64,32},{96,64},{128,96},{160,128},{192,160},{224,1... | collective-permute-start | bytes 786440 | tf_op jit(solution)/shard_map/ppermute | solution.py:291
  7.7 11.6 %collective-permute-start.8 = (f32[8,8192]{1,0:T(8,128)S(1)}, f32[8,8192]{1,0:T(8,128)S(1)}, u32[]{:S(2)}, u32[]{:S(2)}) collective-permute-start(f32[8,8192]{1,0:T(8,128)S(1)} %get-tuple-element.37), channel_id=1, source_target_pairs={{0,32},{32,64},{64,96},{96,128},{128,160},{160,192},{192,224},{224... | collective-permute-start | bytes 786440 | tf_op jit(solution)/shard_map/ppermute | solution.py:290
  7.7 11.6 %collective-permute-start.9 = (f32[8,8192]{1,0:T(8,128)S(1)}, f32[8,8192]{1,0:T(8,128)S(1)}, u32[]{:S(2)}, u32[]{:S(2)}) collective-permute-start(f32[8,8192]{1,0:T(8,128)S(1)} %get-tuple-element.38), channel_id=1, source_target_pairs={{0,224},{32,0},{64,32},{96,64},{128,96},{160,128},{192,160},{224,1... | collective-permute-start | bytes 786440 | tf_op jit(solution)/shard_map/ppermute | solution.py:291
  10.4 0.7 %copy-start.4 = (s32[2,2048]{1,0:T(2,128)S(1)}, s32[2,2048]{1,0:T(2,128)}, u32[]{:S(2)}) copy-start(s32[2,2048]{1,0:T(2,128)} %cells.1) | copy-start | bytes 49156
  11.1 0.7 %copy-start.5 = (f32[2,2048]{1,0:T(2,128)S(1)}, f32[2,2048]{1,0:T(2,128)}, u32[]{:S(2)}) copy-start(f32[2,2048]{1,0:T(2,128)} %vals.1) | copy-start | bytes 49156
  11.8 0.7 copy-start.6
  13.9 11.0 %collective-permute-start.1 = (f32[8,8192]{1,0:T(8,128)S(1)}, f32[8,8192]{1,0:T(8,128)S(1)}, u32[]{:S(2)}, u32[]{:S(2)}) collective-permute-start(f32[8,8192]{1,0:T(8,128)S(1)} %collective-permute-done.refs_0_), channel_id=1, source_target_pairs={{0,32},{32,64},{64,96},{96,128},{128,160},{160,192},{192,224},{224... | collective-permute-start | bytes 786440 | tf_op jit(solution)/shard_map/ppermute | solution.py:290
  14.0 10.9 %collective-permute-start.5 = (f32[8,8192]{1,0:T(8,128)S(1)}, f32[8,8192]{1,0:T(8,128)S(1)}, u32[]{:S(2)}, u32[]{:S(2)}) collective-permute-start(f32[8,8192]{1,0:T(8,128)S(1)} %collective-permute-done.4.refs_3_), channel_id=1, source_target_pairs={{0,224},{32,0},{64,32},{96,64},{128,96},{160,128},{192,160},{224,1... | collective-permute-start | bytes 786440 | tf_op jit(solution)/shard_map/ppermute | solution.py:291
  19.3 11.2 %collective-permute-start.10 = (f32[8,8192]{1,0:T(8,128)S(1)}, f32[8,8192]{1,0:T(8,128)S(1)}, u32[]{:S(2)}, u32[]{:S(2)}) collective-permute-start(f32[8,8192]{1,0:T(8,128)S(1)} %collective-permute-done.8.refs_1_), channel_id=1, source_target_pairs={{0,32},{32,64},{64,96},{96,128},{128,160},{160,192},{192,224},{224... | collective-permute-start | bytes 786440 | tf_op jit(solution)/shard_map/ppermute | solution.py:290
  19.3 11.2 %collective-permute-start.11 = (f32[8,8192]{1,0:T(8,128)S(1)}, f32[8,8192]{1,0:T(8,128)S(1)}, u32[]{:S(2)}, u32[]{:S(2)}) collective-permute-start(f32[8,8192]{1,0:T(8,128)S(1)} %collective-permute-done.9.refs_2_), channel_id=1, source_target_pairs={{0,224},{32,0},{64,32},{96,64},{128,96},{160,128},{192,160},{224,1... | collective-permute-start | bytes 786440 | tf_op jit(solution)/shard_map/ppermute | solution.py:291
  22.0 1.0 %copy-start.1 = (f32[8,16384]{1,0:T(8,128)S(1)}, f32[8,16384]{1,0:T(8,128)}, u32[]{:S(2)}) copy-start(f32[8,16384]{1,0:T(8,128)} %refs_12_.1) | copy-start | bytes 1572868
  23.0 1.2 %copy-start.3 = (f32[2,8,16384]{2,1,0:T(8,128)S(1)}, f32[2,8,16384]{2,1,0:T(8,128)}, u32[]{:S(2)}) copy-start(f32[2,8,16384]{2,1,0:T(8,128)} %noise.1) | copy-start | bytes 3145732
  24.9 10.3 %collective-permute-start.6 = (f32[8,8192]{1,0:T(8,128)S(1)}, f32[8,8192]{1,0:T(8,128)S(1)}, u32[]{:S(2)}, u32[]{:S(2)}) collective-permute-start(f32[8,8192]{1,0:T(8,128)S(1)} %collective-permute-done.5.refs_7_), channel_id=1, source_target_pairs={{0,224},{32,0},{64,32},{96,64},{128,96},{160,128},{192,160},{224,1... | collective-permute-start | bytes 786440 | tf_op jit(solution)/shard_map/ppermute | solution.py:291
  27.4 11.2 %collective-permute-start.2 = (f32[8,8192]{1,0:T(8,128)S(1)}, f32[8,8192]{1,0:T(8,128)S(1)}, u32[]{:S(2)}, u32[]{:S(2)}) collective-permute-start(f32[8,8192]{1,0:T(8,128)S(1)} %collective-permute-done.1.refs_4_), channel_id=1, source_target_pairs={{0,32},{32,64},{64,96},{96,128},{128,160},{160,192},{192,224},{224... | collective-permute-start | bytes 786440 | tf_op jit(solution)/shard_map/ppermute | solution.py:290
  30.5 9.3 %collective-permute-start.12 = (f32[8,8192]{1,0:T(8,128)S(1)}, f32[8,8192]{1,0:T(8,128)S(1)}, u32[]{:S(2)}, u32[]{:S(2)}) collective-permute-start(f32[8,8192]{1,0:T(8,128)S(1)} %collective-permute-done.10.refs_5_), channel_id=1, source_target_pairs={{0,32},{32,64},{64,96},{96,128},{128,160},{160,192},{192,224},{224... | collective-permute-start | bytes 786440 | tf_op jit(solution)/shard_map/ppermute | solution.py:290
  30.5 10.3 %collective-permute-start.13 = (f32[8,8192]{1,0:T(8,128)S(1)}, f32[8,8192]{1,0:T(8,128)S(1)}, u32[]{:S(2)}, u32[]{:S(2)}) collective-permute-start(f32[8,8192]{1,0:T(8,128)S(1)} %collective-permute-done.11.refs_6_), channel_id=1, source_target_pairs={{0,224},{32,0},{64,32},{96,64},{128,96},{160,128},{192,160},{224,1... | collective-permute-start | bytes 786440 | tf_op jit(solution)/shard_map/ppermute | solution.py:291
  35.2 11.2 %collective-permute-start.7 = (f32[8,8192]{1,0:T(8,128)S(1)}, f32[8,8192]{1,0:T(8,128)S(1)}, u32[]{:S(2)}, u32[]{:S(2)}) collective-permute-start(f32[8,8192]{1,0:T(8,128)S(1)} %collective-permute-done.6.refs_11_), channel_id=1, source_target_pairs={{0,224},{32,0},{64,32},{96,64},{128,96},{160,128},{192,160},{224,1... | collective-permute-start | bytes 786440 | tf_op jit(solution)/shard_map/ppermute | solution.py:294
  38.6 7.8 %collective-permute-start.3 = (f32[8,8192]{1,0:T(8,128)S(1)}, f32[8,8192]{1,0:T(8,128)S(1)}, u32[]{:S(2)}, u32[]{:S(2)}) collective-permute-start(f32[8,8192]{1,0:T(8,128)S(1)} %collective-permute-done.2.refs_8_), channel_id=1, source_target_pairs={{0,32},{32,64},{64,96},{96,128},{128,160},{160,192},{192,224},{224... | collective-permute-start | bytes 786440 | tf_op jit(solution)/shard_map/ppermute | solution.py:294
  48.1 3.7 %collective-permute-start.14 = (f32[32,128]{1,0:T(8,128)S(1)}, f32[32,128]{1,0:T(8,128)S(1)}, u32[]{:S(2)}, u32[]{:S(2)}) collective-permute-start(f32[32,128]{1,0:T(8,128)S(1)} %get-tuple-element.33), channel_id=1, source_target_pairs={{0,1},{1,0},{2,3},{3,2},{4,5},{5,4},{6,7},{7,6},{8,9},{9,8},{10,11... | collective-permute-start | bytes 49160 | tf_op jit(solution)/shard_map/ppermute | solution.py:268

commit v8 on v7

--- a/solution.py
+++ b/solution.py
@@ -101,7 +101,7 @@
     return call(local_kernel, (shape, shape, shape), args, 10**9, name="local")
 
 
-CHUNK = 4096
+CHUNK = 8192
 LIMIT = pltpu.CompilerParams(vmem_limit_bytes=16 << 20)
 
 

time: 68.7 us -> 68.7 us (level)
  no operation moved by 1% of the time
where the time goes in v8:
time: 68.7 us; the launch traced here: 68.3 us
  starting transfers between devices  26 us (38%)
  waiting for transfers between devices  14.9 us (22%)
  blocking collectives  14.1 us (21%)
  Pallas kernels  7.44 us (11%)
  local copies, waits for them, and re-layouts  5.56 us (8%)
    ppermute x6, starting transfers between devices, per_device(): falling[c] = lax.ppermute(falling[c], 'member', down)  17.1 us
    all_to_all x1, blocking collectives, total(): lax.all_to_all(x, ('x', 'y'), split_axis=0, concat_axis=0, tiled=True)  14.1 us
    pallas_call x5, Pallas kernels, call(): pl.pallas_call(kernel, out_shape=out_shape, in_specs=[pl.BlockSpec(memory...  7.44 us
    ppermute x6, waiting for transfers between devices, per_device(): rising[c] = lax.ppermute(rising[c], 'member', up)  7.11 us
    unnamed x14, local copies, waits for them, and re-layouts  4.38 us
    ppermute x1, waiting for transfers between devices, per_device(): lax.ppermute(falling[1], 'member', down)  4.02 us
    ppermute x1, starting transfers between devices, per_device(): lax.ppermute(falling[1], 'member', down)  3.41 us
    ppermute x6, waiting for transfers between devices, per_device(): falling[c] = lax.ppermute(falling[c], 'member', down)  2.97 us
  transfers between devices with their start and end apart: 15, of which 8 were waited for; matrix products, arithmetic and copies ran while one was open for 0% of the time, Pallas kernels for 5%

profile of v8, /device:TPU:1, one launch (start us, length us, event | category | flops | bytes accessed | tf_op | source)
XLA Modules:
  0.0 68.3 jit_solution(8679774834860719755)
XLA Ops:
  0.0 0.0 copy-start
  0.0 0.0 copy-start.2
  0.0 1.2 %fusion = (f32[8,8192]{1,0:T(8,128)S(1)}, f32[8,8192]{1,0:T(8,128)S(1)}) fusion(f32[8,16384]{1,0:T(8,128)} %own.1), kind=kLoop, calls=%fused_computation | loop fusion | bytes 1048576 | tf_op jit(solution)/shard_map/slice | solution.py:279
  1.2 2.5 %collective-permute-start = (f32[8,8192]{1,0:T(8,128)S(1)}, f32[8,8192]{1,0:T(8,128)S(1)}, u32[]{:S(2)}, u32[]{:S(2)}) collective-permute-start(f32[8,8192]{1,0:T(8,128)S(1)} %get-tuple-element.38), channel_id=1, source_target_pairs={{0,32},{32,64},{64,96},{96,128},{128,160},{160,192},{192,224},{224... | collective-permute-start | bytes 786440 | tf_op jit(solution)/shard_map/ppermute | solution.py:290
  3.7 4.0 %collective-permute-start.4 = (f32[8,8192]{1,0:T(8,128)S(1)}, f32[8,8192]{1,0:T(8,128)S(1)}, u32[]{:S(2)}, u32[]{:S(2)}) collective-permute-start(f32[8,8192]{1,0:T(8,128)S(1)} %get-tuple-element.37), channel_id=1, source_target_pairs={{0,224},{32,0},{64,32},{96,64},{128,96},{160,128},{192,160},{224,1... | collective-permute-start | bytes 786440 | tf_op jit(solution)/shard_map/ppermute | solution.py:291
  7.7 0.0 collective-permute-start.8
  7.7 2.7 %collective-permute-start.9 = (f32[8,8192]{1,0:T(8,128)S(1)}, f32[8,8192]{1,0:T(8,128)S(1)}, u32[]{:S(2)}, u32[]{:S(2)}) collective-permute-start(f32[8,8192]{1,0:T(8,128)S(1)} %get-tuple-element.38), channel_id=1, source_target_pairs={{0,224},{32,0},{64,32},{96,64},{128,96},{160,128},{192,160},{224,1... | collective-permute-start | bytes 786440 | tf_op jit(solution)/shard_map/ppermute | solution.py:291
  10.4 0.0 copy-start.4
  10.4 0.7 %copy-done.4 = s32[2,2048]{1,0:T(2,128)S(1)} copy-done((s32[2,2048]{1,0:T(2,128)S(1)}, s32[2,2048]{1,0:T(2,128)}, u32[]{:S(2)}) %copy-start.4) | copy-done | bytes 16408
  11.1 0.0 copy-start.5
  11.1 0.7 %copy-done.5 = f32[2,2048]{1,0:T(2,128)S(1)} copy-done((f32[2,2048]{1,0:T(2,128)S(1)}, f32[2,2048]{1,0:T(2,128)}, u32[]{:S(2)}) %copy-start.5) | copy-done | bytes 16408
  11.8 0.7 copy-done.6
  12.5 1.4 %fields.1 = (f32[128,128]{1,0:T(8,128)S(1)}, f32[128,128]{1,0:T(8,128)S(1)}) custom-call(s32[2,2048]{1,0:T(2,128)S(1)} %copy-done.4, f32[2,2048]{1,0:T(2,128)S(1)} %copy-done.5, s32[2,128]{1,0:T(2,128)S(1)} %copy-done.6), custom_call_target="tpu_custom_call" | custom-call | flops 1000000000 | bytes 4000000 | tf_op jit(solution)/shard_map/fields/pallas_call | solution.py:110
  13.9 0.0 collective-permute-done.refs_0_
  13.9 0.1 collective-permute-start.1
  14.0 0.0 collective-permute-done.4.refs_3_
  14.0 2.7 %collective-permute-start.5 = (f32[8,8192]{1,0:T(8,128)S(1)}, f32[8,8192]{1,0:T(8,128)S(1)}, u32[]{:S(2)}, u32[]{:S(2)}) collective-permute-start(f32[8,8192]{1,0:T(8,128)S(1)} %collective-permute-done.4.refs_3_), channel_id=1, source_target_pairs={{0,224},{32,0},{64,32},{96,64},{128,96},{160,128},{192,160},{224,1... | collective-permute-start | bytes 786440 | tf_op jit(solution)/shard_map/ppermute | solution.py:291
  16.7 2.6 %collective-permute-done.8.refs_1_ = f32[8,8192]{1,0:T(8,128)S(1)} collective-permute-done((f32[8,8192]{1,0:T(8,128)S(1)}, f32[8,8192]{1,0:T(8,128)S(1)}, u32[]{:S(2)}, u32[]{:S(2)}) %collective-permute-start.8) | collective-permute-done | bytes 262176 | tf_op jit(solution)/shard_map/ppermute | solution.py:290
  19.3 0.0 collective-permute-start.10
  19.3 0.0 collective-permute-done.9.refs_2_
  19.3 2.7 %collective-permute-start.11 = (f32[8,8192]{1,0:T(8,128)S(1)}, f32[8,8192]{1,0:T(8,128)S(1)}, u32[]{:S(2)}, u32[]{:S(2)}) collective-permute-start(f32[8,8192]{1,0:T(8,128)S(1)} %collective-permute-done.9.refs_2_), channel_id=1, source_target_pairs={{0,224},{32,0},{64,32},{96,64},{128,96},{160,128},{192,160},{224,1... | collective-permute-start | bytes 786440 | tf_op jit(solution)/shard_map/ppermute | solution.py:291
  22.0 1.0 %copy-done.1 = f32[8,16384]{1,0:T(8,128)S(1)} copy-done((f32[8,16384]{1,0:T(8,128)S(1)}, f32[8,16384]{1,0:T(8,128)}, u32[]{:S(2)}) %copy-start.1) | copy-done | bytes 524312
  23.0 1.2 %copy-done.3 = f32[2,8,16384]{2,1,0:T(8,128)S(1)} copy-done((f32[2,8,16384]{2,1,0:T(8,128)S(1)}, f32[2,8,16384]{2,1,0:T(8,128)}, u32[]{:S(2)}) %copy-start.3) | copy-done | bytes 1048600
  24.2 0.5 local.1
  24.8 0.1 collective-permute-done.1.refs_4_
  24.9 0.0 collective-permute-done.5.refs_7_
  24.9 2.4 %collective-permute-start.6 = (f32[8,8192]{1,0:T(8,128)S(1)}, f32[8,8192]{1,0:T(8,128)S(1)}, u32[]{:S(2)}, u32[]{:S(2)}) collective-permute-start(f32[8,8192]{1,0:T(8,128)S(1)} %collective-permute-done.5.refs_7_), channel_id=1, source_target_pairs={{0,224},{32,0},{64,32},{96,64},{128,96},{160,128},{192,160},{224,1... | collective-permute-start | bytes 786440 | tf_op jit(solution)/shard_map/ppermute | solution.py:291
  27.4 0.0 collective-permute-start.2
  27.4 3.2 %collective-permute-done.10.refs_5_ = f32[8,8192]{1,0:T(8,128)S(1)} collective-permute-done((f32[8,8192]{1,0:T(8,128)S(1)}, f32[8,8192]{1,0:T(8,128)S(1)}, u32[]{:S(2)}, u32[]{:S(2)}) %collective-permute-start.10) | collective-permute-done | bytes 262176 | tf_op jit(solution)/shard_map/ppermute | solution.py:290
  30.5 0.0 collective-permute-start.12
  30.5 0.0 collective-permute-done.11.refs_6_
  30.5 2.7 %collective-permute-start.13 = (f32[8,8192]{1,0:T(8,128)S(1)}, f32[8,8192]{1,0:T(8,128)S(1)}, u32[]{:S(2)}, u32[]{:S(2)}) collective-permute-start(f32[8,8192]{1,0:T(8,128)S(1)} %collective-permute-done.11.refs_6_), channel_id=1, source_target_pairs={{0,224},{32,0},{64,32},{96,64},{128,96},{160,128},{192,160},{224,1... | collective-permute-start | bytes 786440 | tf_op jit(solution)/shard_map/ppermute | solution.py:291
  33.2 2.0 %collective-permute-done.6.refs_11_ = f32[8,8192]{1,0:T(8,128)S(1)} collective-permute-done((f32[8,8192]{1,0:T(8,128)S(1)}, f32[8,8192]{1,0:T(8,128)S(1)}, u32[]{:S(2)}, u32[]{:S(2)}) %collective-permute-start.6) | collective-permute-done | bytes 262176 | tf_op jit(solution)/shard_map/ppermute | solution.py:291
  35.2 3.4 %collective-permute-start.7 = (f32[8,8192]{1,0:T(8,128)S(1)}, f32[8,8192]{1,0:T(8,128)S(1)}, u32[]{:S(2)}, u32[]{:S(2)}) collective-permute-start(f32[8,8192]{1,0:T(8,128)S(1)} %collective-permute-done.6.refs_11_), channel_id=1, source_target_pairs={{0,224},{32,0},{64,32},{96,64},{128,96},{160,128},{192,160},{224,1... | collective-permute-start | bytes 786440 | tf_op jit(solution)/shard_map/ppermute | solution.py:294
  38.6 0.0 collective-permute-done.2.refs_8_
  38.6 0.0 collective-permute-start.3
  38.6 1.2 %collective-permute-done.12.refs_9_ = f32[8,8192]{1,0:T(8,128)S(1)} collective-permute-done((f32[8,8192]{1,0:T(8,128)S(1)}, f32[8,8192]{1,0:T(8,128)S(1)}, u32[]{:S(2)}, u32[]{:S(2)}) %collective-permute-start.12) | collective-permute-done | bytes 262176 | tf_op jit(solution)/shard_map/ppermute | solution.py:290
  39.8 1.0 %collective-permute-done.13.refs_10_ = f32[8,8192]{1,0:T(8,128)S(1)} collective-permute-done((f32[8,8192]{1,0:T(8,128)S(1)}, f32[8,8192]{1,0:T(8,128)S(1)}, u32[]{:S(2)}, u32[]{:S(2)}) %collective-permute-start.13) | collective-permute-done | bytes 262176 | tf_op jit(solution)/shard_map/ppermute | solution.py:291
  40.8 0.0 copy-done
  40.8 0.0 copy-done.2
  40.8 1.6 %early.1 = (f32[32,128]{1,0:T(8,128)S(1)}, bf16[160,16384]{1,0:T(8,128)(2,1)S(1)}) custom-call(f32[8,16384]{1,0:T(8,128)S(1)} %copy-done, f32[8,8192]{1,0:T(8,128)S(1)} %collective-permute-done.refs_0_, f32[8,8192]{1,0:T(8,128)S(1)} %collective-permute-done.8.refs_1_, f32[8,8192]{1,0:T(8,128)S(1)} %collective-permute-done.9.refs_2_, ...), custom_call_target="tpu_custom_call" | custom-call | flops 1000000000 | bytes 4000000 | tf_op jit(solution)/shard_map/early/pallas_call | solution.py:110
  42.4 4.0 %collective-permute-done.7.refs_1_ = f32[8,8192]{1,0:T(8,128)S(1)} collective-permute-done((f32[8,8192]{1,0:T(8,128)S(1)}, f32[8,8192]{1,0:T(8,128)S(1)}, u32[]{:S(2)}, u32[]{:S(2)}) %collective-permute-start.7) | collective-permute-done | bytes 262176 | tf_op jit(solution)/shard_map/ppermute | solution.py:294
  46.4 0.0 collective-permute-done.3.refs_0_
  46.4 1.7 %last.1 = (f32[32,128]{1,0:T(8,128)S(1)}, bf16[160,16384]{1,0:T(8,128)(2,1)S(1)}) custom-call(f32[8,8192]{1,0:T(8,128)S(1)} %collective-permute-done.3.refs_0_, f32[8,8192]{1,0:T(8,128)S(1)} %collective-permute-done.7.refs_1_, f32[32,128]{1,0:T(8,128)S(1)} %get-tuple-element.31.refs_2_, ...), custom_call_target="tpu_custom_call", output_to_operand_aliasing={{1}: (3, {})} | custom-call | flops 1000000000 | bytes 4000000 | tf_op jit(solution)/shard_map/last/pallas_call | solution.py:110
  48.1 2.8 %collective-permute-start.14 = (f32[32,128]{1,0:T(8,128)S(1)}, f32[32,128]{1,0:T(8,128)S(1)}, u32[]{:S(2)}, u32[]{:S(2)}) collective-permute-start(f32[32,128]{1,0:T(8,128)S(1)} %get-tuple-element.33), channel_id=1, source_target_pairs={{0,1},{1,0},{2,3},{3,2},{4,5},{5,4},{6,7},{7,6},{8,9},{9,8},{10,11... | collective-permute-start | bytes 49160 | tf_op jit(solution)/shard_map/ppermute | solution.py:268
  50.9 0.8 %collective-permute-done.14 = f32[32,128]{1,0:T(8,128)S(1)} collective-permute-done((f32[32,128]{1,0:T(8,128)S(1)}, f32[32,128]{1,0:T(8,128)S(1)}, u32[]{:S(2)}, u32[]{:S(2)}) %collective-permute-start.14) | collective-permute-done | bytes 16416 | tf_op jit(solution)/shard_map/ppermute | solution.py:268
  51.8 14.1 %all_to_all.5.refs_0_ = f32[16,32,128]{2,1,0:T(8,128)S(1)} all-to-all(f32[16,32,128]{2,1,0:T(8,128)S(1)} %broadcast_in_dim.2), channel_id=1, replica_groups=mesh['member'=8,'x'=4,'y'=4,'core'=2] {'x','y'}, dimensions={0} | all-to-all | bytes 524288 | tf_op jit(solution)/shard_map/all_to_all | solution.py:270
  65.9 2.2 %final.1 = f32[8,16384]{1,0:T(8,128)} custom-call(f32[16,32,128]{2,1,0:T(8,128)S(1)} %all_to_all.5.refs_0_, bf16[160,16384]{1,0:T(8,128)(2,1)S(1)} %get-tuple-element.34.refs_1_, f32[8,16384]{1,0:T(8,128)S(1)} %get-tuple-element.35.refs_2_, f32[8,16384]{1,0:T(8,128)S(1)} %get-tuple-element.36.refs_3_), custom_call_target="tpu_custom_call" | custom-call | flops 1000000000 | bytes 4000000 | tf_op jit(solution)/shard_map/final/pallas_call | solution.py:110
  (5 shorter events, 0.0 us)
Async XLA Ops:
  0.0 40.8 %copy-start = (f32[8,16384]{1,0:T(8,128)S(1)}, f32[8,16384]{1,0:T(8,128)}, u32[]{:S(2)}) copy-start(f32[8,16384]{1,0:T(8,128)} %own.1) | copy-start | bytes 1572868
  0.0 40.8 %copy-start.2 = (f32[8,16384]{1,0:T(8,128)S(1)}, f32[8,16384]{1,0:T(8,128)}, u32[]{:S(2)}) copy-start(f32[8,16384]{1,0:T(8,128)} %refs_12_.1) | copy-start | bytes 1572868
  1.2 12.8 %collective-permute-start = (f32[8,8192]{1,0:T(8,128)S(1)}, f32[8,8192]{1,0:T(8,128)S(1)}, u32[]{:S(2)}, u32[]{:S(2)}) collective-permute-start(f32[8,8192]{1,0:T(8,128)S(1)} %get-tuple-element.38), channel_id=1, source_target_pairs={{0,32},{32,64},{64,96},{96,128},{128,160},{160,192},{192,224},{224... | collective-permute-start | bytes 786440 | tf_op jit(solution)/shard_map/ppermute | solution.py:290
  3.7 10.3 %collective-permute-start.4 = (f32[8,8192]{1,0:T(8,128)S(1)}, f32[8,8192]{1,0:T(8,128)S(1)}, u32[]{:S(2)}, u32[]{:S(2)}) collective-permute-start(f32[8,8192]{1,0:T(8,128)S(1)} %get-tuple-element.37), channel_id=1, source_target_pairs={{0,224},{32,0},{64,32},{96,64},{128,96},{160,128},{192,160},{224,1... | collective-permute-start | bytes 786440 | tf_op jit(solution)/shard_map/ppermute | solution.py:291
  7.7 11.6 %collective-permute-start.8 = (f32[8,8192]{1,0:T(8,128)S(1)}, f32[8,8192]{1,0:T(8,128)S(1)}, u32[]{:S(2)}, u32[]{:S(2)}) collective-permute-start(f32[8,8192]{1,0:T(8,128)S(1)} %get-tuple-element.37), channel_id=1, source_target_pairs={{0,32},{32,64},{64,96},{96,128},{128,160},{160,192},{192,224},{224... | collective-permute-start | bytes 786440 | tf_op jit(solution)/shard_map/ppermute | solution.py:290
  7.7 11.6 %collective-permute-start.9 = (f32[8,8192]{1,0:T(8,128)S(1)}, f32[8,8192]{1,0:T(8,128)S(1)}, u32[]{:S(2)}, u32[]{:S(2)}) collective-permute-start(f32[8,8192]{1,0:T(8,128)S(1)} %get-tuple-element.38), channel_id=1, source_target_pairs={{0,224},{32,0},{64,32},{96,64},{128,96},{160,128},{192,160},{224,1... | collective-permute-start | bytes 786440 | tf_op jit(solution)/shard_map/ppermute | solution.py:291
  10.4 0.7 %copy-start.4 = (s32[2,2048]{1,0:T(2,128)S(1)}, s32[2,2048]{1,0:T(2,128)}, u32[]{:S(2)}) copy-start(s32[2,2048]{1,0:T(2,128)} %cells.1) | copy-start | bytes 49156
  11.1 0.7 %copy-start.5 = (f32[2,2048]{1,0:T(2,128)S(1)}, f32[2,2048]{1,0:T(2,128)}, u32[]{:S(2)}) copy-start(f32[2,2048]{1,0:T(2,128)} %vals.1) | copy-start | bytes 49156
  11.8 0.7 copy-start.6
  13.9 11.0 %collective-permute-start.1 = (f32[8,8192]{1,0:T(8,128)S(1)}, f32[8,8192]{1,0:T(8,128)S(1)}, u32[]{:S(2)}, u32[]{:S(2)}) collective-permute-start(f32[8,8192]{1,0:T(8,128)S(1)} %collective-permute-done.refs_0_), channel_id=1, source_target_pairs={{0,32},{32,64},{64,96},{96,128},{128,160},{160,192},{192,224},{224... | collective-permute-start | bytes 786440 | tf_op jit(solution)/shard_map/ppermute | solution.py:290
  14.0 10.9 %collective-permute-start.5 = (f32[8,8192]{1,0:T(8,128)S(1)}, f32[8,8192]{1,0:T(8,128)S(1)}, u32[]{:S(2)}, u32[]{:S(2)}) collective-permute-start(f32[8,8192]{1,0:T(8,128)S(1)} %collective-permute-done.4.refs_3_), channel_id=1, source_target_pairs={{0,224},{32,0},{64,32},{96,64},{128,96},{160,128},{192,160},{224,1... | collective-permute-start | bytes 786440 | tf_op jit(solution)/shard_map/ppermute | solution.py:291
  19.3 11.2 %collective-permute-start.10 = (f32[8,8192]{1,0:T(8,128)S(1)}, f32[8,8192]{1,0:T(8,128)S(1)}, u32[]{:S(2)}, u32[]{:S(2)}) collective-permute-start(f32[8,8192]{1,0:T(8,128)S(1)} %collective-permute-done.8.refs_1_), channel_id=1, source_target_pairs={{0,32},{32,64},{64,96},{96,128},{128,160},{160,192},{192,224},{224... | collective-permute-start | bytes 786440 | tf_op jit(solution)/shard_map/ppermute | solution.py:290
  19.3 11.2 %collective-permute-start.11 = (f32[8,8192]{1,0:T(8,128)S(1)}, f32[8,8192]{1,0:T(8,128)S(1)}, u32[]{:S(2)}, u32[]{:S(2)}) collective-permute-start(f32[8,8192]{1,0:T(8,128)S(1)} %collective-permute-done.9.refs_2_), channel_id=1, source_target_pairs={{0,224},{32,0},{64,32},{96,64},{128,96},{160,128},{192,160},{224,1... | collective-permute-start | bytes 786440 | tf_op jit(solution)/shard_map/ppermute | solution.py:291
  22.0 1.0 %copy-start.1 = (f32[8,16384]{1,0:T(8,128)S(1)}, f32[8,16384]{1,0:T(8,128)}, u32[]{:S(2)}) copy-start(f32[8,16384]{1,0:T(8,128)} %refs_12_.1) | copy-start | bytes 1572868
  23.0 1.2 %copy-start.3 = (f32[2,8,16384]{2,1,0:T(8,128)S(1)}, f32[2,8,16384]{2,1,0:T(8,128)}, u32[]{:S(2)}) copy-start(f32[2,8,16384]{2,1,0:T(8,128)} %noise.1) | copy-start | bytes 3145732
  24.9 10.3 %collective-permute-start.6 = (f32[8,8192]{1,0:T(8,128)S(1)}, f32[8,8192]{1,0:T(8,128)S(1)}, u32[]{:S(2)}, u32[]{:S(2)}) collective-permute-start(f32[8,8192]{1,0:T(8,128)S(1)} %collective-permute-done.5.refs_7_), channel_id=1, source_target_pairs={{0,224},{32,0},{64,32},{96,64},{128,96},{160,128},{192,160},{224,1... | collective-permute-start | bytes 786440 | tf_op jit(solution)/shard_map/ppermute | solution.py:291
  27.4 11.2 %collective-permute-start.2 = (f32[8,8192]{1,0:T(8,128)S(1)}, f32[8,8192]{1,0:T(8,128)S(1)}, u32[]{:S(2)}, u32[]{:S(2)}) collective-permute-start(f32[8,8192]{1,0:T(8,128)S(1)} %collective-permute-done.1.refs_4_), channel_id=1, source_target_pairs={{0,32},{32,64},{64,96},{96,128},{128,160},{160,192},{192,224},{224... | collective-permute-start | bytes 786440 | tf_op jit(solution)/shard_map/ppermute | solution.py:290
  30.5 9.3 %collective-permute-start.12 = (f32[8,8192]{1,0:T(8,128)S(1)}, f32[8,8192]{1,0:T(8,128)S(1)}, u32[]{:S(2)}, u32[]{:S(2)}) collective-permute-start(f32[8,8192]{1,0:T(8,128)S(1)} %collective-permute-done.10.refs_5_), channel_id=1, source_target_pairs={{0,32},{32,64},{64,96},{96,128},{128,160},{160,192},{192,224},{224... | collective-permute-start | bytes 786440 | tf_op jit(solution)/shard_map/ppermute | solution.py:290
  30.5 10.3 %collective-permute-start.13 = (f32[8,8192]{1,0:T(8,128)S(1)}, f32[8,8192]{1,0:T(8,128)S(1)}, u32[]{:S(2)}, u32[]{:S(2)}) collective-permute-start(f32[8,8192]{1,0:T(8,128)S(1)} %collective-permute-done.11.refs_6_), channel_id=1, source_target_pairs={{0,224},{32,0},{64,32},{96,64},{128,96},{160,128},{192,160},{224,1... | collective-permute-start | bytes 786440 | tf_op jit(solution)/shard_map/ppermute | solution.py:291
  35.2 11.2 %collective-permute-start.7 = (f32[8,8192]{1,0:T(8,128)S(1)}, f32[8,8192]{1,0:T(8,128)S(1)}, u32[]{:S(2)}, u32[]{:S(2)}) collective-permute-start(f32[8,8192]{1,0:T(8,128)S(1)} %collective-permute-done.6.refs_11_), channel_id=1, source_target_pairs={{0,224},{32,0},{64,32},{96,64},{128,96},{160,128},{192,160},{224,1... | collective-permute-start | bytes 786440 | tf_op jit(solution)/shard_map/ppermute | solution.py:294
  38.6 7.8 %collective-permute-start.3 = (f32[8,8192]{1,0:T(8,128)S(1)}, f32[8,8192]{1,0:T(8,128)S(1)}, u32[]{:S(2)}, u32[]{:S(2)}) collective-permute-start(f32[8,8192]{1,0:T(8,128)S(1)} %collective-permute-done.2.refs_8_), channel_id=1, source_target_pairs={{0,32},{32,64},{64,96},{96,128},{128,160},{160,192},{192,224},{224... | collective-permute-start | bytes 786440 | tf_op jit(solution)/shard_map/ppermute | solution.py:294
  48.1 3.7 %collective-permute-start.14 = (f32[32,128]{1,0:T(8,128)S(1)}, f32[32,128]{1,0:T(8,128)S(1)}, u32[]{:S(2)}, u32[]{:S(2)}) collective-permute-start(f32[32,128]{1,0:T(8,128)S(1)} %get-tuple-element.33), channel_id=1, source_target_pairs={{0,1},{1,0},{2,3},{3,2},{4,5},{5,4},{6,7},{7,6},{8,9},{9,8},{10,11... | collective-permute-start | bytes 49160 | tf_op jit(solution)/shard_map/ppermute | solution.py:268
